TPU v7x, 32 devices: a whole 2x2x4 slice. The times are simulated.
32 devices in a mesh: blk: 8 (over z, y), beam: 4 (over x, core).
Axes of the slice: x: 2, y: 2, z: 4, core: 2. Of those that a mesh axis runs over, the one named last changes fastest.
Arguments:
- signal: float32 [524288], P(('blk', 'beam')), may hold values from -6 to 6
- weight: float32 [524288], P(('blk', 'beam')), may hold values from 0.25 to 1
- cycle: int32 [524288], P(('blk', 'beam')), may hold values from 0 to 1
- phi: int32 [524288], P(('blk', 'beam')), may hold values from 0 to 2047
- psi: int32 [524288], P(('blk', 'beam')), may hold values from 0 to 31
- owner: int32 [4096, 1], P(('blk', 'beam')), may hold values from 0 to 7; in each aligned block of 128 rows (0 to 127, 128 to 255, ...) at most 40 rows name the same one
- wigner: bfloat16 [1024, 32, 16, 1152], P('blk', 'beam'), may hold values from -0.375 to 0.375
Outputs:
- alm: float32 [1024, 2, 1152], P(('blk', 'beam'))
Inputs may be any that keep to these rules, and one draw needn't show every extreme that they name: `owner`: among the 128 blocks of one device no cycle group is named by more than 40 blocks, and in some device's blocks one group is named by exactly 40.
All inputs are finite; a program needn't handle non-finite values.
Results may differ from a plain program's by a relative error of at most 0.02.
Values may be sent and summed in bfloat16 or wider, within the bound.
No kernel may reach another device: no remote copies, remote signals or barrier semaphores. Data moves between devices by JAX's collectives and lax.ppermute only.
A program may use at most 128 MiB of HBM per device.

v0:
```python
import math

import jax
import jax.numpy as jnp
from jax import lax
from jax.sharding import PartitionSpec as P

BLOCK_ROWS = 128
CYCLE_DEV = 2
NPSI = 32
NPHI = 2048


def psi_rows(psi_index, length):
    component = jnp.arange(length, dtype=jnp.int32)[:, None]
    middle = length // 2
    frequency = jnp.where(component <= middle, component, component - middle)
    residue = (frequency * psi_index[None, :] % length).astype(jnp.float32)
    angles = residue * jnp.float32(2.0 * math.pi / length)
    return jnp.where(component <= middle, jnp.cos(angles), jnp.sin(angles)) * jnp.float32(
        1.0 / math.sqrt(length)
    )


def phi_table(length):
    cell_index = jnp.arange(length, dtype=jnp.int32)[:, None]
    column = jnp.arange(length, dtype=jnp.int32)[None, :]
    residue = (column // 2 * cell_index % length).astype(jnp.float32)
    angles = residue * jnp.float32(2.0 * math.pi / length)
    values = jnp.where(column % 2 == 0, jnp.cos(angles), jnp.sin(angles)) * jnp.float32(
        1.0 / math.sqrt(length)
    )
    return values.astype(jnp.bfloat16)


def block_turns(total):
    turns = max(1, total // 2048)
    while total % turns != 0:
        turns = turns - 1
    return turns


def shards(signal, weight, cycle, phi, psi, owner, wigner):
    groups = lax.axis_size("blk")
    beams = lax.axis_size("beam")
    blocks = owner.shape[0]
    capacity = max(2, 5 * blocks // (2 * groups))
    slots = capacity * BLOCK_ROWS
    target_group = owner[:, 0]
    hits = (target_group[:, None] == jnp.arange(groups, dtype=jnp.int32)[None, :]).astype(jnp.int32)
    earlier = jnp.cumsum(hits, axis=0) - hits
    within = jnp.sum(earlier * hits, axis=1)
    position = target_group * capacity + within
    source = (
        jnp.zeros((groups * capacity,), jnp.int32)
        .at[position]
        .set(jnp.arange(blocks, dtype=jnp.int32))
    )
    filled = jnp.zeros((groups * capacity,), jnp.int32).at[position].set(1)

    def arrange(data):
        leading = data.shape[0]
        shaped = data.reshape(leading, blocks, BLOCK_ROWS)
        taken = jnp.take(shaped, source, axis=1)
        taken = jnp.where(filled[None, :, None] > 0, taken, jnp.zeros_like(taken))
        return taken.reshape(leading, groups, slots)

    sample_value = signal * weight
    packed = (cycle * NPSI + psi) * NPHI + phi
    total = groups * slots
    got_value, got_code = (
        lax.all_to_all(
            arrange(sample_value[None, :]).astype(jnp.bfloat16),
            "blk",
            split_axis=1,
            concat_axis=1,
            tiled=True,
        ).astype(jnp.float32),
        lax.all_to_all(arrange(packed[None, :]), "blk", split_axis=1, concat_axis=1, tiled=True),
    )
    codes = got_code.reshape(total)
    arrived = got_value.reshape(total)
    received = (psi_rows(codes // NPHI % NPSI, NPSI) * arrived[None, :]).astype(jnp.bfloat16)
    cycle_of = codes // (NPSI * NPHI)
    phi_of = codes % NPHI
    spread = jnp.concatenate(
        [
            jnp.where(cycle_of[None, :] == level, received, jnp.zeros_like(received))
            for level in range(CYCLE_DEV)
        ],
        axis=0,
    )
    turns = block_turns(total)
    width = total // turns
    columns = jnp.arange(NPHI, dtype=jnp.int32)

    def bin_block(number, carry):
        start = number * width
        part = lax.dynamic_slice_in_dim(spread, start, width, 1)
        place = lax.dynamic_slice_in_dim(phi_of, start, width, 0)
        onehot = (place[:, None] == columns[None, :]).astype(jnp.bfloat16)
        return carry + jnp.dot(part, onehot, preferred_element_type=jnp.float32)

    cube = lax.fori_loop(0, turns, bin_block, jnp.zeros((CYCLE_DEV * NPSI, NPHI), jnp.float32))
    cube = cube.reshape(CYCLE_DEV, NPSI, NPHI)
    share = NPSI // beams
    summed = lax.psum(cube.astype(jnp.bfloat16), "beam").astype(jnp.float32)
    mine = lax.dynamic_slice_in_dim(summed, lax.axis_index("beam") * share, share, 1)
    spectra = jnp.dot(
        mine.astype(jnp.bfloat16).reshape(CYCLE_DEV * share, NPHI),
        phi_table(NPHI),
        preferred_element_type=jnp.float32,
    )
    spectra = spectra.astype(jnp.bfloat16).reshape(CYCLE_DEV, share, NPHI)
    regrouped = lax.all_to_all(spectra, "blk", split_axis=2, concat_axis=0, tiled=True)
    orders = regrouped.shape[2] // 2
    coeffs = regrouped.reshape(regrouped.shape[0], share, orders, 2).transpose(2, 1, 0, 3)
    partial_sum = jnp.einsum("mqtl,mqtp->mpl", wigner, coeffs, preferred_element_type=jnp.float32)
    totals = lax.psum(partial_sum.astype(jnp.bfloat16), "beam").astype(jnp.float32)
    return lax.dynamic_slice_in_dim(
        totals, lax.axis_index("beam") * (orders // beams), orders // beams, 0
    )


def solution(mesh):
    return jax.shard_map(
        shards,
        mesh=mesh,
        in_specs=(
            P(("blk", "beam")),
            P(("blk", "beam")),
            P(("blk", "beam")),
            P(("blk", "beam")),
            P(("blk", "beam")),
            P(("blk", "beam"), None),
            P("blk", "beam", None, None),
        ),
        out_specs=P(("blk", "beam"), None, None),
        check_vma=False,
    )
```

profile of v0, /device:TPU:0, one launch (start us, length us, event | category | flops | bytes accessed | tf_op | source)
XLA Modules:
  0.0 333.1 jit_solution(5072294114963490575)
XLA Ops:
  16.1 7.3 %all-to-all-start.1 = ((bf16[8,2,2560]{2,1,0:T(2,128)(2,1)}), bf16[8,2,2560]{2,1,0:T(2,128)(2,1)S(1)}, u32[]{:S(2)}, u32[]{:S(2)}) async-start(bf16[8,2,2560]{2,1,0:T(2,128)(2,1)} %reshape.312), calls=%async_computation.1 | async-start | bytes 163840 | tf_op jit(solution)/shard_map/all_to_all | solution.py:72
  26.4 4.1 %all-to-all-done.1 = bf16[8,2,2560]{2,1,0:T(2,128)(2,1)S(1)} async-done(((bf16[8,2,2560]{2,1,0:T(2,128)(2,1)}), bf16[8,2,2560]{2,1,0:T(2,128)(2,1)S(1)}, u32[]{:S(2)}, u32[]{:S(2)}) %all-to-all-start.1) | async-done | bytes 81952 | tf_op jit(solution)/shard_map/all_to_all | solution.py:72
  30.5 3.4 %all-to-all-start = ((s32[1,8,5120]{2,0,1:T(1,128)}), s32[1,8,5120]{2,0,1:T(1,128)S(1)}, u32[]{:S(2)}, u32[]{:S(2)}) async-start(s32[1,8,5120]{2,0,1:T(1,128)} %copy.17), calls=%async_computation | async-start | bytes 327680 | tf_op jit(solution)/shard_map/all_to_all | solution.py:79
  34.4 7.0 %all-to-all-done = s32[1,8,5120]{2,0,1:T(1,128)S(1)} async-done(((s32[1,8,5120]{2,0,1:T(1,128)}), s32[1,8,5120]{2,0,1:T(1,128)S(1)}, u32[]{:S(2)}, u32[]{:S(2)}) %all-to-all-start) | async-done | bytes 163872 | tf_op jit(solution)/shard_map/all_to_all | solution.py:79
  41.7 21.8 %broadcast_select_fusion.1 = (bf16[32,40960]{1,0:T(8,128)(2,1)S(1)}, bf16[32,40960]{1,0:T(8,128)(2,1)S(1)}) fusion(pred[40960]{0:T(1024)(128)(4,1)S(1)} %get-tuple-element.129, f32[40960]{0:T(1024)S(1)} %bitcast.53, s32[40960]{0:T(1024)S(1)} %get-tuple-element.128, s32[32]{0:T(128)S(1)} %add_select_fusion.8, pred[32]{0:T(512)(128)(4,1)S(1)} %iota_compare_fusion.5, ...), kind=kLoop, calls=%fused_computation.37 | loop fusion | flops 24903680 | bytes 5652640 | tf_op jit(solution)/shard_map/jit(_where)/select_n | solution.py:88
  63.6 2.7 pad_maximum_fusion
  66.2 90.4 %while.14 = (s32[]{:T(128)}, f32[64,2048]{1,0:T(8,128)S(1)}, bf16[64,40960]{1,0:T(8,128)(2,1)}, s32[40960]{0:T(1024)S(1)}, s32[]{:T(128)}, /*index=5*/s32[]{:T(128)}, s32[]{:T(128)}, s32[]{:T(128)}) while((s32[]{:T(128)}, f32[64,2048]{1,0:T(8,128)S(1)}, bf16[64,40960]{1,0:T(8,128)(2,1)}, s32[40960]{0:T(1024)S(1)}, s32[]{:T(128)}, ...), condition=%wide.region_5.6_spmd.clone, body=%wide.region_4.5_spmd.clone.sunk | while | flops 541327360 | bytes 1335445 | solution.py:104
  66.2 4.5 %fusion.59 = f32[64,2048]{1,0:T(8,128)S(1)} fusion(s32[2048]{0:T(1024)S(1)} %dynamic_slice.39, f32[64,2048]{1,0:T(8,128)S(1)} %get-tuple-element.165, bf16[64,40960]{1,0:T(8,128)(2,1)} %get-tuple-element.174, s32[]{:T(128)S(6)} %select_n.263, pred[]{:T(512)S(6)} %compare.34), kind=kOutput, calls=%fused_computation.8.clone.1 | convolution fusion | flops 541327360 | bytes 1318917 | tf_op jit(solution)/shard_map/while/body/eval_jaxpr/dot_general | solution.py:102
  70.7 4.5 %fusion.59 = f32[64,2048]{1,0:T(8,128)S(1)} fusion(s32[2048]{0:T(1024)S(1)} %dynamic_slice.39, f32[64,2048]{1,0:T(8,128)S(1)} %get-tuple-element.165, bf16[64,40960]{1,0:T(8,128)(2,1)} %get-tuple-element.174, s32[]{:T(128)S(6)} %select_n.263, pred[]{:T(512)S(6)} %compare.34), kind=kOutput, calls=%fused_computation.8.clone.1 | convolution fusion | flops 541327360 | bytes 1318917 | tf_op jit(solution)/shard_map/while/body/eval_jaxpr/dot_general | solution.py:102
  75.3 4.5 %fusion.59 = f32[64,2048]{1,0:T(8,128)S(1)} fusion(s32[2048]{0:T(1024)S(1)} %dynamic_slice.39, f32[64,2048]{1,0:T(8,128)S(1)} %get-tuple-element.165, bf16[64,40960]{1,0:T(8,128)(2,1)} %get-tuple-element.174, s32[]{:T(128)S(6)} %select_n.263, pred[]{:T(512)S(6)} %compare.34), kind=kOutput, calls=%fused_computation.8.clone.1 | convolution fusion | flops 541327360 | bytes 1318917 | tf_op jit(solution)/shard_map/while/body/eval_jaxpr/dot_general | solution.py:102
  79.8 4.5 %fusion.59 = f32[64,2048]{1,0:T(8,128)S(1)} fusion(s32[2048]{0:T(1024)S(1)} %dynamic_slice.39, f32[64,2048]{1,0:T(8,128)S(1)} %get-tuple-element.165, bf16[64,40960]{1,0:T(8,128)(2,1)} %get-tuple-element.174, s32[]{:T(128)S(6)} %select_n.263, pred[]{:T(512)S(6)} %compare.34), kind=kOutput, calls=%fused_computation.8.clone.1 | convolution fusion | flops 541327360 | bytes 1318917 | tf_op jit(solution)/shard_map/while/body/eval_jaxpr/dot_general | solution.py:102
  84.3 4.5 %fusion.59 = f32[64,2048]{1,0:T(8,128)S(1)} fusion(s32[2048]{0:T(1024)S(1)} %dynamic_slice.39, f32[64,2048]{1,0:T(8,128)S(1)} %get-tuple-element.165, bf16[64,40960]{1,0:T(8,128)(2,1)} %get-tuple-element.174, s32[]{:T(128)S(6)} %select_n.263, pred[]{:T(512)S(6)} %compare.34), kind=kOutput, calls=%fused_computation.8.clone.1 | convolution fusion | flops 541327360 | bytes 1318917 | tf_op jit(solution)/shard_map/while/body/eval_jaxpr/dot_general | solution.py:102
  88.8 4.5 %fusion.59 = f32[64,2048]{1,0:T(8,128)S(1)} fusion(s32[2048]{0:T(1024)S(1)} %dynamic_slice.39, f32[64,2048]{1,0:T(8,128)S(1)} %get-tuple-element.165, bf16[64,40960]{1,0:T(8,128)(2,1)} %get-tuple-element.174, s32[]{:T(128)S(6)} %select_n.263, pred[]{:T(512)S(6)} %compare.34), kind=kOutput, calls=%fused_computation.8.clone.1 | convolution fusion | flops 541327360 | bytes 1318917 | tf_op jit(solution)/shard_map/while/body/eval_jaxpr/dot_general | solution.py:102
  93.3 4.5 %fusion.59 = f32[64,2048]{1,0:T(8,128)S(1)} fusion(s32[2048]{0:T(1024)S(1)} %dynamic_slice.39, f32[64,2048]{1,0:T(8,128)S(1)} %get-tuple-element.165, bf16[64,40960]{1,0:T(8,128)(2,1)} %get-tuple-element.174, s32[]{:T(128)S(6)} %select_n.263, pred[]{:T(512)S(6)} %compare.34), kind=kOutput, calls=%fused_computation.8.clone.1 | convolution fusion | flops 541327360 | bytes 1318917 | tf_op jit(solution)/shard_map/while/body/eval_jaxpr/dot_general | solution.py:102
  97.9 4.5 %fusion.59 = f32[64,2048]{1,0:T(8,128)S(1)} fusion(s32[2048]{0:T(1024)S(1)} %dynamic_slice.39, f32[64,2048]{1,0:T(8,128)S(1)} %get-tuple-element.165, bf16[64,40960]{1,0:T(8,128)(2,1)} %get-tuple-element.174, s32[]{:T(128)S(6)} %select_n.263, pred[]{:T(512)S(6)} %compare.34), kind=kOutput, calls=%fused_computation.8.clone.1 | convolution fusion | flops 541327360 | bytes 1318917 | tf_op jit(solution)/shard_map/while/body/eval_jaxpr/dot_general | solution.py:102
  102.4 4.5 %fusion.59 = f32[64,2048]{1,0:T(8,128)S(1)} fusion(s32[2048]{0:T(1024)S(1)} %dynamic_slice.39, f32[64,2048]{1,0:T(8,128)S(1)} %get-tuple-element.165, bf16[64,40960]{1,0:T(8,128)(2,1)} %get-tuple-element.174, s32[]{:T(128)S(6)} %select_n.263, pred[]{:T(512)S(6)} %compare.34), kind=kOutput, calls=%fused_computation.8.clone.1 | convolution fusion | flops 541327360 | bytes 1318917 | tf_op jit(solution)/shard_map/while/body/eval_jaxpr/dot_general | solution.py:102
  106.9 4.5 %fusion.59 = f32[64,2048]{1,0:T(8,128)S(1)} fusion(s32[2048]{0:T(1024)S(1)} %dynamic_slice.39, f32[64,2048]{1,0:T(8,128)S(1)} %get-tuple-element.165, bf16[64,40960]{1,0:T(8,128)(2,1)} %get-tuple-element.174, s32[]{:T(128)S(6)} %select_n.263, pred[]{:T(512)S(6)} %compare.34), kind=kOutput, calls=%fused_computation.8.clone.1 | convolution fusion | flops 541327360 | bytes 1318917 | tf_op jit(solution)/shard_map/while/body/eval_jaxpr/dot_general | solution.py:102
  111.4 4.5 %fusion.59 = f32[64,2048]{1,0:T(8,128)S(1)} fusion(s32[2048]{0:T(1024)S(1)} %dynamic_slice.39, f32[64,2048]{1,0:T(8,128)S(1)} %get-tuple-element.165, bf16[64,40960]{1,0:T(8,128)(2,1)} %get-tuple-element.174, s32[]{:T(128)S(6)} %select_n.263, pred[]{:T(512)S(6)} %compare.34), kind=kOutput, calls=%fused_computation.8.clone.1 | convolution fusion | flops 541327360 | bytes 1318917 | tf_op jit(solution)/shard_map/while/body/eval_jaxpr/dot_general | solution.py:102
  116.0 4.5 %fusion.59 = f32[64,2048]{1,0:T(8,128)S(1)} fusion(s32[2048]{0:T(1024)S(1)} %dynamic_slice.39, f32[64,2048]{1,0:T(8,128)S(1)} %get-tuple-element.165, bf16[64,40960]{1,0:T(8,128)(2,1)} %get-tuple-element.174, s32[]{:T(128)S(6)} %select_n.263, pred[]{:T(512)S(6)} %compare.34), kind=kOutput, calls=%fused_computation.8.clone.1 | convolution fusion | flops 541327360 | bytes 1318917 | tf_op jit(solution)/shard_map/while/body/eval_jaxpr/dot_general | solution.py:102
  120.5 4.5 %fusion.59 = f32[64,2048]{1,0:T(8,128)S(1)} fusion(s32[2048]{0:T(1024)S(1)} %dynamic_slice.39, f32[64,2048]{1,0:T(8,128)S(1)} %get-tuple-element.165, bf16[64,40960]{1,0:T(8,128)(2,1)} %get-tuple-element.174, s32[]{:T(128)S(6)} %select_n.263, pred[]{:T(512)S(6)} %compare.34), kind=kOutput, calls=%fused_computation.8.clone.1 | convolution fusion | flops 541327360 | bytes 1318917 | tf_op jit(solution)/shard_map/while/body/eval_jaxpr/dot_general | solution.py:102
  125.0 4.5 %fusion.59 = f32[64,2048]{1,0:T(8,128)S(1)} fusion(s32[2048]{0:T(1024)S(1)} %dynamic_slice.39, f32[64,2048]{1,0:T(8,128)S(1)} %get-tuple-element.165, bf16[64,40960]{1,0:T(8,128)(2,1)} %get-tuple-element.174, s32[]{:T(128)S(6)} %select_n.263, pred[]{:T(512)S(6)} %compare.34), kind=kOutput, calls=%fused_computation.8.clone.1 | convolution fusion | flops 541327360 | bytes 1318917 | tf_op jit(solution)/shard_map/while/body/eval_jaxpr/dot_general | solution.py:102
  129.5 4.5 %fusion.59 = f32[64,2048]{1,0:T(8,128)S(1)} fusion(s32[2048]{0:T(1024)S(1)} %dynamic_slice.39, f32[64,2048]{1,0:T(8,128)S(1)} %get-tuple-element.165, bf16[64,40960]{1,0:T(8,128)(2,1)} %get-tuple-element.174, s32[]{:T(128)S(6)} %select_n.263, pred[]{:T(512)S(6)} %compare.34), kind=kOutput, calls=%fused_computation.8.clone.1 | convolution fusion | flops 541327360 | bytes 1318917 | tf_op jit(solution)/shard_map/while/body/eval_jaxpr/dot_general | solution.py:102
  134.0 4.5 %fusion.59 = f32[64,2048]{1,0:T(8,128)S(1)} fusion(s32[2048]{0:T(1024)S(1)} %dynamic_slice.39, f32[64,2048]{1,0:T(8,128)S(1)} %get-tuple-element.165, bf16[64,40960]{1,0:T(8,128)(2,1)} %get-tuple-element.174, s32[]{:T(128)S(6)} %select_n.263, pred[]{:T(512)S(6)} %compare.34), kind=kOutput, calls=%fused_computation.8.clone.1 | convolution fusion | flops 541327360 | bytes 1318917 | tf_op jit(solution)/shard_map/while/body/eval_jaxpr/dot_general | solution.py:102
  138.6 4.5 %fusion.59 = f32[64,2048]{1,0:T(8,128)S(1)} fusion(s32[2048]{0:T(1024)S(1)} %dynamic_slice.39, f32[64,2048]{1,0:T(8,128)S(1)} %get-tuple-element.165, bf16[64,40960]{1,0:T(8,128)(2,1)} %get-tuple-element.174, s32[]{:T(128)S(6)} %select_n.263, pred[]{:T(512)S(6)} %compare.34), kind=kOutput, calls=%fused_computation.8.clone.1 | convolution fusion | flops 541327360 | bytes 1318917 | tf_op jit(solution)/shard_map/while/body/eval_jaxpr/dot_general | solution.py:102
  143.1 4.5 %fusion.59 = f32[64,2048]{1,0:T(8,128)S(1)} fusion(s32[2048]{0:T(1024)S(1)} %dynamic_slice.39, f32[64,2048]{1,0:T(8,128)S(1)} %get-tuple-element.165, bf16[64,40960]{1,0:T(8,128)(2,1)} %get-tuple-element.174, s32[]{:T(128)S(6)} %select_n.263, pred[]{:T(512)S(6)} %compare.34), kind=kOutput, calls=%fused_computation.8.clone.1 | convolution fusion | flops 541327360 | bytes 1318917 | tf_op jit(solution)/shard_map/while/body/eval_jaxpr/dot_general | solution.py:102
  147.6 4.5 %fusion.59 = f32[64,2048]{1,0:T(8,128)S(1)} fusion(s32[2048]{0:T(1024)S(1)} %dynamic_slice.39, f32[64,2048]{1,0:T(8,128)S(1)} %get-tuple-element.165, bf16[64,40960]{1,0:T(8,128)(2,1)} %get-tuple-element.174, s32[]{:T(128)S(6)} %select_n.263, pred[]{:T(512)S(6)} %compare.34), kind=kOutput, calls=%fused_computation.8.clone.1 | convolution fusion | flops 541327360 | bytes 1318917 | tf_op jit(solution)/shard_map/while/body/eval_jaxpr/dot_general | solution.py:102
  152.1 4.5 %fusion.59 = f32[64,2048]{1,0:T(8,128)S(1)} fusion(s32[2048]{0:T(1024)S(1)} %dynamic_slice.39, f32[64,2048]{1,0:T(8,128)S(1)} %get-tuple-element.165, bf16[64,40960]{1,0:T(8,128)(2,1)} %get-tuple-element.174, s32[]{:T(128)S(6)} %select_n.263, pred[]{:T(512)S(6)} %compare.34), kind=kOutput, calls=%fused_computation.8.clone.1 | convolution fusion | flops 541327360 | bytes 1318917 | tf_op jit(solution)/shard_map/while/body/eval_jaxpr/dot_general | solution.py:102
  157.7 30.0 %all-reduce.3.cloned.1.call-done = bf16[2,32,2048]{2,1,0:T(8,128)(2,1)} async-done(((bf16[2,32,2048]{2,1,0:T(8,128)(2,1)}), bf16[2,32,2048]{2,1,0:T(8,128)(2,1)}) %all-reduce.3.cloned.1.call-update) | async-done | bytes 262160 | tf_op jit(solution)/shard_map/psum | solution.py:107
  187.7 68.3 %fusion.27 = bf16[2,8,2048]{2,1,0:T(8,128)(2,1)S(1)} fusion(s32[2048]{0:T(1024)S(1)} %add_select_fusion.6, pred[2048]{0:T(1024)(128)(4,1)S(1)} %fusion.36, bf16[2,32,2048]{2,1,0:T(8,128)(2,1)} %all-reduce.3.cloned.1.call-done, s32[]{:T(128)S(6)} %select_n.186), kind=kOutput, calls=%fused_computation.40 | convolution fusion | flops 205619200 | bytes 141316 | tf_op jit(solution)/shard_map/dot_general | solution.py:109
  257.8 12.2 %all_to_all.25 = bf16[8,2,2048]{2,1,0:T(2,128)(2,1)S(1)} all-to-all(bf16[8,2,2048]{2,1,0:T(2,128)(2,1)S(1)} %reshape.314), channel_id=1, replica_groups=mesh['blk'=8,'beam'=4] {'blk'}, dimensions={0} | all-to-all | bytes 131072 | tf_op jit(solution)/shard_map/all_to_all | solution.py:115
  271.5 22.5 %fusion.23 = bf16[128,2,1152]{2,1,0:T(2,128)(2,1)} fusion(bf16[128,8,16,2]{1,3,0,2:T(2,128)(2,1)S(1)} %bitcast.52, bf16[128,8,16,1152]{3,2,1,0:T(8,128)(2,1)} %param.15), kind=kOutput, calls=%fused_computation.38 | convolution fusion | flops 75792384 | bytes 38404096 | tf_op jit(solution)/shard_map/mqtl,mqtp->mpl/dot_general | solution.py:118
  294.0 30.5 %all-reduce.5.cloned.1.call-done = bf16[128,2,1152]{2,1,0:T(2,128)(2,1)} async-done(((bf16[128,2,1152]{2,1,0:T(2,128)(2,1)}), bf16[128,2,1152]{2,1,0:T(2,128)(2,1)}) %all-reduce.5.cloned.1.call-update) | async-done | bytes 589840 | tf_op jit(solution)/shard_map/psum | solution.py:119
  (68 shorter events, 19.4 us)
Async XLA Ops:
  16.1 14.3 %all-to-all-start.1 = ((bf16[8,2,2560]{2,1,0:T(2,128)(2,1)}), bf16[8,2,2560]{2,1,0:T(2,128)(2,1)S(1)}, u32[]{:S(2)}, u32[]{:S(2)}) async-start(bf16[8,2,2560]{2,1,0:T(2,128)(2,1)} %reshape.312), calls=%async_computation.1 | async-start | bytes 163840 | tf_op jit(solution)/shard_map/all_to_all | solution.py:72
  30.5 10.9 %all-to-all-start = ((s32[1,8,5120]{2,0,1:T(1,128)}), s32[1,8,5120]{2,0,1:T(1,128)S(1)}, u32[]{:S(2)}, u32[]{:S(2)}) async-start(s32[1,8,5120]{2,0,1:T(1,128)} %copy.17), calls=%async_computation | async-start | bytes 327680 | tf_op jit(solution)/shard_map/all_to_all | solution.py:79
  33.9 153.8 %all-reduce.3.cloned.1.call-start = ((), (), s32[]{:S(2)}) async-start(), calls=%async_computation.3 | async-start | bytes 524288 | tf_op jit(solution)/shard_map/psum | solution.py:107
  157.4 167.1 %all-reduce.5.cloned.1.call-start = ((), (), s32[]{:S(2)}) async-start(), calls=%async_computation.4 | async-start | bytes 1179648 | tf_op jit(solution)/shard_map/psum | solution.py:119
Sparse Core Ops, SparseCore 0:
  157.5 30.1 all-reduce.2
  294.1 30.3 all-reduce.4
where the time goes:
time: 334 us; the launch traced here: 333 us
  matrix products  180 us (54%)
  waiting for transfers between devices  71.6 us (21%)
  other arithmetic  33 us (10%)
  between operations  13.7 us (4%)
  blocking collectives  12.2 us (4%)
  starting transfers between devices  11.2 us (3%)
  local copies, waits for them, and re-layouts  10.4 us (3%)
    dot_general x20, matrix products, bin_block(): return carry + jnp.dot(part, onehot, preferred_element_type=jnp.float32)  89.4 us
    dot_general x1, matrix products, shards(): jnp.dot(mine.astype(jnp.bfloat16).reshape(CYCLE_DEV * share, NPHI), phi_t...  68.3 us
    psum x1, waiting for transfers between devices, shards(): lax.psum(partial_sum.astype(jnp.bfloat16), 'beam').astype(jnp.float32)  30.5 us
    psum x1, waiting for transfers between devices, shards(): summed = lax.psum(cube.astype(jnp.bfloat16), 'beam').astype(jnp.float32)  30 us
    dot_general x1, matrix products, shards(): jnp.einsum('mqtl,mqtp->mpl', wigner, coeffs, preferred_element_type=jnp.f...  22.5 us
    select_n x1, other arithmetic, shards(): jnp.where(cycle_of[None, :] == level, received, jnp.zeros_like(received))  21.8 us
    all_to_all x1, blocking collectives, shards(): lax.all_to_all(spectra, 'blk', split_axis=2, concat_axis=0, tiled=True)  12.2 us
    all_to_all x1, starting transfers between devices, shards(): lax.all_to_all(arrange(sample_value[None, :]).astype(jnp.bfloat16), 'blk'...  7.31 us
  transfers between devices with their start and end apart: 4, of which 4 were waited for; matrix products, arithmetic and copies ran while one was open for 1% of the time, Pallas kernels for 0%

commit v1 on v0

v1 whole, which is shorter than its diff:
```python
import math

import jax
import jax.numpy as jnp
import numpy as np
from jax import lax
from jax.experimental import pallas as pl
from jax.experimental.pallas import tpu as pltpu
from jax.sharding import PartitionSpec as P

BLOCK_ROWS = 128
CYCLE_DEV = 2
NPSI = 32
NPHI = 2048
LOW = 256
HIGH = NPHI // LOW
HALF = HIGH // 2
LANES = 128
F32 = jnp.float32
BF16 = jnp.bfloat16


def round_up(value, step):
    return -(-value // step) * step


def psi_matrix():
    component = np.arange(NPSI)[:, None]
    cell = np.arange(NPSI)[None, :]
    middle = NPSI // 2
    frequency = np.where(component <= middle, component, component - middle)
    angles = (frequency * cell % NPSI) * (2.0 * math.pi / NPSI)
    return np.where(component <= middle, np.cos(angles), np.sin(angles)) / math.sqrt(NPSI)


def first_matrix():
    psi = psi_matrix()
    out = np.zeros((2, HALF, NPSI, NPSI, HIGH))
    for parity in range(2):
        for a in range(HIGH):
            sign = -1.0 if parity == 1 and a >= HALF else 1.0
            out[parity, a % HALF, :, :, a] = sign * psi
    return out.reshape(2 * HALF * NPSI, NPSI * HIGH)


def second_tables(groups):
    orders = NPHI // 2 // groups
    width = round_up(orders, LANES)
    f = np.arange(NPHI // 2)
    out = np.zeros((2, NPHI // 2, groups, width))
    for parity in range(2):
        k = np.arange(orders // 2)
        m = np.arange(groups)[:, None] * orders + 2 * k[None, :] + parity
        angles = (f[:, None, None] * m[None] % NPHI) * (2.0 * math.pi / NPHI)
        out[parity, :, :, 0:orders:2] = np.cos(angles)
        out[parity, :, :, 1:orders:2] = np.sin(angles)
    out = out / math.sqrt(NPHI)
    return out.reshape(2, NPHI // 2, groups * width), width


def dot(a, b, ca, cb):
    return lax.dot_general(a, b, (((ca,), (cb,)), ((), ())), preferred_element_type=F32)


def pack_kernel(groups, cap, owner_ref, signal_ref, weight_ref, cycle_ref, phi_ref, psi_ref, out_ref):
    blocks = owner_ref.shape[1]
    padded = out_ref.shape[2]
    owner = owner_ref[...]
    rows = round_up(groups, 8)
    hits = (owner == lax.broadcasted_iota(jnp.int32, (rows, blocks), 0)).astype(F32)
    before = (
        lax.broadcasted_iota(jnp.int32, (blocks, blocks), 0)
        < lax.broadcasted_iota(jnp.int32, (blocks, blocks), 1)
    ).astype(F32)
    earlier = dot(hits.astype(BF16), before.astype(BF16), 1, 0)
    within = jnp.sum(earlier * hits, axis=0, keepdims=True)
    position = owner * padded + within.astype(jnp.int32)
    spread = (
        (position == lax.broadcasted_iota(jnp.int32, (groups * padded, blocks), 0))
        .astype(F32)
        .astype(BF16)
    )
    value = (signal_ref[...] * weight_ref[...]).astype(BF16)
    phi = phi_ref[...]
    high = (psi_ref[...] * HIGH + phi // LOW).astype(F32).astype(BF16)
    low = phi % LOW + 1
    low = jnp.where(cycle_ref[...] == 0, low, -low).astype(F32).astype(BF16)
    for number, plane in enumerate((value, high, low)):
        moved = dot(spread, plane, 1, 0).astype(BF16)
        for group in range(groups):
            out_ref[group, number] = moved[group * padded : (group + 1) * padded]


def bin_kernel(share, step, recv_ref, first_ref, second_ref, out_ref, acc_ref, table_ref, sem):
    groups, _, padded, _ = recv_ref.shape
    width = out_ref.shape[-1]
    copy = pltpu.make_async_copy(second_ref, table_ref, sem)
    copy.start()
    acc_ref[...] = jnp.zeros_like(acc_ref)
    places = lax.broadcasted_iota(jnp.int32, (LOW, LANES), 0).astype(F32)
    places_hi = places.astype(BF16)
    places_lo = (places + 1.0).astype(BF16)
    zero = jnp.zeros((LOW, LANES), BF16)
    one = jnp.ones((LOW, LANES), BF16)

    def one_source(source, carry):
        for start in range(0, padded, step):
            value = recv_ref[source, 0, start : start + step, :]
            high = recv_ref[source, 1, start : start + step, :]
            low = recv_ref[source, 2, start : start + step, :]
            parts = [[], [], []]
            blank = jnp.zeros_like(value)
            value0 = jnp.where(low > 0, value, blank)
            value1 = jnp.where(low > 0, blank, value)
            low = jnp.abs(low)
            for row in range(step):
                same = places_hi == high[row : row + 1, :]
                parts[0].append(jnp.where(same, value0[row : row + 1, :], zero))
                parts[1].append(jnp.where(same, value1[row : row + 1, :], zero))
                parts[2].append(jnp.where(places_lo == low[row : row + 1, :], one, zero))
            left0 = jnp.concatenate(parts[0], axis=1)
            left1 = jnp.concatenate(parts[1], axis=1)
            right = jnp.concatenate(parts[2], axis=1)
            acc_ref[0] += dot(left0, right, 1, 1)
            acc_ref[1] += dot(left1, right, 1, 1)
        return carry

    lax.fori_loop(0, groups, one_source, 0)
    first = first_ref[...]
    mixed = [dot(first, acc_ref[t].astype(BF16), 1, 0).astype(BF16) for t in range(CYCLE_DEV)]
    copy.wait()
    for parity in range(2):
        total = None
        for a0 in range(HALF):
            base = (parity * HALF + a0) * NPSI
            left = jnp.concatenate([part[base : base + NPSI] for part in mixed], axis=0)
            term = dot(left, table_ref[parity, a0 * LOW : (a0 + 1) * LOW, :], 1, 0)
            total = term if total is None else total + term
        total = total.astype(BF16)
        for group in range(groups):
            for beam in range(NPSI // share):
                for t in range(CYCLE_DEV):
                    base = t * NPSI + beam * share
                    out_ref[group, beam, parity, t] = total[
                        base : base + share, group * width : (group + 1) * width
                    ]


def coeff_kernel(groups, orders, recv_ref, out_ref):
    _, beams, _, cycles, share, width = recv_ref.shape
    thetas = groups * cycles
    depth = thetas * share
    row = lax.broadcasted_iota(jnp.int32, (depth, depth), 0)
    column = lax.broadcasted_iota(jnp.int32, (depth, depth), 1)
    swap = ((row % share) * thetas + row // share == column).astype(F32).astype(BF16)
    total = None
    for parity in range(2):
        parts = []
        for group in range(groups):
            for t in range(cycles):
                piece = recv_ref[group, 0, parity, t].astype(F32)
                for beam in range(1, beams):
                    piece = piece + recv_ref[group, beam, parity, t].astype(F32)
                parts.append(piece)
        stacked = jnp.concatenate(parts, axis=0).astype(BF16)
        turned = dot(stacked, swap, 0, 0).astype(BF16)
        row = lax.broadcasted_iota(jnp.int32, (2 * orders, width), 0)
        column = lax.broadcasted_iota(jnp.int32, (2 * orders, width), 1)
        place = (row // 4 * 2 + row % 2 == column) & (row // 2 % 2 == parity)
        term = dot(place.astype(F32).astype(BF16), turned, 1, 0)
        total = term if total is None else total + term
    out_ref[...] = total.astype(BF16)


def order_kernel(chunk, where_ref, coeff_ref, wigner_ref, out_ref):
    depth = coeff_ref.shape[1]
    coeff = coeff_ref[...]
    wide = jnp.concatenate([coeff] * chunk, axis=1)
    row = lax.broadcasted_iota(jnp.int32, wide.shape, 0) // 2
    column = lax.broadcasted_iota(jnp.int32, wide.shape, 1) // depth
    wide = jnp.where(row == column, wide.astype(F32), 0.0).astype(BF16)
    out_ref[...] = dot(wide, wigner_ref[...], 1, 0).astype(out_ref.dtype)


def shards(signal, weight, cycle, phi, psi, owner, wigner):
    groups = lax.axis_size("blk")
    beams = lax.axis_size("beam")
    blocks = owner.shape[0]
    cap = max(2, 5 * blocks // (2 * groups))
    padded = round_up(cap, 8)
    share = NPSI // beams
    orders = wigner.shape[0]
    ells = wigner.shape[3]
    depth = share * groups * CYCLE_DEV

    def square(data):
        return data.reshape(blocks, BLOCK_ROWS)

    sent = pl.pallas_call(
        lambda *refs: pack_kernel(groups, cap, *refs),
        out_shape=jax.ShapeDtypeStruct((groups, 3, padded, BLOCK_ROWS), BF16),
        name="pack",
    )(owner.reshape(1, blocks), square(signal), square(weight), square(cycle), square(phi), square(psi))
    got = lax.all_to_all(sent, "blk", split_axis=0, concat_axis=0, tiled=True)
    tables, width = second_tables(groups)
    whole = pl.BlockSpec(memory_space=pltpu.VMEM)
    spectra = pl.pallas_call(
        lambda *refs: bin_kernel(share, 8, *refs),
        out_shape=jax.ShapeDtypeStruct((groups, beams, 2, CYCLE_DEV, share, width), BF16),
        in_specs=[whole, whole, pl.BlockSpec(memory_space=pl.ANY)],
        scratch_shapes=[
            pltpu.VMEM((CYCLE_DEV, LOW, LOW), F32),
            pltpu.VMEM(tables.shape, BF16),
            pltpu.SemaphoreType.DMA,
        ],
        name="bin",
    )(got, jnp.asarray(first_matrix(), BF16), jnp.asarray(tables, BF16))
    rows = 2 * CYCLE_DEV * share
    spectra = spectra.reshape(groups * beams, rows, width)
    parts = lax.all_to_all(spectra, ("blk", "beam"), split_axis=0, concat_axis=0, tiled=True)
    parts = parts.reshape(groups, beams, 2, CYCLE_DEV, share, width)
    coeff = pl.pallas_call(
        lambda *refs: coeff_kernel(groups, orders, *refs),
        out_shape=jax.ShapeDtypeStruct((2 * orders, depth), BF16),
        name="coeff",
    )(parts)

    me = lax.axis_index("beam").astype(jnp.int32)
    flat = wigner.reshape(orders * depth, ells)
    mine = orders // beams
    chunk = 8
    steps = mine // chunk

    def piece(offset, kind):
        target = (me ^ offset).reshape(1)
        return pl.pallas_call(
            lambda *refs: order_kernel(chunk, *refs),
            out_shape=jax.ShapeDtypeStruct((2 * mine, ells), kind),
            grid_spec=pltpu.PrefetchScalarGridSpec(
                num_scalar_prefetch=1,
                grid=(steps,),
                in_specs=[
                    pl.BlockSpec((2 * chunk, depth), lambda i, at: (at[0] * steps + i, 0)),
                    pl.BlockSpec((chunk * depth, ells), lambda i, at: (at[0] * steps + i, 0)),
                ],
                out_specs=pl.BlockSpec((2 * chunk, ells), lambda i, at: (i, 0)),
            ),
            name="order",
        )(target, coeff, flat)

    total = None
    for offset in range(beams - 1, -1, -1):
        part = piece(offset, BF16 if offset else F32)
        if offset:
            part = lax.ppermute(part, "beam", [(i, i ^ offset) for i in range(beams)])
        part = part.astype(F32)
        total = part if total is None else total + part
    return total.reshape(mine, 2, ells)


def solution(mesh):
    return jax.shard_map(
        shards,
        mesh=mesh,
        in_specs=(
            P(("blk", "beam")),
            P(("blk", "beam")),
            P(("blk", "beam")),
            P(("blk", "beam")),
            P(("blk", "beam")),
            P(("blk", "beam"), None),
            P("blk", "beam", None, None),
        ),
        out_specs=P(("blk", "beam"), None, None),
        check_vma=False,
    )
```

time: 334 us -> 79.3 us (0.24)
  matrix products: 180 us -> 0 us
  waiting for transfers between devices: 71.6 us -> 12.5 us
  Pallas kernels: 0 us -> 42.2 us
  other arithmetic: 33 us -> 1.02 us
  between operations: 13.7 us -> 0.03 us
  local copies, waits for them, and re-layouts: 10.4 us -> 1.59 us
  starting transfers between devices: 11.2 us -> 5.36 us
  blocking collectives: 12.2 us -> 16.1 us
    dot_general x22 -> x0, matrix products: 180 us -> none  [the longest x20 89.4 us: bin_block(): return carry + jnp.dot(part, onehot, preferred_element_type=jnp.float32)]
    psum x2 -> x0, waiting for transfers between devices: 60.6 us -> none  [the longest x1 30.5 us: shards(): lax.psum(partial_sum.astype(jnp.bfloat16), 'beam').astype(jnp.float32)]
    pallas_call x0 -> x7, Pallas kernels: none -> 42.2 us  [the longest x4 22.9 us: piece(): pl.pallas_call(lambda *refs: order_kernel(chunk, *refs), out_shape=jax.Sh...]
    select_n x7 -> x0, other arithmetic: 22.8 us -> none  [the longest x1 21.8 us: shards(): jnp.where(cycle_of[None, :] == level, received, jnp.zeros_like(received))]
    all_to_all x2 -> x1, starting transfers between devices: 10.7 us -> 3.49 us  [shards(): lax.all_to_all(spectra, ('blk', 'beam'), split_axis=0, concat_axis=0, til...]
    all_to_all x1, blocking collectives: 12.2 us -> 16.1 us  [shards(): got = lax.all_to_all(sent, 'blk', split_axis=0, concat_axis=0, tiled=True)]
    all_to_all x2 -> x1, waiting for transfers between devices: 11 us -> 10.6 us  [shards(): lax.all_to_all(spectra, ('blk', 'beam'), split_axis=0, concat_axis=0, til...]
  transfers between devices with their start and end apart: 4 -> 4, of which waited for: 4 -> 2; matrix products, arithmetic and copies ran while one was open for 1% -> 0% of each run, Pallas kernels for 0% -> 7%
where the time goes in v1:
time: 79.3 us; the launch traced here: 78.7 us
  Pallas kernels  42.2 us (53%)
  blocking collectives  16.1 us (20%)
  waiting for transfers between devices  12.5 us (16%)
  starting transfers between devices  5.36 us (7%)
  local copies, waits for them, and re-layouts  1.59 us (2%)
  other arithmetic  1.02 us (1%)
    pallas_call x4, Pallas kernels, piece(): pl.pallas_call(lambda *refs: order_kernel(chunk, *refs), out_shape=jax.Sh...  22.9 us
    all_to_all x1, blocking collectives, shards(): got = lax.all_to_all(sent, 'blk', split_axis=0, concat_axis=0, tiled=True)  16.1 us
    pallas_call x1, Pallas kernels, shards(): pl.pallas_call(lambda *refs: bin_kernel(share, 8, *refs), out_shape=jax.S...  15.3 us
    all_to_all x1, waiting for transfers between devices, shards(): lax.all_to_all(spectra, ('blk', 'beam'), split_axis=0, concat_axis=0, til...  10.6 us
    all_to_all x1, starting transfers between devices, shards(): lax.all_to_all(spectra, ('blk', 'beam'), split_axis=0, concat_axis=0, til...  3.49 us
    pallas_call x1, Pallas kernels, shards(): pl.pallas_call(lambda *refs: pack_kernel(groups, cap, *refs), out_shape=j...  2.02 us
    pallas_call x1, Pallas kernels, shards(): pl.pallas_call(lambda *refs: coeff_kernel(groups, orders, *refs), out_sha...  1.95 us
    ppermute x3, waiting for transfers between devices, shards(): part = lax.ppermute(part, 'beam', [(i, i ^ offset) for i in range(beams)])  1.92 us
  transfers between devices with their start and end apart: 4, of which 2 were waited for; matrix products, arithmetic and copies ran while one was open for 0% of the time, Pallas kernels for 7%

profile of v1, /device:TPU:0, one launch (start us, length us, event | category | flops | bytes accessed | tf_op | source)
XLA Modules:
  0.0 78.7 jit_solution(13900491919876309629)
XLA Ops:
  0.0 2.0 %pack.1 = bf16[8,3,40,128]{3,2,1,0:T(8,128)(2,1)} custom-call(s32[1,128]{1,0:T(1,128)} %bitcast.24, f32[128,128]{1,0:T(8,128)} %bitcast.19, f32[128,128]{1,0:T(8,128)} %bitcast.20, s32[128,128]{1,0:T(8,128)} %bitcast.21, s32[128,128]{1,0:T(8,128)} %bitcast.22, s32[128,128]{1,0:T(8,128)} %bitcast.23), custom_call_target="tpu_custom_call" | custom-call | tf_op jit(solution)/shard_map/pack/pallas_call | solution.py:199
  2.0 16.1 %all_to_all.10.refs_0_ = bf16[8,3,40,128]{3,2,1,0:T(8,128)(2,1)} all-to-all(bf16[8,3,40,128]{3,2,1,0:T(8,128)(2,1)} %pack.1), channel_id=1, replica_groups=mesh['blk'=8,'beam'=4] {'blk'}, dimensions={0} | all-to-all | bytes 491520 | tf_op jit(solution)/shard_map/all_to_all | solution.py:204
  18.1 15.3 %bin.1 = bf16[8,4,2,2,8,128]{5,4,3,2,1,0:T(8,128)(2,1)} custom-call(bf16[8,3,40,128]{3,2,1,0:T(8,128)(2,1)} %all_to_all.10.refs_0_, bf16[256,256]{1,0:T(8,128)(2,1)} %constant.14.clone.refs_1_, bf16[2,1024,1024]{2,1,0:T(8,128)(2,1)} %constant.15.clone.refs_2_), custom_call_target="tpu_custom_call" | custom-call | tf_op jit(solution)/shard_map/bin/pallas_call | solution.py:207
  33.4 3.5 %all-to-all-start.1 = ((bf16[32,32,128]{2,1,0:T(8,128)(2,1)}), bf16[32,32,128]{2,1,0:T(8,128)(2,1)S(1)}, u32[]{:S(2)}, u32[]{:S(2)}) async-start(bf16[32,32,128]{2,1,0:T(8,128)(2,1)} %bitcast.17), calls=%async_computation.1 | async-start | bytes 524288 | tf_op jit(solution)/shard_map/all_to_all | solution.py:220
  36.9 10.6 %all-to-all-done.1 = bf16[32,32,128]{2,1,0:T(8,128)(2,1)S(1)} async-done(((bf16[32,32,128]{2,1,0:T(8,128)(2,1)}), bf16[32,32,128]{2,1,0:T(8,128)(2,1)S(1)}, u32[]{:S(2)}, u32[]{:S(2)}) %all-to-all-start.1) | async-done | bytes 262176 | tf_op jit(solution)/shard_map/all_to_all | solution.py:220
  47.5 0.0 copy-start
  47.5 0.7 copy-done
  48.2 1.9 %coeff.1.refs_1_ = bf16[256,128]{1,0:T(8,128)(2,1)} custom-call(bf16[8,4,2,2,8,128]{5,4,3,2,1,0:T(8,128)(2,1)} %bitcast.18), custom_call_target="tpu_custom_call" | custom-call | tf_op jit(solution)/shard_map/coeff/pallas_call | solution.py:222
  50.1 5.7 %order.6 = bf16[64,1152]{1,0:T(8,128)(2,1)} custom-call(s32[1]{0:T(128)} %bitcast.11.refs_0_, bf16[256,128]{1,0:T(8,128)(2,1)} %coeff.1.refs_1_, bf16[16384,1152]{1,0:T(8,128)(2,1)} %bitcast.13), custom_call_target="tpu_custom_call" | custom-call | tf_op jit(solution)/shard_map/order/pallas_call | solution.py:236
  55.8 0.0 copy-start.1
  55.8 5.7 %order.5 = bf16[64,1152]{1,0:T(8,128)(2,1)} custom-call(s32[1]{0:T(128)} %bitcast.10.refs_0_, bf16[256,128]{1,0:T(8,128)(2,1)} %coeff.1.refs_1_, bf16[16384,1152]{1,0:T(8,128)(2,1)} %bitcast.14), custom_call_target="tpu_custom_call" | custom-call | tf_op jit(solution)/shard_map/order/pallas_call | solution.py:236
  61.6 0.0 copy-start.2
  61.6 5.7 %order.4 = bf16[64,1152]{1,0:T(8,128)(2,1)} custom-call(s32[1]{0:T(128)} %bitcast.refs_0_, bf16[256,128]{1,0:T(8,128)(2,1)} %coeff.1.refs_1_, bf16[16384,1152]{1,0:T(8,128)(2,1)} %bitcast.15), custom_call_target="tpu_custom_call" | custom-call | tf_op jit(solution)/shard_map/order/pallas_call | solution.py:236
  67.3 0.4 collective-permute-start
  67.7 0.0 copy-done.2
  67.7 1.1 %collective-permute-start.1 = (bf16[64,1152]{1,0:T(8,128)(2,1)S(1)}, bf16[64,1152]{1,0:T(8,128)(2,1)S(1)}, u32[]{:S(2)}, u32[]{:S(2)}) collective-permute-start(bf16[64,1152]{1,0:T(8,128)(2,1)S(1)} %copy-done.2), channel_id=1, source_target_pairs={{0,2},{1,3},{2,0},{3,1},{4,6},{5,7},{6,4},{7,5},{8,10},{9,11},{10,... | collective-permute-start | bytes 442376 | tf_op jit(solution)/shard_map/ppermute | solution.py:255
  68.9 0.0 copy-done.1
  68.9 0.3 collective-permute-start.2
  69.2 5.7 %order.7 = f32[64,1152]{1,0:T(8,128)} custom-call(s32[1]{0:T(128)} %bitcast.12.refs_0_, bf16[256,128]{1,0:T(8,128)(2,1)} %coeff.1.refs_1_, bf16[16384,1152]{1,0:T(8,128)(2,1)} %bitcast.16), custom_call_target="tpu_custom_call" | custom-call | tf_op jit(solution)/shard_map/order/pallas_call | solution.py:236
  74.9 0.0 collective-permute-done
  74.9 1.9 %collective-permute-done.1 = bf16[64,1152]{1,0:T(8,128)(2,1)S(1)} collective-permute-done((bf16[64,1152]{1,0:T(8,128)(2,1)S(1)}, bf16[64,1152]{1,0:T(8,128)(2,1)S(1)}, u32[]{:S(2)}, u32[]{:S(2)}) %collective-permute-start.1) | collective-permute-done | bytes 147488 | tf_op jit(solution)/shard_map/ppermute | solution.py:255
  76.8 0.0 collective-permute-done.2
  76.8 1.0 %add_add_fusion = f32[64,1152]{1,0:T(8,128)S(1)} fusion(f32[64,1152]{1,0:T(8,128)} %order.7, bf16[64,1152]{1,0:T(8,128)(2,1)S(1)} %collective-permute-done.2, bf16[64,1152]{1,0:T(8,128)(2,1)S(1)} %collective-permute-done.1, bf16[64,1152]{1,0:T(8,128)(2,1)S(1)} %collective-permute-done), kind=kLoop, calls=%fused_computation | loop fusion | flops 442368 | bytes 1032192 | tf_op jit(solution)/shard_map/add | solution.py:257
  77.9 0.9 %reshape.55 = f32[32,2,1152]{2,1,0:T(2,128)} reshape(f32[64,1152]{1,0:T(8,128)S(1)} %add_add_fusion) | data formatting | bytes 589824 | tf_op jit(solution)/shard_map/reshape | solution.py:258
Async XLA Ops:
  33.4 14.1 %all-to-all-start.1 = ((bf16[32,32,128]{2,1,0:T(8,128)(2,1)}), bf16[32,32,128]{2,1,0:T(8,128)(2,1)S(1)}, u32[]{:S(2)}, u32[]{:S(2)}) async-start(bf16[32,32,128]{2,1,0:T(8,128)(2,1)} %bitcast.17), calls=%async_computation.1 | async-start | bytes 524288 | tf_op jit(solution)/shard_map/all_to_all | solution.py:220
  47.5 0.7 copy-start
  55.8 13.0 %copy-start.1 = (bf16[64,1152]{1,0:T(8,128)(2,1)S(1)}, bf16[64,1152]{1,0:T(8,128)(2,1)}, u32[]{:S(2)}) copy-start(bf16[64,1152]{1,0:T(8,128)(2,1)} %order.6) | copy-start | bytes 442372
  61.6 6.2 %copy-start.2 = (bf16[64,1152]{1,0:T(8,128)(2,1)S(1)}, bf16[64,1152]{1,0:T(8,128)(2,1)}, u32[]{:S(2)}) copy-start(bf16[64,1152]{1,0:T(8,128)(2,1)} %order.5) | copy-start | bytes 442372
  67.3 7.6 %collective-permute-start = (bf16[64,1152]{1,0:T(8,128)(2,1)}, bf16[64,1152]{1,0:T(8,128)(2,1)S(1)}, u32[]{:S(2)}, u32[]{:S(2)}) collective-permute-start(bf16[64,1152]{1,0:T(8,128)(2,1)} %order.4), channel_id=1, source_target_pairs={{0,3},{1,2},{2,1},{3,0},{4,7},{5,6},{6,5},{7,4},{8,11},{9,10},{10,... | collective-permute-start | bytes 442376 | tf_op jit(solution)/shard_map/ppermute | solution.py:255
  67.7 9.1 %collective-permute-start.1 = (bf16[64,1152]{1,0:T(8,128)(2,1)S(1)}, bf16[64,1152]{1,0:T(8,128)(2,1)S(1)}, u32[]{:S(2)}, u32[]{:S(2)}) collective-permute-start(bf16[64,1152]{1,0:T(8,128)(2,1)S(1)} %copy-done.2), channel_id=1, source_target_pairs={{0,2},{1,3},{2,0},{3,1},{4,6},{5,7},{6,4},{7,5},{8,10},{9,11},{10,... | collective-permute-start | bytes 442376 | tf_op jit(solution)/shard_map/ppermute | solution.py:255
  68.9 8.0 %collective-permute-start.2 = (bf16[64,1152]{1,0:T(8,128)(2,1)S(1)}, bf16[64,1152]{1,0:T(8,128)(2,1)S(1)}, u32[]{:S(2)}, u32[]{:S(2)}) collective-permute-start(bf16[64,1152]{1,0:T(8,128)(2,1)S(1)} %copy-done.1), channel_id=1, source_target_pairs={{0,1},{1,0},{2,3},{3,2},{4,5},{5,4},{6,7},{7,6},{8,9},{9,8},{10,11... | collective-permute-start | bytes 442376 | tf_op jit(solution)/shard_map/ppermute | solution.py:255

commit v2 on v1

--- a/solution.py
+++ b/solution.py
@@ -62,7 +62,9 @@
     return lax.dot_general(a, b, (((ca,), (cb,)), ((), ())), preferred_element_type=F32)
 
 
-def pack_kernel(groups, cap, owner_ref, signal_ref, weight_ref, cycle_ref, phi_ref, psi_ref, out_ref):
+def pack_kernel(groups, me_ref, owner_ref, signal_ref, weight_ref, cycle_ref, phi_ref, psi_ref, out_ref, targets_ref):
+    for offset in range(targets_ref.shape[0]):
+        targets_ref[offset] = me_ref[0] ^ offset
     blocks = owner_ref.shape[1]
     padded = out_ref.shape[2]
     owner = owner_ref[...]
@@ -91,11 +93,18 @@
             out_ref[group, number] = moved[group * padded : (group + 1) * padded]
 
 
-def bin_kernel(share, step, recv_ref, first_ref, second_ref, out_ref, acc_ref, table_ref, sem):
+def bin_kernel(share, step, targets_ref, recv_ref, first_ref, second_ref, wigner_ref, out_ref, *rest):
+    *held_refs, acc_ref, table_ref, sem, held_sem = rest
     groups, _, padded, _ = recv_ref.shape
     width = out_ref.shape[-1]
     copy = pltpu.make_async_copy(second_ref, table_ref, sem)
     copy.start()
+    held = []
+    size = held_refs[0].shape[0]
+    for offset, held_ref in enumerate(held_refs):
+        source = wigner_ref.at[pl.ds(targets_ref[offset] * size, size), :]
+        held.append(pltpu.make_async_copy(source, held_ref, held_sem.at[offset]))
+        held[-1].start()
     acc_ref[...] = jnp.zeros_like(acc_ref)
     places = lax.broadcasted_iota(jnp.int32, (LOW, LANES), 0).astype(F32)
     places_hi = places.astype(BF16)
@@ -144,6 +153,8 @@
                     out_ref[group, beam, parity, t] = total[
                         base : base + share, group * width : (group + 1) * width
                     ]
+    for one in held:
+        one.wait()
 
 
 def coeff_kernel(groups, orders, recv_ref, out_ref):
@@ -172,14 +183,15 @@
     out_ref[...] = total.astype(BF16)
 
 
-def order_kernel(chunk, where_ref, coeff_ref, wigner_ref, out_ref):
+def order_kernel(chunk, offset, where_ref, coeff_ref, wigner_ref, out_ref):
     depth = coeff_ref.shape[1]
+    step = pl.program_id(0)
     coeff = coeff_ref[...]
     wide = jnp.concatenate([coeff] * chunk, axis=1)
     row = lax.broadcasted_iota(jnp.int32, wide.shape, 0) // 2
     column = lax.broadcasted_iota(jnp.int32, wide.shape, 1) // depth
     wide = jnp.where(row == column, wide.astype(F32), 0.0).astype(BF16)
-    out_ref[...] = dot(wide, wigner_ref[...], 1, 0).astype(out_ref.dtype)
+    out_ref[...] = dot(wide, wigner_ref[pl.ds(step * chunk * depth, chunk * depth), :], 1, 0).astype(out_ref.dtype)
 
 
 def shards(signal, weight, cycle, phi, psi, owner, wigner):
@@ -196,25 +208,45 @@
     def square(data):
         return data.reshape(blocks, BLOCK_ROWS)
 
-    sent = pl.pallas_call(
-        lambda *refs: pack_kernel(groups, cap, *refs),
-        out_shape=jax.ShapeDtypeStruct((groups, 3, padded, BLOCK_ROWS), BF16),
+    whole = pl.BlockSpec(memory_space=pltpu.VMEM)
+    me = lax.axis_index("beam").astype(jnp.int32)
+    sent, targets = pl.pallas_call(
+        lambda *refs: pack_kernel(groups, *refs),
+        out_shape=(
+            jax.ShapeDtypeStruct((groups, 3, padded, BLOCK_ROWS), BF16),
+            jax.ShapeDtypeStruct((beams,), jnp.int32),
+        ),
+        in_specs=[pl.BlockSpec(memory_space=pltpu.SMEM)] + [whole] * 6,
+        out_specs=(whole, pl.BlockSpec(memory_space=pltpu.SMEM)),
+        compiler_params=pltpu.CompilerParams(vmem_limit_bytes=6 << 20),
         name="pack",
-    )(owner.reshape(1, blocks), square(signal), square(weight), square(cycle), square(phi), square(psi))
+    )(me.reshape(1), owner.reshape(1, blocks), square(signal), square(weight), square(cycle), square(phi), square(psi))
     got = lax.all_to_all(sent, "blk", split_axis=0, concat_axis=0, tiled=True)
     tables, width = second_tables(groups)
-    whole = pl.BlockSpec(memory_space=pltpu.VMEM)
-    spectra = pl.pallas_call(
+    flat = wigner.reshape(orders * depth, ells)
+    spectra, *held = pl.pallas_call(
         lambda *refs: bin_kernel(share, 8, *refs),
-        out_shape=jax.ShapeDtypeStruct((groups, beams, 2, CYCLE_DEV, share, width), BF16),
-        in_specs=[whole, whole, pl.BlockSpec(memory_space=pl.ANY)],
+        out_shape=(
+            jax.ShapeDtypeStruct((groups, beams, 2, CYCLE_DEV, share, width), BF16),
+        )
+        + tuple(pltpu.VMEM((flat.shape[0] // beams, ells), BF16) for _ in range(beams)),
+        in_specs=[
+            pl.BlockSpec(memory_space=pltpu.SMEM),
+            whole,
+            whole,
+            pl.BlockSpec(memory_space=pltpu.HBM),
+            pl.BlockSpec(memory_space=pl.ANY),
+        ],
+        out_specs=(whole,) * (1 + beams),
         scratch_shapes=[
             pltpu.VMEM((CYCLE_DEV, LOW, LOW), F32),
             pltpu.VMEM(tables.shape, BF16),
             pltpu.SemaphoreType.DMA,
+            pltpu.SemaphoreType.DMA((beams,)),
         ],
+        compiler_params=pltpu.CompilerParams(vmem_limit_bytes=2 * tables.size + (4 << 20)),
         name="bin",
-    )(got, jnp.asarray(first_matrix(), BF16), jnp.asarray(tables, BF16))
+    )(targets, got, jnp.asarray(first_matrix(), BF16), pltpu.with_memory_space_constraint(jnp.asarray(tables, BF16), pltpu.HBM), flat)
     rows = 2 * CYCLE_DEV * share
     spectra = spectra.reshape(groups * beams, rows, width)
     parts = lax.all_to_all(spectra, ("blk", "beam"), split_axis=0, concat_axis=0, tiled=True)
@@ -222,31 +254,30 @@
     coeff = pl.pallas_call(
         lambda *refs: coeff_kernel(groups, orders, *refs),
         out_shape=jax.ShapeDtypeStruct((2 * orders, depth), BF16),
+        compiler_params=pltpu.CompilerParams(vmem_limit_bytes=6 << 20),
         name="coeff",
     )(parts)
 
-    me = lax.axis_index("beam").astype(jnp.int32)
-    flat = wigner.reshape(orders * depth, ells)
     mine = orders // beams
     chunk = 8
     steps = mine // chunk
 
     def piece(offset, kind):
-        target = (me ^ offset).reshape(1)
         return pl.pallas_call(
-            lambda *refs: order_kernel(chunk, *refs),
+            lambda *refs: order_kernel(chunk, offset, *refs),
             out_shape=jax.ShapeDtypeStruct((2 * mine, ells), kind),
             grid_spec=pltpu.PrefetchScalarGridSpec(
                 num_scalar_prefetch=1,
                 grid=(steps,),
                 in_specs=[
-                    pl.BlockSpec((2 * chunk, depth), lambda i, at: (at[0] * steps + i, 0)),
-                    pl.BlockSpec((chunk * depth, ells), lambda i, at: (at[0] * steps + i, 0)),
+                    pl.BlockSpec((2 * chunk, depth), lambda i, at: (at[offset] * steps + i, 0)),
+                    pl.BlockSpec(memory_space=pltpu.VMEM),
                 ],
                 out_specs=pl.BlockSpec((2 * chunk, ells), lambda i, at: (i, 0)),
             ),
+            compiler_params=pltpu.CompilerParams(vmem_limit_bytes=6 << 20),
             name="order",
-        )(target, coeff, flat)
+        )(targets, coeff, pltpu.with_memory_space_constraint(held[offset], pltpu.VMEM))
 
     total = None
     for offset in range(beams - 1, -1, -1):

time: 79.3 us -> 68.1 us (0.86)
  Pallas kernels: 42.2 us -> 24.2 us
  blocking collectives: 16.1 us -> 29.7 us
  waiting for transfers between devices: 12.5 us -> 5.2 us
  local copies, waits for them, and re-layouts: 1.59 us -> 6.63 us
  starting transfers between devices: 5.36 us -> 1.93 us
  other arithmetic: 1.02 us -> 0.06 us
    pallas_call x6, Pallas kernels: 40.2 us -> 23.8 us  [the longest x1 14.1 us: shards(): pl.pallas_call(lambda *refs: bin_kernel(share, 8, *refs), out_shape=(jax....]
    all_to_all x0 -> x1, blocking collectives: none -> 13.9 us  [shards(): lax.all_to_all(spectra, ('blk', 'beam'), split_axis=0, concat_axis=0, til...]
    all_to_all x1 -> x0, waiting for transfers between devices: 10.6 us -> none  [shards(): lax.all_to_all(spectra, ('blk', 'beam'), split_axis=0, concat_axis=0, til...]
    unnamed x6 -> x14, local copies, waits for them, and re-layouts: 0.71 us -> 5.75 us
    all_to_all x1 -> x0, starting transfers between devices: 3.49 us -> none  [shards(): lax.all_to_all(spectra, ('blk', 'beam'), split_axis=0, concat_axis=0, til...]
    ppermute x3, waiting for transfers between devices: 1.92 us -> 5.2 us  [shards(): part = lax.ppermute(part, 'beam', [(i, i ^ offset) for i in range(beams)])]
    pallas_call x1, Pallas kernels: 1.95 us -> 0.38 us  [shards(): pl.pallas_call(lambda *refs: coeff_kernel(groups, orders, *refs), out_sha...]
    add x1, other arithmetic: 1.02 us -> 0.06 us  [shards(): total = part if total is None else total + part]
  transfers between devices with their start and end apart: 4 -> 3, of which waited for: 2 -> 2; matrix products, arithmetic and copies ran while one was open for 0% -> 0% of each run, Pallas kernels for 7% -> 3%
where the time goes in v2:
time: 68.1 us; the launch traced here: 67.7 us
  blocking collectives  29.7 us (44%)
  Pallas kernels  24.2 us (36%)
  local copies, waits for them, and re-layouts  6.63 us (10%)
  waiting for transfers between devices  5.2 us (8%)
  starting transfers between devices  1.93 us (3%)
    all_to_all x1, blocking collectives, shards(): got = lax.all_to_all(sent, 'blk', split_axis=0, concat_axis=0, tiled=True)  15.8 us
    pallas_call x1, Pallas kernels, shards(): pl.pallas_call(lambda *refs: bin_kernel(share, 8, *refs), out_shape=(jax....  14.1 us
    all_to_all x1, blocking collectives, shards(): lax.all_to_all(spectra, ('blk', 'beam'), split_axis=0, concat_axis=0, til...  13.9 us
    pallas_call x4, Pallas kernels, piece(): pl.pallas_call(lambda *refs: order_kernel(chunk, offset, *refs), out_shap...  9.01 us
    unnamed x14, local copies, waits for them, and re-layouts  5.75 us
    ppermute x3, waiting for transfers between devices, shards(): part = lax.ppermute(part, 'beam', [(i, i ^ offset) for i in range(beams)])  5.2 us
    ppermute x3, starting transfers between devices, shards(): part = lax.ppermute(part, 'beam', [(i, i ^ offset) for i in range(beams)])  1.93 us
  transfers between devices with their start and end apart: 3, of which 2 were waited for; matrix products, arithmetic and copies ran while one was open for 0% of the time, Pallas kernels for 3%

profile of v2, /device:TPU:0, one launch (start us, length us, event | category | flops | bytes accessed | tf_op | source)
XLA Modules:
  0.0 67.7 jit_solution(17960533723536550758)
XLA Ops:
  0.0 0.0 copy-start.1
  0.0 0.8 %copy-done.1 = f32[16384]{0:T(1024)S(1)} copy-done((f32[16384]{0:T(1024)S(1)}, f32[16384]{0:T(1024)}, u32[]{:S(2)}) %copy-start.1) | copy-done | bytes 65560
  0.8 0.0 copy-start.2
  0.8 0.8 %copy-done.2 = f32[16384]{0:T(1024)S(1)} copy-done((f32[16384]{0:T(1024)S(1)}, f32[16384]{0:T(1024)}, u32[]{:S(2)}) %copy-start.2) | copy-done | bytes 65560
  1.7 0.0 copy-start.3
  1.7 0.8 %copy-done.3 = s32[16384]{0:T(1024)S(1)} copy-done((s32[16384]{0:T(1024)S(1)}, s32[16384]{0:T(1024)}, u32[]{:S(2)}) %copy-start.3) | copy-done | bytes 65560
  2.5 0.0 copy-start.4
  2.5 0.8 %copy-done.4 = s32[16384]{0:T(1024)S(1)} copy-done((s32[16384]{0:T(1024)S(1)}, s32[16384]{0:T(1024)}, u32[]{:S(2)}) %copy-start.4) | copy-done | bytes 65560
  3.4 0.0 copy-start.5
  3.4 0.8 %copy-done.5 = s32[16384]{0:T(1024)S(1)} copy-done((s32[16384]{0:T(1024)S(1)}, s32[16384]{0:T(1024)}, u32[]{:S(2)}) %copy-start.5) | copy-done | bytes 65560
  4.2 0.0 copy-start.6
  4.2 0.7 copy-done.6
  4.9 0.6 pack.1
  5.5 15.8 %all_to_all.10.refs_1_ = bf16[8,3,40,128]{3,2,1,0:T(8,128)(2,1)S(1)} all-to-all(bf16[8,3,40,128]{3,2,1,0:T(8,128)(2,1)S(1)} %get-tuple-element.13), channel_id=1, replica_groups=mesh['blk'=8,'beam'=4] {'blk'}, dimensions={0} | all-to-all | bytes 491520 | tf_op jit(solution)/shard_map/all_to_all | solution.py:224
  21.3 0.0 copy-start
  21.3 0.9 %copy-done = bf16[256,256]{1,0:T(8,128)(2,1)S(1)} copy-done((bf16[256,256]{1,0:T(8,128)(2,1)S(1)}, bf16[256,256]{1,0:T(8,128)(2,1)}, u32[]{:S(2)}) %copy-start) | copy-done | bytes 131096
  22.2 14.1 %bin.1 = (bf16[8,4,2,2,8,128]{5,4,3,2,1,0:T(8,128)(2,1)S(1)}, bf16[4096,1152]{1,0:T(8,128)(2,1)S(1)}, bf16[4096,1152]{1,0:T(8,128)(2,1)S(1)}, bf16[4096,1152]{1,0:T(8,128)(2,1)S(1)}, bf16[4096,1152]{1,0:T(8,128)(2,1)S(1)}) custom-call(s32[4]{0:T(128)S(1)} %get-tuple-element.12.refs_0_, bf16[8,3,40,128]{3,2,1,0:T(8,128)(2,1)S(1)} %all_to_all.10.refs_1_, ...), custom_call_target="tpu_custom_call" | custom-call | tf_op jit(solution)/shard_map/bin/pallas_call | solution.py:227
  36.3 13.9 %all_to_all.11 = bf16[32,32,128]{2,1,0:T(8,128)(2,1)S(1)} all-to-all(bf16[32,32,128]{2,1,0:T(8,128)(2,1)S(1)} %bitcast.11), channel_id=1, replica_groups=mesh['blk'=8,'beam'=4] {'blk','beam'}, dimensions={0} | all-to-all | bytes 524288 | tf_op jit(solution)/shard_map/all_to_all | solution.py:252
  50.2 0.4 coeff.1.refs_1_
  50.6 2.3 %order.6 = bf16[64,1152]{1,0:T(8,128)(2,1)S(1)} custom-call(s32[4]{0:T(128)S(1)} %get-tuple-element.12.refs_0_, bf16[256,128]{1,0:T(8,128)(2,1)S(1)} %coeff.1.refs_1_, bf16[4096,1152]{1,0:T(8,128)(2,1)S(1)} %get-tuple-element.17.refs_2_), custom_call_target="tpu_custom_call" | custom-call | tf_op jit(solution)/shard_map/order/pallas_call | solution.py:266
  52.9 2.3 %order.5 = bf16[64,1152]{1,0:T(8,128)(2,1)S(1)} custom-call(s32[4]{0:T(128)S(1)} %get-tuple-element.12.refs_0_, bf16[256,128]{1,0:T(8,128)(2,1)S(1)} %coeff.1.refs_1_, bf16[4096,1152]{1,0:T(8,128)(2,1)S(1)} %get-tuple-element.16.refs_2_), custom_call_target="tpu_custom_call" | custom-call | tf_op jit(solution)/shard_map/order/pallas_call | solution.py:266
  55.1 2.3 %order.4 = bf16[64,1152]{1,0:T(8,128)(2,1)S(1)} custom-call(s32[4]{0:T(128)S(1)} %get-tuple-element.12.refs_0_, bf16[256,128]{1,0:T(8,128)(2,1)S(1)} %coeff.1.refs_1_, bf16[4096,1152]{1,0:T(8,128)(2,1)S(1)} %get-tuple-element.15.refs_2_), custom_call_target="tpu_custom_call" | custom-call | tf_op jit(solution)/shard_map/order/pallas_call | solution.py:266
  57.4 0.5 collective-permute-start
  57.9 1.1 %collective-permute-start.1 = (bf16[64,1152]{1,0:T(8,128)(2,1)S(1)}, bf16[64,1152]{1,0:T(8,128)(2,1)S(1)}, u32[]{:S(2)}, u32[]{:S(2)}) collective-permute-start(bf16[64,1152]{1,0:T(8,128)(2,1)S(1)} %order.5), channel_id=1, source_target_pairs={{0,2},{1,3},{2,0},{3,1},{4,6},{5,7},{6,4},{7,5},{8,10},{9,11},{10,... | collective-permute-start | bytes 442376 | tf_op jit(solution)/shard_map/ppermute | solution.py:286
  59.0 0.3 collective-permute-start.2
  59.3 2.2 %order.7 = f32[64,1152]{1,0:T(8,128)S(1)} custom-call(s32[4]{0:T(128)S(1)} %get-tuple-element.12.refs_0_, bf16[256,128]{1,0:T(8,128)(2,1)S(1)} %coeff.1.refs_1_, bf16[4096,1152]{1,0:T(8,128)(2,1)S(1)} %get-tuple-element.18.refs_2_), custom_call_target="tpu_custom_call" | custom-call | tf_op jit(solution)/shard_map/order/pallas_call | solution.py:266
  61.6 1.9 %collective-permute-done = bf16[64,1152]{1,0:T(8,128)(2,1)S(1)} collective-permute-done((bf16[64,1152]{1,0:T(8,128)(2,1)S(1)}, bf16[64,1152]{1,0:T(8,128)(2,1)S(1)}, u32[]{:S(2)}, u32[]{:S(2)}) %collective-permute-start) | collective-permute-done | bytes 147488 | tf_op jit(solution)/shard_map/ppermute | solution.py:286
  63.5 3.3 %collective-permute-done.1 = bf16[64,1152]{1,0:T(8,128)(2,1)S(1)} collective-permute-done((bf16[64,1152]{1,0:T(8,128)(2,1)S(1)}, bf16[64,1152]{1,0:T(8,128)(2,1)S(1)}, u32[]{:S(2)}, u32[]{:S(2)}) %collective-permute-start.1) | collective-permute-done | bytes 147488 | tf_op jit(solution)/shard_map/ppermute | solution.py:286
  66.8 0.0 collective-permute-done.2
  66.8 0.1 add_add_fusion
  66.8 0.9 %reshape.43 = f32[32,2,1152]{2,1,0:T(2,128)} reshape(f32[64,1152]{1,0:T(8,128)S(1)} %add_add_fusion) | data formatting | bytes 589824 | tf_op jit(solution)/shard_map/reshape | solution.py:289
Async XLA Ops:
  0.0 0.8 %copy-start.1 = (f32[16384]{0:T(1024)S(1)}, f32[16384]{0:T(1024)}, u32[]{:S(2)}) copy-start(f32[16384]{0:T(1024)} %param.9) | copy-start | bytes 196612
  0.8 0.8 %copy-start.2 = (f32[16384]{0:T(1024)S(1)}, f32[16384]{0:T(1024)}, u32[]{:S(2)}) copy-start(f32[16384]{0:T(1024)} %param.10) | copy-start | bytes 196612
  1.7 0.8 %copy-start.3 = (s32[16384]{0:T(1024)S(1)}, s32[16384]{0:T(1024)}, u32[]{:S(2)}) copy-start(s32[16384]{0:T(1024)} %param.11) | copy-start | bytes 196612
  2.5 0.8 %copy-start.4 = (s32[16384]{0:T(1024)S(1)}, s32[16384]{0:T(1024)}, u32[]{:S(2)}) copy-start(s32[16384]{0:T(1024)} %param.12) | copy-start | bytes 196612
  3.4 0.8 %copy-start.5 = (s32[16384]{0:T(1024)S(1)}, s32[16384]{0:T(1024)}, u32[]{:S(2)}) copy-start(s32[16384]{0:T(1024)} %param.13) | copy-start | bytes 196612
  4.2 0.7 copy-start.6
  21.3 0.9 %copy-start = (bf16[256,256]{1,0:T(8,128)(2,1)S(1)}, bf16[256,256]{1,0:T(8,128)(2,1)}, u32[]{:S(2)}) copy-start(bf16[256,256]{1,0:T(8,128)(2,1)} %constant.8.clone.refs_2_) | copy-start | bytes 393220
  57.4 6.1 %collective-permute-start = (bf16[64,1152]{1,0:T(8,128)(2,1)S(1)}, bf16[64,1152]{1,0:T(8,128)(2,1)S(1)}, u32[]{:S(2)}, u32[]{:S(2)}) collective-permute-start(bf16[64,1152]{1,0:T(8,128)(2,1)S(1)} %order.4), channel_id=1, source_target_pairs={{0,3},{1,2},{2,1},{3,0},{4,7},{5,6},{6,5},{7,4},{8,11},{9,10},{10,... | collective-permute-start | bytes 442376 | tf_op jit(solution)/shard_map/ppermute | solution.py:286
  57.9 8.9 %collective-permute-start.1 = (bf16[64,1152]{1,0:T(8,128)(2,1)S(1)}, bf16[64,1152]{1,0:T(8,128)(2,1)S(1)}, u32[]{:S(2)}, u32[]{:S(2)}) collective-permute-start(bf16[64,1152]{1,0:T(8,128)(2,1)S(1)} %order.5), channel_id=1, source_target_pairs={{0,2},{1,3},{2,0},{3,1},{4,6},{5,7},{6,4},{7,5},{8,10},{9,11},{10,... | collective-permute-start | bytes 442376 | tf_op jit(solution)/shard_map/ppermute | solution.py:286
  59.0 7.8 %collective-permute-start.2 = (bf16[64,1152]{1,0:T(8,128)(2,1)S(1)}, bf16[64,1152]{1,0:T(8,128)(2,1)S(1)}, u32[]{:S(2)}, u32[]{:S(2)}) collective-permute-start(bf16[64,1152]{1,0:T(8,128)(2,1)S(1)} %order.6), channel_id=1, source_target_pairs={{0,1},{1,0},{2,3},{3,2},{4,5},{5,4},{6,7},{7,6},{8,9},{9,8},{10,11... | collective-permute-start | bytes 442376 | tf_op jit(solution)/shard_map/ppermute | solution.py:286

commit v3 on v2

--- a/solution.py
+++ b/solution.py
@@ -7,6 +7,7 @@
 from jax.experimental import pallas as pl
 from jax.experimental.pallas import tpu as pltpu
 from jax.sharding import PartitionSpec as P
+
 
 BLOCK_ROWS = 128
 CYCLE_DEV = 2
@@ -62,7 +63,16 @@
     return lax.dot_general(a, b, (((ca,), (cb,)), ((), ())), preferred_element_type=F32)
 
 
-def pack_kernel(groups, me_ref, owner_ref, signal_ref, weight_ref, cycle_ref, phi_ref, psi_ref, out_ref, targets_ref):
+def pack_kernel(groups, me_ref, *refs):
+    sources, (out_ref, targets_ref), held, sems = refs[:6], refs[6:8], refs[8:14], refs[14]
+    copies = [
+        pltpu.make_async_copy(source, place, sems.at[number])
+        for number, (source, place) in enumerate(zip(sources, held))
+    ]
+    for copy in copies:
+        copy.start()
+    owner_ref, signal_ref, weight_ref, cycle_ref, phi_ref, psi_ref = held
+    copies[0].wait()
     for offset in range(targets_ref.shape[0]):
         targets_ref[offset] = me_ref[0] ^ offset
     blocks = owner_ref.shape[1]
@@ -82,6 +92,8 @@
         .astype(F32)
         .astype(BF16)
     )
+    for copy in copies[1:]:
+        copy.wait()
     value = (signal_ref[...] * weight_ref[...]).astype(BF16)
     phi = phi_ref[...]
     high = (psi_ref[...] * HIGH + phi // LOW).astype(F32).astype(BF16)
@@ -94,7 +106,9 @@
 
 
 def bin_kernel(share, step, targets_ref, recv_ref, first_ref, second_ref, wigner_ref, out_ref, *rest):
-    *held_refs, acc_ref, table_ref, sem, held_sem = rest
+    *held_refs, acc_ref, first_vmem, table_ref, first_sem, sem, held_sem = rest
+    first_copy = pltpu.make_async_copy(first_ref, first_vmem, first_sem)
+    first_copy.start()
     groups, _, padded, _ = recv_ref.shape
     width = out_ref.shape[-1]
     copy = pltpu.make_async_copy(second_ref, table_ref, sem)
@@ -135,7 +149,8 @@
         return carry
 
     lax.fori_loop(0, groups, one_source, 0)
-    first = first_ref[...]
+    first_copy.wait()
+    first = first_vmem[...]
     mixed = [dot(first, acc_ref[t].astype(BF16), 1, 0).astype(BF16) for t in range(CYCLE_DEV)]
     copy.wait()
     for parity in range(2):
@@ -183,7 +198,7 @@
     out_ref[...] = total.astype(BF16)
 
 
-def order_kernel(chunk, offset, where_ref, coeff_ref, wigner_ref, out_ref):
+def order_kernel(chunk, where_ref, coeff_ref, wigner_ref, out_ref):
     depth = coeff_ref.shape[1]
     step = pl.program_id(0)
     coeff = coeff_ref[...]
@@ -206,21 +221,36 @@
     depth = share * groups * CYCLE_DEV
 
     def square(data):
-        return data.reshape(blocks, BLOCK_ROWS)
+        return pltpu.with_memory_space_constraint(data.reshape(blocks, BLOCK_ROWS), pltpu.HBM)
 
     whole = pl.BlockSpec(memory_space=pltpu.VMEM)
+    scalars = pl.BlockSpec(memory_space=pltpu.SMEM)
+    anywhere = pl.BlockSpec(memory_space=pl.ANY)
     me = lax.axis_index("beam").astype(jnp.int32)
+    shape = (blocks, BLOCK_ROWS)
     sent, targets = pl.pallas_call(
         lambda *refs: pack_kernel(groups, *refs),
         out_shape=(
             jax.ShapeDtypeStruct((groups, 3, padded, BLOCK_ROWS), BF16),
             jax.ShapeDtypeStruct((beams,), jnp.int32),
         ),
-        in_specs=[pl.BlockSpec(memory_space=pltpu.SMEM)] + [whole] * 6,
-        out_specs=(whole, pl.BlockSpec(memory_space=pltpu.SMEM)),
+        in_specs=[scalars] + [anywhere] * 6,
+        out_specs=(whole, scalars),
+        scratch_shapes=[pltpu.VMEM((1, blocks), jnp.int32)]
+        + [pltpu.VMEM(shape, F32)] * 2
+        + [pltpu.VMEM(shape, jnp.int32)] * 3
+        + [pltpu.SemaphoreType.DMA((6,))],
         compiler_params=pltpu.CompilerParams(vmem_limit_bytes=6 << 20),
         name="pack",
-    )(me.reshape(1), owner.reshape(1, blocks), square(signal), square(weight), square(cycle), square(phi), square(psi))
+    )(
+        me.reshape(1),
+        pltpu.with_memory_space_constraint(owner.reshape(1, blocks), pltpu.HBM),
+        square(signal),
+        square(weight),
+        square(cycle),
+        square(phi),
+        square(psi),
+    )
     got = lax.all_to_all(sent, "blk", split_axis=0, concat_axis=0, tiled=True)
     tables, width = second_tables(groups)
     flat = wigner.reshape(orders * depth, ells)
@@ -230,23 +260,25 @@
             jax.ShapeDtypeStruct((groups, beams, 2, CYCLE_DEV, share, width), BF16),
         )
         + tuple(pltpu.VMEM((flat.shape[0] // beams, ells), BF16) for _ in range(beams)),
-        in_specs=[
-            pl.BlockSpec(memory_space=pltpu.SMEM),
-            whole,
-            whole,
-            pl.BlockSpec(memory_space=pltpu.HBM),
-            pl.BlockSpec(memory_space=pl.ANY),
-        ],
+        in_specs=[scalars, whole, anywhere, anywhere, anywhere],
         out_specs=(whole,) * (1 + beams),
         scratch_shapes=[
             pltpu.VMEM((CYCLE_DEV, LOW, LOW), F32),
+            pltpu.VMEM((LOW, LOW), BF16),
             pltpu.VMEM(tables.shape, BF16),
+            pltpu.SemaphoreType.DMA,
             pltpu.SemaphoreType.DMA,
             pltpu.SemaphoreType.DMA((beams,)),
         ],
         compiler_params=pltpu.CompilerParams(vmem_limit_bytes=2 * tables.size + (4 << 20)),
         name="bin",
-    )(targets, got, jnp.asarray(first_matrix(), BF16), pltpu.with_memory_space_constraint(jnp.asarray(tables, BF16), pltpu.HBM), flat)
+    )(
+        targets,
+        got,
+        pltpu.with_memory_space_constraint(jnp.asarray(first_matrix(), BF16), pltpu.HBM),
+        pltpu.with_memory_space_constraint(jnp.asarray(tables, BF16), pltpu.HBM),
+        flat,
+    )
     rows = 2 * CYCLE_DEV * share
     spectra = spectra.reshape(groups * beams, rows, width)
     parts = lax.all_to_all(spectra, ("blk", "beam"), split_axis=0, concat_axis=0, tiled=True)
@@ -264,7 +296,7 @@
 
     def piece(offset, kind):
         return pl.pallas_call(
-            lambda *refs: order_kernel(chunk, offset, *refs),
+            lambda *refs: order_kernel(chunk, *refs),
             out_shape=jax.ShapeDtypeStruct((2 * mine, ells), kind),
             grid_spec=pltpu.PrefetchScalarGridSpec(
                 num_scalar_prefetch=1,

time: 68.1 us -> 63.1 us (0.927)
  local copies, waits for them, and re-layouts: 6.63 us -> 0.88 us
  Pallas kernels: 24.2 us -> 25.1 us
    unnamed x14 -> x0, local copies, waits for them, and re-layouts: 5.75 us -> none
    pallas_call x1, Pallas kernels: 0.64 us -> 1.62 us  [shards(): pl.pallas_call(lambda *refs: pack_kernel(groups, *refs), out_shape=(jax.S...]
  transfers between devices with their start and end apart: 3 -> 3, of which waited for: 2 -> 2; matrix products, arithmetic and copies ran while one was open for 0% -> 0% of each run, Pallas kernels for 3% -> 4%
where the time goes in v3:
time: 63.1 us; the launch traced here: 62.9 us
  blocking collectives  29.7 us (47%)
  Pallas kernels  25.1 us (40%)
  waiting for transfers between devices  5.2 us (8%)
  starting transfers between devices  1.93 us (3%)
  local copies, waits for them, and re-layouts  0.88 us (1%)
    all_to_all x1, blocking collectives, shards(): got = lax.all_to_all(sent, 'blk', split_axis=0, concat_axis=0, tiled=True)  15.8 us
    pallas_call x1, Pallas kernels, shards(): pl.pallas_call(lambda *refs: bin_kernel(share, 8, *refs), out_shape=(jax....  14.1 us
    all_to_all x1, blocking collectives, shards(): lax.all_to_all(spectra, ('blk', 'beam'), split_axis=0, concat_axis=0, til...  13.9 us
    pallas_call x4, Pallas kernels, piece(): pl.pallas_call(lambda *refs: order_kernel(chunk, *refs), out_shape=jax.Sh...  9.01 us
    ppermute x3, waiting for transfers between devices, shards(): part = lax.ppermute(part, 'beam', [(i, i ^ offset) for i in range(beams)])  5.2 us
    ppermute x3, starting transfers between devices, shards(): part = lax.ppermute(part, 'beam', [(i, i ^ offset) for i in range(beams)])  1.93 us
    pallas_call x1, Pallas kernels, shards(): pl.pallas_call(lambda *refs: pack_kernel(groups, *refs), out_shape=(jax.S...  1.62 us
  transfers between devices with their start and end apart: 3, of which 2 were waited for; matrix products, arithmetic and copies ran while one was open for 0% of the time, Pallas kernels for 4%

profile of v3, /device:TPU:0, one launch (start us, length us, event | category | flops | bytes accessed | tf_op | source)
XLA Modules:
  0.0 62.9 jit_solution(14239172281414048949)
XLA Ops:
  0.0 1.6 %pack.1 = (bf16[8,3,40,128]{3,2,1,0:T(8,128)(2,1)S(1)}, s32[4]{0:T(128)S(1)}) custom-call(s32[1]{0:T(128)} %bitcast.refs_0_, s32[1,128]{1,0:T(1,128)} %bitcast.18, f32[128,128]{1,0:T(8,128)} %bitcast.13, f32[128,128]{1,0:T(8,128)} %bitcast.14, s32[128,128]{1,0:T(8,128)} %bitcast.15, s32[128,128]{1,0:T(8,128)} %bitcast.16, s32[128,128]{1,0:T(8,128)} %bitcast.17), custom_call_target="tpu_custom_call" | custom-call | tf_op jit(solution)/shard_map/pack/pallas_call | solution.py:231
  1.6 15.8 %all_to_all.10.refs_1_ = bf16[8,3,40,128]{3,2,1,0:T(8,128)(2,1)S(1)} all-to-all(bf16[8,3,40,128]{3,2,1,0:T(8,128)(2,1)S(1)} %get-tuple-element.13), channel_id=1, replica_groups=mesh['blk'=8,'beam'=4] {'blk'}, dimensions={0} | all-to-all | bytes 491520 | tf_op jit(solution)/shard_map/all_to_all | solution.py:254
  17.4 14.1 %bin.1 = (bf16[8,4,2,2,8,128]{5,4,3,2,1,0:T(8,128)(2,1)S(1)}, bf16[4096,1152]{1,0:T(8,128)(2,1)S(1)}, bf16[4096,1152]{1,0:T(8,128)(2,1)S(1)}, bf16[4096,1152]{1,0:T(8,128)(2,1)S(1)}, bf16[4096,1152]{1,0:T(8,128)(2,1)S(1)}) custom-call(s32[4]{0:T(128)S(1)} %get-tuple-element.12.refs_0_, bf16[8,3,40,128]{3,2,1,0:T(8,128)(2,1)S(1)} %all_to_all.10.refs_1_, ...), custom_call_target="tpu_custom_call" | custom-call | tf_op jit(solution)/shard_map/bin/pallas_call | solution.py:257
  31.6 13.9 %all_to_all.11 = bf16[32,32,128]{2,1,0:T(8,128)(2,1)S(1)} all-to-all(bf16[32,32,128]{2,1,0:T(8,128)(2,1)S(1)} %bitcast.11), channel_id=1, replica_groups=mesh['blk'=8,'beam'=4] {'blk','beam'}, dimensions={0} | all-to-all | bytes 524288 | tf_op jit(solution)/shard_map/all_to_all | solution.py:284
  45.4 0.4 coeff.1.refs_1_
  45.8 2.3 %order.6 = bf16[64,1152]{1,0:T(8,128)(2,1)S(1)} custom-call(s32[4]{0:T(128)S(1)} %get-tuple-element.12.refs_0_, bf16[256,128]{1,0:T(8,128)(2,1)S(1)} %coeff.1.refs_1_, bf16[4096,1152]{1,0:T(8,128)(2,1)S(1)} %get-tuple-element.17.refs_2_), custom_call_target="tpu_custom_call" | custom-call | tf_op jit(solution)/shard_map/order/pallas_call | solution.py:298
  48.1 2.3 %order.5 = bf16[64,1152]{1,0:T(8,128)(2,1)S(1)} custom-call(s32[4]{0:T(128)S(1)} %get-tuple-element.12.refs_0_, bf16[256,128]{1,0:T(8,128)(2,1)S(1)} %coeff.1.refs_1_, bf16[4096,1152]{1,0:T(8,128)(2,1)S(1)} %get-tuple-element.16.refs_2_), custom_call_target="tpu_custom_call" | custom-call | tf_op jit(solution)/shard_map/order/pallas_call | solution.py:298
  50.3 2.3 %order.4 = bf16[64,1152]{1,0:T(8,128)(2,1)S(1)} custom-call(s32[4]{0:T(128)S(1)} %get-tuple-element.12.refs_0_, bf16[256,128]{1,0:T(8,128)(2,1)S(1)} %coeff.1.refs_1_, bf16[4096,1152]{1,0:T(8,128)(2,1)S(1)} %get-tuple-element.15.refs_2_), custom_call_target="tpu_custom_call" | custom-call | tf_op jit(solution)/shard_map/order/pallas_call | solution.py:298
  52.6 0.5 collective-permute-start
  53.1 1.1 %collective-permute-start.1 = (bf16[64,1152]{1,0:T(8,128)(2,1)S(1)}, bf16[64,1152]{1,0:T(8,128)(2,1)S(1)}, u32[]{:S(2)}, u32[]{:S(2)}) collective-permute-start(bf16[64,1152]{1,0:T(8,128)(2,1)S(1)} %order.5), channel_id=1, source_target_pairs={{0,2},{1,3},{2,0},{3,1},{4,6},{5,7},{6,4},{7,5},{8,10},{9,11},{10,... | collective-permute-start | bytes 442376 | tf_op jit(solution)/shard_map/ppermute | solution.py:318
  54.2 0.3 collective-permute-start.2
  54.5 2.2 %order.7 = f32[64,1152]{1,0:T(8,128)S(1)} custom-call(s32[4]{0:T(128)S(1)} %get-tuple-element.12.refs_0_, bf16[256,128]{1,0:T(8,128)(2,1)S(1)} %coeff.1.refs_1_, bf16[4096,1152]{1,0:T(8,128)(2,1)S(1)} %get-tuple-element.18.refs_2_), custom_call_target="tpu_custom_call" | custom-call | tf_op jit(solution)/shard_map/order/pallas_call | solution.py:298
  56.8 1.9 %collective-permute-done = bf16[64,1152]{1,0:T(8,128)(2,1)S(1)} collective-permute-done((bf16[64,1152]{1,0:T(8,128)(2,1)S(1)}, bf16[64,1152]{1,0:T(8,128)(2,1)S(1)}, u32[]{:S(2)}, u32[]{:S(2)}) %collective-permute-start) | collective-permute-done | bytes 147488 | tf_op jit(solution)/shard_map/ppermute | solution.py:318
  58.7 3.3 %collective-permute-done.1 = bf16[64,1152]{1,0:T(8,128)(2,1)S(1)} collective-permute-done((bf16[64,1152]{1,0:T(8,128)(2,1)S(1)}, bf16[64,1152]{1,0:T(8,128)(2,1)S(1)}, u32[]{:S(2)}, u32[]{:S(2)}) %collective-permute-start.1) | collective-permute-done | bytes 147488 | tf_op jit(solution)/shard_map/ppermute | solution.py:318
  62.0 0.0 collective-permute-done.2
  62.0 0.1 add_add_fusion
  62.0 0.9 %reshape.43 = f32[32,2,1152]{2,1,0:T(2,128)} reshape(f32[64,1152]{1,0:T(8,128)S(1)} %add_add_fusion) | data formatting | bytes 589824 | tf_op jit(solution)/shard_map/reshape | solution.py:321
Async XLA Ops:
  52.6 6.1 %collective-permute-start = (bf16[64,1152]{1,0:T(8,128)(2,1)S(1)}, bf16[64,1152]{1,0:T(8,128)(2,1)S(1)}, u32[]{:S(2)}, u32[]{:S(2)}) collective-permute-start(bf16[64,1152]{1,0:T(8,128)(2,1)S(1)} %order.4), channel_id=1, source_target_pairs={{0,3},{1,2},{2,1},{3,0},{4,7},{5,6},{6,5},{7,4},{8,11},{9,10},{10,... | collective-permute-start | bytes 442376 | tf_op jit(solution)/shard_map/ppermute | solution.py:318
  53.1 8.9 %collective-permute-start.1 = (bf16[64,1152]{1,0:T(8,128)(2,1)S(1)}, bf16[64,1152]{1,0:T(8,128)(2,1)S(1)}, u32[]{:S(2)}, u32[]{:S(2)}) collective-permute-start(bf16[64,1152]{1,0:T(8,128)(2,1)S(1)} %order.5), channel_id=1, source_target_pairs={{0,2},{1,3},{2,0},{3,1},{4,6},{5,7},{6,4},{7,5},{8,10},{9,11},{10,... | collective-permute-start | bytes 442376 | tf_op jit(solution)/shard_map/ppermute | solution.py:318
  54.2 7.8 %collective-permute-start.2 = (bf16[64,1152]{1,0:T(8,128)(2,1)S(1)}, bf16[64,1152]{1,0:T(8,128)(2,1)S(1)}, u32[]{:S(2)}, u32[]{:S(2)}) collective-permute-start(bf16[64,1152]{1,0:T(8,128)(2,1)S(1)} %order.6), channel_id=1, source_target_pairs={{0,1},{1,0},{2,3},{3,2},{4,5},{5,4},{6,7},{7,6},{8,9},{9,8},{10,11... | collective-permute-start | bytes 442376 | tf_op jit(solution)/shard_map/ppermute | solution.py:318

commit v4 on v3

--- a/solution.py
+++ b/solution.py
@@ -105,8 +105,35 @@
             out_ref[group, number] = moved[group * padded : (group + 1) * padded]
 
 
-def bin_kernel(share, step, targets_ref, recv_ref, first_ref, second_ref, wigner_ref, out_ref, *rest):
-    *held_refs, acc_ref, first_vmem, table_ref, first_sem, sem, held_sem = rest
+def network(count):
+    size = 1
+    while size < count:
+        size *= 2
+    pairs = []
+    run = 1
+    while run < size:
+        gap = run
+        while gap >= 1:
+            for base in range(gap % run, size - gap, 2 * gap):
+                for i in range(base, min(base + gap, size - gap)):
+                    if i // (2 * run) == (i + gap) // (2 * run) and i + gap < count:
+                        pairs.append((i, i + gap))
+            gap //= 2
+        run *= 2
+    return pairs
+
+
+def sort_tiles(tiles, first, last):
+    for i, j in network(last - first):
+        i, j = i + first, j + first
+        (value0, high0, low0), (value1, high1, low1) = tiles[i], tiles[j]
+        swap = low0 < low1
+        tiles[i] = (jnp.where(swap, value1, value0), jnp.where(swap, high1, high0), jnp.maximum(low0, low1))
+        tiles[j] = (jnp.where(swap, value0, value1), jnp.where(swap, high0, high1), jnp.minimum(low0, low1))
+
+
+def bin_kernel(share, unit, targets_ref, recv_ref, first_ref, second_ref, wigner_ref, out_ref, *rest):
+    *held_refs, sorted_ref, acc_ref, first_vmem, table_ref, first_sem, sem, held_sem = rest
     first_copy = pltpu.make_async_copy(first_ref, first_vmem, first_sem)
     first_copy.start()
     groups, _, padded, _ = recv_ref.shape
@@ -126,29 +153,44 @@
     zero = jnp.zeros((LOW, LANES), BF16)
     one = jnp.ones((LOW, LANES), BF16)
 
-    def one_source(source, carry):
-        for start in range(0, padded, step):
-            value = recv_ref[source, 0, start : start + step, :]
-            high = recv_ref[source, 1, start : start + step, :]
-            low = recv_ref[source, 2, start : start + step, :]
-            parts = [[], [], []]
+    tiles = [
+        tuple(recv_ref[source, plane, start : start + 8, :].astype(F32) for plane in range(3))
+        for source in range(groups)
+        for start in range(0, padded, 8)
+    ]
+    count = len(tiles)
+    sort_tiles(tiles, 0, count)
+    start, stop = count // 5, count - count // 5
+    for number in range(start, stop):
+        tiles[number] = tuple(pltpu.roll(x, number * 29 % LANES, 1) for x in tiles[number])
+    sort_tiles(tiles, start, stop)
+    end0 = jnp.zeros((8, LANES), F32)
+    for number in range(count):
+        end0 = jnp.where(tiles[number][2] > 0, float(number + 1), end0)
+    begin1 = jnp.full((8, LANES), float(count), F32)
+    for number in range(count - 1, -1, -1):
+        begin1 = jnp.where(tiles[number][2] < 0, float(number), begin1)
+    for number in range(count):
+        for plane in range(3):
+            sorted_ref[plane, number] = tiles[number][plane].astype(BF16)
+
+    def one_unit(t, number, carry):
+        for step in range(unit):
+            value, high, low = (sorted_ref[plane, number * unit + step] for plane in range(3))
             blank = jnp.zeros_like(value)
-            value0 = jnp.where(low > 0, value, blank)
-            value1 = jnp.where(low > 0, blank, value)
+            value = jnp.where(low > 0, value, blank) if t == 0 else jnp.where(low > 0, blank, value)
             low = jnp.abs(low)
-            for row in range(step):
-                same = places_hi == high[row : row + 1, :]
-                parts[0].append(jnp.where(same, value0[row : row + 1, :], zero))
-                parts[1].append(jnp.where(same, value1[row : row + 1, :], zero))
-                parts[2].append(jnp.where(places_lo == low[row : row + 1, :], one, zero))
-            left0 = jnp.concatenate(parts[0], axis=1)
-            left1 = jnp.concatenate(parts[1], axis=1)
-            right = jnp.concatenate(parts[2], axis=1)
-            acc_ref[0] += dot(left0, right, 1, 1)
-            acc_ref[1] += dot(left1, right, 1, 1)
+            left, right = [], []
+            for row in range(8):
+                left.append(jnp.where(places_hi == high[row : row + 1, :], value[row : row + 1, :], zero))
+                right.append(jnp.where(places_lo == low[row : row + 1, :], one, zero))
+            acc_ref[t] += dot(jnp.concatenate(left, axis=1), jnp.concatenate(right, axis=1), 1, 1)
         return carry
 
-    lax.fori_loop(0, groups, one_source, 0)
+    end0 = lax.div(jnp.max(end0).astype(jnp.int32) + (unit - 1), unit)
+    begin1 = lax.div(jnp.min(begin1).astype(jnp.int32), unit)
+    lax.fori_loop(0, end0, lambda number, carry: one_unit(0, number, carry), 0)
+    lax.fori_loop(begin1, count // unit, lambda number, carry: one_unit(1, number, carry), 0)
     first_copy.wait()
     first = first_vmem[...]
     mixed = [dot(first, acc_ref[t].astype(BF16), 1, 0).astype(BF16) for t in range(CYCLE_DEV)]
@@ -198,15 +240,18 @@
     out_ref[...] = total.astype(BF16)
 
 
-def order_kernel(chunk, where_ref, coeff_ref, wigner_ref, out_ref):
+def order_kernel(chunk, offset, where_ref, coeff_ref, wigner_ref, out_ref):
     depth = coeff_ref.shape[1]
-    step = pl.program_id(0)
-    coeff = coeff_ref[...]
-    wide = jnp.concatenate([coeff] * chunk, axis=1)
-    row = lax.broadcasted_iota(jnp.int32, wide.shape, 0) // 2
-    column = lax.broadcasted_iota(jnp.int32, wide.shape, 1) // depth
-    wide = jnp.where(row == column, wide.astype(F32), 0.0).astype(BF16)
-    out_ref[...] = dot(wide, wigner_ref[pl.ds(step * chunk * depth, chunk * depth), :], 1, 0).astype(out_ref.dtype)
+    rows = out_ref.shape[0]
+    base = where_ref[offset] * rows
+    shape = (2 * chunk, chunk * depth)
+    own = lax.broadcasted_iota(jnp.int32, shape, 0) // 2 == lax.broadcasted_iota(jnp.int32, shape, 1) // depth
+    for number in range(rows // (2 * chunk)):
+        start = pl.multiple_of(base + number * 2 * chunk, 2 * chunk)
+        coeff = coeff_ref[pl.ds(start, 2 * chunk), :].astype(F32)
+        wide = jnp.where(own, jnp.concatenate([coeff] * chunk, axis=1), 0.0).astype(BF16)
+        part = dot(wide, wigner_ref[number * chunk * depth : (number + 1) * chunk * depth, :], 1, 0)
+        out_ref[number * 2 * chunk : (number + 1) * 2 * chunk, :] = part.astype(out_ref.dtype)
 
 
 def shards(signal, weight, cycle, phi, psi, owner, wigner):
@@ -253,9 +298,11 @@
     )
     got = lax.all_to_all(sent, "blk", split_axis=0, concat_axis=0, tiled=True)
     tables, width = second_tables(groups)
+    tiles = groups * padded // 8
+    unit = next(size for size in (5, 4, 2, 1) if tiles % size == 0)
     flat = wigner.reshape(orders * depth, ells)
     spectra, *held = pl.pallas_call(
-        lambda *refs: bin_kernel(share, 8, *refs),
+        lambda *refs: bin_kernel(share, unit, *refs),
         out_shape=(
             jax.ShapeDtypeStruct((groups, beams, 2, CYCLE_DEV, share, width), BF16),
         )
@@ -263,6 +310,7 @@
         in_specs=[scalars, whole, anywhere, anywhere, anywhere],
         out_specs=(whole,) * (1 + beams),
         scratch_shapes=[
+            pltpu.VMEM((3, tiles, 8, LANES), BF16),
             pltpu.VMEM((CYCLE_DEV, LOW, LOW), F32),
             pltpu.VMEM((LOW, LOW), BF16),
             pltpu.VMEM(tables.shape, BF16),
@@ -292,21 +340,13 @@
 
     mine = orders // beams
     chunk = 8
-    steps = mine // chunk
 
     def piece(offset, kind):
         return pl.pallas_call(
-            lambda *refs: order_kernel(chunk, *refs),
+            lambda *refs: order_kernel(chunk, offset, *refs),
             out_shape=jax.ShapeDtypeStruct((2 * mine, ells), kind),
-            grid_spec=pltpu.PrefetchScalarGridSpec(
-                num_scalar_prefetch=1,
-                grid=(steps,),
-                in_specs=[
-                    pl.BlockSpec((2 * chunk, depth), lambda i, at: (at[offset] * steps + i, 0)),
-                    pl.BlockSpec(memory_space=pltpu.VMEM),
-                ],
-                out_specs=pl.BlockSpec((2 * chunk, ells), lambda i, at: (i, 0)),
-            ),
+            in_specs=[scalars, whole, whole],
+            out_specs=whole,
             compiler_params=pltpu.CompilerParams(vmem_limit_bytes=6 << 20),
             name="order",
         )(targets, coeff, pltpu.with_memory_space_constraint(held[offset], pltpu.VMEM))

time: 63.1 us -> 62 us (0.983)
  Pallas kernels: 25.1 us -> 23.7 us
    pallas_call x5, Pallas kernels: 23.1 us -> 21.7 us  [the longest x1 14.1 us: shards(): pl.pallas_call(lambda *refs: bin_kernel(share, unit, *refs), out_shape=(j...]
  transfers between devices with their start and end apart: 3 -> 3, of which waited for: 2 -> 2; matrix products, arithmetic and copies ran while one was open for 0% -> 0% of each run, Pallas kernels for 4% -> 3%
where the time goes in v4:
time: 62 us; the launch traced here: 61.8 us
  blocking collectives  29.7 us (48%)
  Pallas kernels  23.7 us (38%)
  waiting for transfers between devices  5.58 us (9%)
  starting transfers between devices  1.92 us (3%)
  local copies, waits for them, and re-layouts  0.88 us (1%)
    all_to_all x1, blocking collectives, shards(): got = lax.all_to_all(sent, 'blk', split_axis=0, concat_axis=0, tiled=True)  15.8 us
    pallas_call x1, Pallas kernels, shards(): pl.pallas_call(lambda *refs: bin_kernel(share, unit, *refs), out_shape=(j...  14.1 us
    all_to_all x1, blocking collectives, shards(): lax.all_to_all(spectra, ('blk', 'beam'), split_axis=0, concat_axis=0, til...  13.9 us
    pallas_call x4, Pallas kernels, piece(): pl.pallas_call(lambda *refs: order_kernel(chunk, offset, *refs), out_shap...  7.5 us
    ppermute x3, waiting for transfers between devices, shards(): part = lax.ppermute(part, 'beam', [(i, i ^ offset) for i in range(beams)])  5.58 us
    ppermute x3, starting transfers between devices, shards(): part = lax.ppermute(part, 'beam', [(i, i ^ offset) for i in range(beams)])  1.92 us
    pallas_call x1, Pallas kernels, shards(): pl.pallas_call(lambda *refs: pack_kernel(groups, *refs), out_shape=(jax.S...  1.62 us
  transfers between devices with their start and end apart: 3, of which 2 were waited for; matrix products, arithmetic and copies ran while one was open for 0% of the time, Pallas kernels for 3%

profile of v4, /device:TPU:0, one launch (start us, length us, event | category | flops | bytes accessed | tf_op | source)
XLA Modules:
  0.0 61.8 jit_solution(7331494608265439114)
XLA Ops:
  0.0 1.6 %pack.1 = (bf16[8,3,40,128]{3,2,1,0:T(8,128)(2,1)S(1)}, s32[4]{0:T(128)S(1)}) custom-call(s32[1]{0:T(128)} %bitcast.refs_0_, s32[1,128]{1,0:T(1,128)} %bitcast.18, f32[128,128]{1,0:T(8,128)} %bitcast.13, f32[128,128]{1,0:T(8,128)} %bitcast.14, s32[128,128]{1,0:T(8,128)} %bitcast.15, s32[128,128]{1,0:T(8,128)} %bitcast.16, s32[128,128]{1,0:T(8,128)} %bitcast.17), custom_call_target="tpu_custom_call" | custom-call | tf_op jit(solution)/shard_map/pack/pallas_call | solution.py:276
  1.6 15.8 %all_to_all.10.refs_1_ = bf16[8,3,40,128]{3,2,1,0:T(8,128)(2,1)S(1)} all-to-all(bf16[8,3,40,128]{3,2,1,0:T(8,128)(2,1)S(1)} %get-tuple-element.13), channel_id=1, replica_groups=mesh['blk'=8,'beam'=4] {'blk'}, dimensions={0} | all-to-all | bytes 491520 | tf_op jit(solution)/shard_map/all_to_all | solution.py:299
  17.4 14.1 %bin.1 = (bf16[8,4,2,2,8,128]{5,4,3,2,1,0:T(8,128)(2,1)S(1)}, bf16[4096,1152]{1,0:T(8,128)(2,1)S(1)}, bf16[4096,1152]{1,0:T(8,128)(2,1)S(1)}, bf16[4096,1152]{1,0:T(8,128)(2,1)S(1)}, bf16[4096,1152]{1,0:T(8,128)(2,1)S(1)}) custom-call(s32[4]{0:T(128)S(1)} %get-tuple-element.12.refs_0_, bf16[8,3,40,128]{3,2,1,0:T(8,128)(2,1)S(1)} %all_to_all.10.refs_1_, ...), custom_call_target="tpu_custom_call" | custom-call | tf_op jit(solution)/shard_map/bin/pallas_call | solution.py:304
  31.6 13.9 %all_to_all.11 = bf16[32,32,128]{2,1,0:T(8,128)(2,1)S(1)} all-to-all(bf16[32,32,128]{2,1,0:T(8,128)(2,1)S(1)} %bitcast.11), channel_id=1, replica_groups=mesh['blk'=8,'beam'=4] {'blk','beam'}, dimensions={0} | all-to-all | bytes 524288 | tf_op jit(solution)/shard_map/all_to_all | solution.py:332
  45.4 0.4 coeff.1.refs_1_
  45.8 1.9 %order.6 = bf16[64,1152]{1,0:T(8,128)(2,1)S(1)} custom-call(s32[4]{0:T(128)S(1)} %get-tuple-element.12.refs_0_, bf16[256,128]{1,0:T(8,128)(2,1)S(1)} %coeff.1.refs_1_, bf16[4096,1152]{1,0:T(8,128)(2,1)S(1)} %get-tuple-element.17.refs_2_), custom_call_target="tpu_custom_call" | custom-call | tf_op jit(solution)/shard_map/order/pallas_call | solution.py:345
  47.7 1.9 %order.5 = bf16[64,1152]{1,0:T(8,128)(2,1)S(1)} custom-call(s32[4]{0:T(128)S(1)} %get-tuple-element.12.refs_0_, bf16[256,128]{1,0:T(8,128)(2,1)S(1)} %coeff.1.refs_1_, bf16[4096,1152]{1,0:T(8,128)(2,1)S(1)} %get-tuple-element.16.refs_2_), custom_call_target="tpu_custom_call" | custom-call | tf_op jit(solution)/shard_map/order/pallas_call | solution.py:345
  49.6 1.9 %order.4 = bf16[64,1152]{1,0:T(8,128)(2,1)S(1)} custom-call(s32[4]{0:T(128)S(1)} %get-tuple-element.12.refs_0_, bf16[256,128]{1,0:T(8,128)(2,1)S(1)} %coeff.1.refs_1_, bf16[4096,1152]{1,0:T(8,128)(2,1)S(1)} %get-tuple-element.15.refs_2_), custom_call_target="tpu_custom_call" | custom-call | tf_op jit(solution)/shard_map/order/pallas_call | solution.py:345
  51.5 0.5 collective-permute-start
  52.0 1.1 %collective-permute-start.1 = (bf16[64,1152]{1,0:T(8,128)(2,1)S(1)}, bf16[64,1152]{1,0:T(8,128)(2,1)S(1)}, u32[]{:S(2)}, u32[]{:S(2)}) collective-permute-start(bf16[64,1152]{1,0:T(8,128)(2,1)S(1)} %order.5), channel_id=1, source_target_pairs={{0,2},{1,3},{2,0},{3,1},{4,6},{5,7},{6,4},{7,5},{8,10},{9,11},{10,... | collective-permute-start | bytes 442376 | tf_op jit(solution)/shard_map/ppermute | solution.py:358
  53.1 0.3 collective-permute-start.2
  53.4 1.9 %order.7 = f32[64,1152]{1,0:T(8,128)S(1)} custom-call(s32[4]{0:T(128)S(1)} %get-tuple-element.12.refs_0_, bf16[256,128]{1,0:T(8,128)(2,1)S(1)} %coeff.1.refs_1_, bf16[4096,1152]{1,0:T(8,128)(2,1)S(1)} %get-tuple-element.18.refs_2_), custom_call_target="tpu_custom_call" | custom-call | tf_op jit(solution)/shard_map/order/pallas_call | solution.py:345
  55.3 2.3 %collective-permute-done = bf16[64,1152]{1,0:T(8,128)(2,1)S(1)} collective-permute-done((bf16[64,1152]{1,0:T(8,128)(2,1)S(1)}, bf16[64,1152]{1,0:T(8,128)(2,1)S(1)}, u32[]{:S(2)}, u32[]{:S(2)}) %collective-permute-start) | collective-permute-done | bytes 147488 | tf_op jit(solution)/shard_map/ppermute | solution.py:358
  57.6 3.3 %collective-permute-done.1 = bf16[64,1152]{1,0:T(8,128)(2,1)S(1)} collective-permute-done((bf16[64,1152]{1,0:T(8,128)(2,1)S(1)}, bf16[64,1152]{1,0:T(8,128)(2,1)S(1)}, u32[]{:S(2)}, u32[]{:S(2)}) %collective-permute-start.1) | collective-permute-done | bytes 147488 | tf_op jit(solution)/shard_map/ppermute | solution.py:358
  60.8 0.0 collective-permute-done.2
  60.8 0.1 add_add_fusion
  60.9 0.9 %reshape.43 = f32[32,2,1152]{2,1,0:T(2,128)} reshape(f32[64,1152]{1,0:T(8,128)S(1)} %add_add_fusion) | data formatting | bytes 589824 | tf_op jit(solution)/shard_map/reshape | solution.py:361
Async XLA Ops:
  51.5 6.1 %collective-permute-start = (bf16[64,1152]{1,0:T(8,128)(2,1)S(1)}, bf16[64,1152]{1,0:T(8,128)(2,1)S(1)}, u32[]{:S(2)}, u32[]{:S(2)}) collective-permute-start(bf16[64,1152]{1,0:T(8,128)(2,1)S(1)} %order.4), channel_id=1, source_target_pairs={{0,3},{1,2},{2,1},{3,0},{4,7},{5,6},{6,5},{7,4},{8,11},{9,10},{10,... | collective-permute-start | bytes 442376 | tf_op jit(solution)/shard_map/ppermute | solution.py:358
  52.0 8.9 %collective-permute-start.1 = (bf16[64,1152]{1,0:T(8,128)(2,1)S(1)}, bf16[64,1152]{1,0:T(8,128)(2,1)S(1)}, u32[]{:S(2)}, u32[]{:S(2)}) collective-permute-start(bf16[64,1152]{1,0:T(8,128)(2,1)S(1)} %order.5), channel_id=1, source_target_pairs={{0,2},{1,3},{2,0},{3,1},{4,6},{5,7},{6,4},{7,5},{8,10},{9,11},{10,... | collective-permute-start | bytes 442376 | tf_op jit(solution)/shard_map/ppermute | solution.py:358
  53.1 7.8 %collective-permute-start.2 = (bf16[64,1152]{1,0:T(8,128)(2,1)S(1)}, bf16[64,1152]{1,0:T(8,128)(2,1)S(1)}, u32[]{:S(2)}, u32[]{:S(2)}) collective-permute-start(bf16[64,1152]{1,0:T(8,128)(2,1)S(1)} %order.6), channel_id=1, source_target_pairs={{0,1},{1,0},{2,3},{3,2},{4,5},{5,4},{6,7},{7,6},{8,9},{9,8},{10,11... | collective-permute-start | bytes 442376 | tf_op jit(solution)/shard_map/ppermute | solution.py:358

commit v5 on v4

--- a/solution.py
+++ b/solution.py
@@ -142,9 +142,9 @@
     copy.start()
     held = []
     size = held_refs[0].shape[0]
-    for offset, held_ref in enumerate(held_refs):
-        source = wigner_ref.at[pl.ds(targets_ref[offset] * size, size), :]
-        held.append(pltpu.make_async_copy(source, held_ref, held_sem.at[offset]))
+    for number, held_ref in enumerate(held_refs):
+        source = wigner_ref.at[pl.ds(targets_ref[number + 1] * size, size), :]
+        held.append(pltpu.make_async_copy(source, held_ref, held_sem.at[number]))
         held[-1].start()
     acc_ref[...] = jnp.zeros_like(acc_ref)
     places = lax.broadcasted_iota(jnp.int32, (LOW, LANES), 0).astype(F32)
@@ -240,18 +240,35 @@
     out_ref[...] = total.astype(BF16)
 
 
-def order_kernel(chunk, offset, where_ref, coeff_ref, wigner_ref, out_ref):
+def order_kernel(chunk, offset, fetch, tables, where_ref, coeff_ref, *refs):
     depth = coeff_ref.shape[1]
+    size = chunk * depth
+    wigner_refs, refs = refs[:tables], refs[tables:]
+    copies = []
+    if fetch:
+        source_ref, out_ref, *held_refs, sem = refs
+        for number, held_ref in zip(fetch, held_refs):
+            first = where_ref[0] * (out_ref.shape[0] * depth // 2) + number * size
+            source = source_ref.at[pl.ds(first, size), :]
+            copies.append(pltpu.make_async_copy(source, held_ref, sem.at[len(copies)]))
+            copies[-1].start()
+    else:
+        (out_ref,) = refs
     rows = out_ref.shape[0]
     base = where_ref[offset] * rows
-    shape = (2 * chunk, chunk * depth)
+    shape = (2 * chunk, size)
     own = lax.broadcasted_iota(jnp.int32, shape, 0) // 2 == lax.broadcasted_iota(jnp.int32, shape, 1) // depth
-    for number in range(rows // (2 * chunk)):
-        start = pl.multiple_of(base + number * 2 * chunk, 2 * chunk)
-        coeff = coeff_ref[pl.ds(start, 2 * chunk), :].astype(F32)
-        wide = jnp.where(own, jnp.concatenate([coeff] * chunk, axis=1), 0.0).astype(BF16)
-        part = dot(wide, wigner_ref[number * chunk * depth : (number + 1) * chunk * depth, :], 1, 0)
-        out_ref[number * 2 * chunk : (number + 1) * 2 * chunk, :] = part.astype(out_ref.dtype)
+    number = 0
+    for wigner_ref in wigner_refs:
+        for first in range(0, wigner_ref.shape[0], size):
+            start = pl.multiple_of(base + number * 2 * chunk, 2 * chunk)
+            coeff = coeff_ref[pl.ds(start, 2 * chunk), :].astype(F32)
+            wide = jnp.where(own, jnp.concatenate([coeff] * chunk, axis=1), 0.0).astype(BF16)
+            part = dot(wide, wigner_ref[first : first + size, :], 1, 0)
+            out_ref[number * 2 * chunk : (number + 1) * 2 * chunk, :] = part.astype(out_ref.dtype)
+            number += 1
+    for copy in copies:
+        copy.wait()
 
 
 def shards(signal, weight, cycle, phi, psi, owner, wigner):
@@ -306,9 +323,9 @@
         out_shape=(
             jax.ShapeDtypeStruct((groups, beams, 2, CYCLE_DEV, share, width), BF16),
         )
-        + tuple(pltpu.VMEM((flat.shape[0] // beams, ells), BF16) for _ in range(beams)),
+        + tuple(pltpu.VMEM((flat.shape[0] // beams, ells), BF16) for _ in range(beams - 1)),
         in_specs=[scalars, whole, anywhere, anywhere, anywhere],
-        out_specs=(whole,) * (1 + beams),
+        out_specs=(whole,) * beams,
         scratch_shapes=[
             pltpu.VMEM((3, tiles, 8, LANES), BF16),
             pltpu.VMEM((CYCLE_DEV, LOW, LOW), F32),
@@ -316,7 +333,7 @@
             pltpu.VMEM(tables.shape, BF16),
             pltpu.SemaphoreType.DMA,
             pltpu.SemaphoreType.DMA,
-            pltpu.SemaphoreType.DMA((beams,)),
+            pltpu.SemaphoreType.DMA((beams - 1,)),
         ],
         compiler_params=pltpu.CompilerParams(vmem_limit_bytes=2 * tables.size + (4 << 20)),
         name="bin",
@@ -340,24 +357,46 @@
 
     mine = orders // beams
     chunk = 8
-
-    def piece(offset, kind):
-        return pl.pallas_call(
-            lambda *refs: order_kernel(chunk, offset, *refs),
-            out_shape=jax.ShapeDtypeStruct((2 * mine, ells), kind),
-            in_specs=[scalars, whole, whole],
-            out_specs=whole,
+    parts = mine // chunk
+    last = {}
+
+    def piece(offset, fetch, kind):
+        tables = [held[offset - 1]] if offset else [last[number] for number in range(parts)]
+        tables = [pltpu.with_memory_space_constraint(table, pltpu.VMEM) for table in tables]
+        source = [pltpu.with_memory_space_constraint(flat, pltpu.HBM)] if fetch else []
+        part, *fetched = pl.pallas_call(
+            lambda *refs: order_kernel(chunk, offset, fetch, len(tables), *refs),
+            out_shape=(jax.ShapeDtypeStruct((2 * mine, ells), kind),)
+            + tuple(pltpu.VMEM((chunk * depth, ells), BF16) for _ in fetch),
+            in_specs=[scalars] + [whole] * (1 + len(tables)) + [anywhere] * len(source),
+            out_specs=(whole,) * (1 + len(fetch)),
+            scratch_shapes=[pltpu.SemaphoreType.DMA((len(fetch),))] if fetch else [],
             compiler_params=pltpu.CompilerParams(vmem_limit_bytes=6 << 20),
             name="order",
-        )(targets, coeff, pltpu.with_memory_space_constraint(held[offset], pltpu.VMEM))
-
-    total = None
-    for offset in range(beams - 1, -1, -1):
-        part = piece(offset, BF16 if offset else F32)
-        if offset:
-            part = lax.ppermute(part, "beam", [(i, i ^ offset) for i in range(beams)])
-        part = part.astype(F32)
-        total = part if total is None else total + part
+        )(targets, coeff, *tables, *source)
+        last.update(zip(fetch, fetched))
+        return part
+
+    def send(part, distance):
+        return lax.ppermute(part, "beam", [(i, i ^ distance) for i in range(beams)])
+
+    sequence = [offset for chip in range(beams // 2 - 1, -1, -1) for offset in (2 * chip + 1, 2 * chip)]
+    shares_of = {offset: [] for offset in sequence}
+    for number in range(parts):
+        shares_of[sequence[number % (beams - 1)]].append(number)
+    terms = []
+    near = None
+    for offset in sequence:
+        fetch = sorted(shares_of[offset])
+        part = piece(offset, fetch, BF16 if offset % 2 else F32)
+        if offset % 2:
+            near = send(part, 1)
+        else:
+            part = part + near.astype(F32)
+            terms.append(send(part.astype(BF16), offset).astype(F32) if offset else part)
+    total = terms[-1]
+    for term in terms[:-1]:
+        total = total + term
     return total.reshape(mine, 2, ells)
 
 

time: 62 us -> 60.6 us (0.977)
  waiting for transfers between devices: 5.58 us -> 3.57 us
  Pallas kernels: 23.7 us -> 25.1 us
  starting transfers between devices: 1.92 us -> 1.03 us
    pallas_call x4, Pallas kernels: 7.5 us -> 11.6 us  [piece(): pl.pallas_call(lambda *refs: order_kernel(chunk, offset, fetch, len(table...]
    pallas_call x1, Pallas kernels: 14.1 us -> 11.5 us  [shards(): pl.pallas_call(lambda *refs: bin_kernel(share, unit, *refs), out_shape=(j...]
    ppermute x3, waiting for transfers between devices: 5.58 us -> 3.57 us  [send(): return lax.ppermute(part, 'beam', [(i, i ^ distance) for i in range(beams)])]
    ppermute x3, starting transfers between devices: 1.92 us -> 1.03 us  [send(): return lax.ppermute(part, 'beam', [(i, i ^ distance) for i in range(beams)])]
  transfers between devices with their start and end apart: 3 -> 3, of which waited for: 2 -> 1; matrix products, arithmetic and copies ran while one was open for 0% -> 0% of each run, Pallas kernels for 3% -> 12%
where the time goes in v5:
time: 60.6 us; the launch traced here: 60.3 us
  blocking collectives  29.6 us (49%)
  Pallas kernels  25.1 us (41%)
  waiting for transfers between devices  3.57 us (6%)
  starting transfers between devices  1.03 us (2%)
  local copies, waits for them, and re-layouts  0.88 us (1%)
    all_to_all x1, blocking collectives, shards(): got = lax.all_to_all(sent, 'blk', split_axis=0, concat_axis=0, tiled=True)  15.8 us
    all_to_all x1, blocking collectives, shards(): lax.all_to_all(spectra, ('blk', 'beam'), split_axis=0, concat_axis=0, til...  13.8 us
    pallas_call x4, Pallas kernels, piece(): pl.pallas_call(lambda *refs: order_kernel(chunk, offset, fetch, len(table...  11.6 us
    pallas_call x1, Pallas kernels, shards(): pl.pallas_call(lambda *refs: bin_kernel(share, unit, *refs), out_shape=(j...  11.5 us
    ppermute x3, waiting for transfers between devices, send(): return lax.ppermute(part, 'beam', [(i, i ^ distance) for i in range(beams)])  3.57 us
    pallas_call x1, Pallas kernels, shards(): pl.pallas_call(lambda *refs: pack_kernel(groups, *refs), out_shape=(jax.S...  1.62 us
  transfers between devices with their start and end apart: 3, of which 1 were waited for; matrix products, arithmetic and copies ran while one was open for 0% of the time, Pallas kernels for 12%

profile of v5, /device:TPU:0, one launch (start us, length us, event | category | flops | bytes accessed | tf_op | source)
XLA Modules:
  0.0 60.3 jit_solution(17643354192683522090)
XLA Ops:
  0.0 1.6 %pack.1 = (bf16[8,3,40,128]{3,2,1,0:T(8,128)(2,1)S(1)}, s32[4]{0:T(128)S(1)}) custom-call(s32[1]{0:T(128)} %bitcast.refs_0_, s32[1,128]{1,0:T(1,128)} %bitcast.21, f32[128,128]{1,0:T(8,128)} %bitcast.16, f32[128,128]{1,0:T(8,128)} %bitcast.17, s32[128,128]{1,0:T(8,128)} %bitcast.18, s32[128,128]{1,0:T(8,128)} %bitcast.19, s32[128,128]{1,0:T(8,128)} %bitcast.20), custom_call_target="tpu_custom_call" | custom-call | tf_op jit(solution)/shard_map/pack/pallas_call | solution.py:293
  1.6 15.8 %all_to_all.10.refs_1_ = bf16[8,3,40,128]{3,2,1,0:T(8,128)(2,1)S(1)} all-to-all(bf16[8,3,40,128]{3,2,1,0:T(8,128)(2,1)S(1)} %get-tuple-element.19), channel_id=1, replica_groups=mesh['blk'=8,'beam'=4] {'blk'}, dimensions={0} | all-to-all | bytes 491520 | tf_op jit(solution)/shard_map/all_to_all | solution.py:316
  17.4 11.5 %bin.1 = (bf16[8,4,2,2,8,128]{5,4,3,2,1,0:T(8,128)(2,1)S(1)}, bf16[4096,1152]{1,0:T(8,128)(2,1)S(1)}, bf16[4096,1152]{1,0:T(8,128)(2,1)S(1)}, bf16[4096,1152]{1,0:T(8,128)(2,1)S(1)}) custom-call(s32[4]{0:T(128)S(1)} %get-tuple-element.18.refs_0_, bf16[8,3,40,128]{3,2,1,0:T(8,128)(2,1)S(1)} %all_to_all.10.refs_1_, bf16[256,256]{1,0:T(8,128)(2,1)} %constant.8.clone.refs_2_, ...), custom_call_target="tpu_custom_call" | custom-call | tf_op jit(solution)/shard_map/bin/pallas_call | solution.py:321
  28.9 13.8 %all_to_all.11 = bf16[32,32,128]{2,1,0:T(8,128)(2,1)S(1)} all-to-all(bf16[32,32,128]{2,1,0:T(8,128)(2,1)S(1)} %bitcast.11), channel_id=1, replica_groups=mesh['blk'=8,'beam'=4] {'blk','beam'}, dimensions={0} | all-to-all | bytes 524288 | tf_op jit(solution)/shard_map/all_to_all | solution.py:349
  42.7 0.4 coeff.1.refs_1_
  43.1 4.1 %order.4 = (bf16[64,1152]{1,0:T(8,128)(2,1)S(1)}, bf16[1024,1152]{1,0:T(8,128)(2,1)S(1)}, bf16[1024,1152]{1,0:T(8,128)(2,1)S(1)}) custom-call(s32[4]{0:T(128)S(1)} %get-tuple-element.18.refs_0_, bf16[256,128]{1,0:T(8,128)(2,1)S(1)} %coeff.1.refs_1_, bf16[4096,1152]{1,0:T(8,128)(2,1)S(1)} %get-tuple-element.21.refs_2_, bf16[16384,1152]{1,0:T(8,128)(2,1)} %bitcast.13), custom_call_target="tpu_custom_call" | custom-call | tf_op jit(solution)/shard_map/order/pallas_call | solution.py:367
  47.3 0.1 collective-permute-start.1
  47.4 3.1 %order.6 = (bf16[64,1152]{1,0:T(8,128)(2,1)S(1)}, bf16[1024,1152]{1,0:T(8,128)(2,1)S(1)}) custom-call(s32[4]{0:T(128)S(1)} %get-tuple-element.18.refs_0_, bf16[256,128]{1,0:T(8,128)(2,1)S(1)} %coeff.1.refs_1_, bf16[4096,1152]{1,0:T(8,128)(2,1)S(1)} %get-tuple-element.25.refs_2_, bf16[16384,1152]{1,0:T(8,128)(2,1)} %bitcast.14), custom_call_target="tpu_custom_call" | custom-call | tf_op jit(solution)/shard_map/order/pallas_call | solution.py:367
  50.5 2.5 %order.5 = (f32[64,1152]{1,0:T(8,128)S(1)}, bf16[1024,1152]{1,0:T(8,128)(2,1)S(1)}) custom-call(s32[4]{0:T(128)S(1)} %get-tuple-element.18.refs_0_, bf16[256,128]{1,0:T(8,128)(2,1)S(1)} %coeff.1.refs_1_, bf16[4096,1152]{1,0:T(8,128)(2,1)S(1)} %get-tuple-element.23.refs_2_, bf16[16384,1152]{1,0:T(8,128)(2,1)} %bitcast.15), custom_call_target="tpu_custom_call" | custom-call | tf_op jit(solution)/shard_map/order/pallas_call | solution.py:367
  53.0 0.6 collective-permute-start
  53.5 0.0 collective-permute-done.1
  53.6 0.4 collective-permute-start.2
  54.0 1.9 %order.7 = f32[64,1152]{1,0:T(8,128)S(1)} custom-call(s32[4]{0:T(128)S(1)} %get-tuple-element.18.refs_0_, bf16[256,128]{1,0:T(8,128)(2,1)S(1)} %coeff.1.refs_1_, bf16[1024,1152]{1,0:T(8,128)(2,1)S(1)} %get-tuple-element.22.refs_2_, bf16[1024,1152]{1,0:T(8,128)(2,1)S(1)} %get-tuple-element.24.refs_3_, bf16[1024,1152]{1,0:T(8,128)(2,1)S(1)} %get-tuple-element.26.refs_4_, ...), custom_call_target="tpu_custom_call" | custom-call | tf_op jit(solution)/shard_map/order/pallas_call | solution.py:367
  55.8 0.0 collective-permute-done
  55.8 3.6 %collective-permute-done.2 = bf16[64,1152]{1,0:T(8,128)(2,1)S(1)} collective-permute-done((bf16[64,1152]{1,0:T(8,128)(2,1)S(1)}, bf16[64,1152]{1,0:T(8,128)(2,1)S(1)}, u32[]{:S(2)}, u32[]{:S(2)}) %collective-permute-start.2) | collective-permute-done | bytes 147488 | tf_op jit(solution)/shard_map/ppermute | solution.py:381
  59.5 0.9 %reshape.43 = f32[32,2,1152]{2,1,0:T(2,128)} reshape(f32[64,1152]{1,0:T(8,128)S(1)} %convert_add_fusion) | data formatting | bytes 589824 | tf_op jit(solution)/shard_map/reshape | solution.py:400
  (2 shorter events, 0.1 us)
Async XLA Ops:
  47.3 6.3 %collective-permute-start.1 = (bf16[64,1152]{1,0:T(8,128)(2,1)S(1)}, bf16[64,1152]{1,0:T(8,128)(2,1)S(1)}, u32[]{:S(2)}, u32[]{:S(2)}) collective-permute-start(bf16[64,1152]{1,0:T(8,128)(2,1)S(1)} %get-tuple-element.30), channel_id=1, source_target_pairs={{0,1},{1,0},{2,3},{3,2},{4,5},{5,4},{6,7},{7,6},{8,9},{9,8},{10,11... | collective-permute-start | bytes 442376 | tf_op jit(solution)/shard_map/ppermute | solution.py:381
  53.0 2.9 %collective-permute-start = (bf16[64,1152]{1,0:T(8,128)(2,1)S(1)}, bf16[64,1152]{1,0:T(8,128)(2,1)S(1)}, u32[]{:S(2)}, u32[]{:S(2)}) collective-permute-start(bf16[64,1152]{1,0:T(8,128)(2,1)S(1)} %get-tuple-element.28), channel_id=1, source_target_pairs={{0,1},{1,0},{2,3},{3,2},{4,5},{5,4},{6,7},{7,6},{8,9},{9,8},{10,11... | collective-permute-start | bytes 442376 | tf_op jit(solution)/shard_map/ppermute | solution.py:381
  53.6 5.8 %collective-permute-start.2 = (bf16[64,1152]{1,0:T(8,128)(2,1)S(1)}, bf16[64,1152]{1,0:T(8,128)(2,1)S(1)}, u32[]{:S(2)}, u32[]{:S(2)}) collective-permute-start(bf16[64,1152]{1,0:T(8,128)(2,1)S(1)} %add_convert_fusion), channel_id=1, source_target_pairs={{0,2},{1,3},{2,0},{3,1},{4,6},{5,7},{6,4},{7,5},{8,10},{9,11},{10,... | collective-permute-start | bytes 442376 | tf_op jit(solution)/shard_map/ppermute | solution.py:381

commit v6 on v4

--- a/solution.py
+++ b/solution.py
@@ -142,9 +142,9 @@
     copy.start()
     held = []
     size = held_refs[0].shape[0]
-    for offset, held_ref in enumerate(held_refs):
-        source = wigner_ref.at[pl.ds(targets_ref[offset] * size, size), :]
-        held.append(pltpu.make_async_copy(source, held_ref, held_sem.at[offset]))
+    for number, held_ref in enumerate(held_refs):
+        source = wigner_ref.at[pl.ds(targets_ref[number] * size, size), :]
+        held.append(pltpu.make_async_copy(source, held_ref, held_sem.at[number]))
         held[-1].start()
     acc_ref[...] = jnp.zeros_like(acc_ref)
     places = lax.broadcasted_iota(jnp.int32, (LOW, LANES), 0).astype(F32)
@@ -242,15 +242,16 @@
 
 def order_kernel(chunk, offset, where_ref, coeff_ref, wigner_ref, out_ref):
     depth = coeff_ref.shape[1]
+    size = chunk * depth
     rows = out_ref.shape[0]
     base = where_ref[offset] * rows
-    shape = (2 * chunk, chunk * depth)
+    shape = (2 * chunk, size)
     own = lax.broadcasted_iota(jnp.int32, shape, 0) // 2 == lax.broadcasted_iota(jnp.int32, shape, 1) // depth
     for number in range(rows // (2 * chunk)):
         start = pl.multiple_of(base + number * 2 * chunk, 2 * chunk)
         coeff = coeff_ref[pl.ds(start, 2 * chunk), :].astype(F32)
         wide = jnp.where(own, jnp.concatenate([coeff] * chunk, axis=1), 0.0).astype(BF16)
-        part = dot(wide, wigner_ref[number * chunk * depth : (number + 1) * chunk * depth, :], 1, 0)
+        part = dot(wide, wigner_ref[number * size : (number + 1) * size, :], 1, 0)
         out_ref[number * 2 * chunk : (number + 1) * 2 * chunk, :] = part.astype(out_ref.dtype)
 
 
@@ -286,6 +287,7 @@
         + [pltpu.VMEM(shape, jnp.int32)] * 3
         + [pltpu.SemaphoreType.DMA((6,))],
         compiler_params=pltpu.CompilerParams(vmem_limit_bytes=6 << 20),
+        cost_estimate=pl.CostEstimate(flops=10**11, transcendentals=0, bytes_accessed=10**8),
         name="pack",
     )(
         me.reshape(1),
@@ -324,8 +326,8 @@
         targets,
         got,
         pltpu.with_memory_space_constraint(jnp.asarray(first_matrix(), BF16), pltpu.HBM),
-        pltpu.with_memory_space_constraint(jnp.asarray(tables, BF16), pltpu.HBM),
-        flat,
+        jnp.asarray(tables, BF16),
+        pltpu.with_memory_space_constraint(flat, pltpu.HBM),
     )
     rows = 2 * CYCLE_DEV * share
     spectra = spectra.reshape(groups * beams, rows, width)
@@ -351,13 +353,22 @@
             name="order",
         )(targets, coeff, pltpu.with_memory_space_constraint(held[offset], pltpu.VMEM))
 
-    total = None
-    for offset in range(beams - 1, -1, -1):
-        part = piece(offset, BF16 if offset else F32)
-        if offset:
-            part = lax.ppermute(part, "beam", [(i, i ^ offset) for i in range(beams)])
-        part = part.astype(F32)
-        total = part if total is None else total + part
+    def send(part, distance):
+        return lax.ppermute(part, "beam", [(i, i ^ distance) for i in range(beams)])
+
+    sequence = [offset for chip in range(beams // 2 - 1, -1, -1) for offset in (2 * chip + 1, 2 * chip)]
+    terms = []
+    near = None
+    for offset in sequence:
+        part = piece(offset, BF16 if offset % 2 else F32)
+        if offset % 2:
+            near = send(part, 1)
+        else:
+            part = part + near.astype(F32)
+            terms.append(send(part.astype(BF16), offset).astype(F32) if offset else part)
+    total = terms[-1]
+    for term in terms[:-1]:
+        total = total + term
     return total.reshape(mine, 2, ells)
 
 

time: 62 us -> 58.3 us (0.940)
  waiting for transfers between devices: 5.58 us -> 3.57 us
  starting transfers between devices: 1.92 us -> 1.02 us
  Pallas kernels: 23.7 us -> 22.8 us
    ppermute x3, waiting for transfers between devices: 5.58 us -> 3.57 us  [send(): return lax.ppermute(part, 'beam', [(i, i ^ distance) for i in range(beams)])]
    pallas_call x1, Pallas kernels: 14.1 us -> 13.2 us  [shards(): pl.pallas_call(lambda *refs: bin_kernel(share, unit, *refs), out_shape=(j...]
    ppermute x3, starting transfers between devices: 1.92 us -> 1.02 us  [send(): return lax.ppermute(part, 'beam', [(i, i ^ distance) for i in range(beams)])]
  transfers between devices with their start and end apart: 3 -> 3, of which waited for: 2 -> 1; matrix products, arithmetic and copies ran while one was open for 0% -> 0% of each run, Pallas kernels for 3% -> 10%
where the time goes in v6:
time: 58.3 us; the launch traced here: 58.1 us
  blocking collectives  29.7 us (51%)
  Pallas kernels  22.8 us (39%)
  waiting for transfers between devices  3.57 us (6%)
  starting transfers between devices  1.02 us (2%)
  local copies, waits for them, and re-layouts  0.88 us (2%)
    all_to_all x1, blocking collectives, shards(): got = lax.all_to_all(sent, 'blk', split_axis=0, concat_axis=0, tiled=True)  15.8 us
    all_to_all x1, blocking collectives, shards(): lax.all_to_all(spectra, ('blk', 'beam'), split_axis=0, concat_axis=0, til...  13.9 us
    pallas_call x1, Pallas kernels, shards(): pl.pallas_call(lambda *refs: bin_kernel(share, unit, *refs), out_shape=(j...  13.2 us
    pallas_call x4, Pallas kernels, piece(): pl.pallas_call(lambda *refs: order_kernel(chunk, offset, *refs), out_shap...  7.49 us
    ppermute x3, waiting for transfers between devices, send(): return lax.ppermute(part, 'beam', [(i, i ^ distance) for i in range(beams)])  3.57 us
    pallas_call x1, Pallas kernels, shards(): pl.pallas_call(lambda *refs: pack_kernel(groups, *refs), out_shape=(jax.S...  1.77 us
  transfers between devices with their start and end apart: 3, of which 1 were waited for; matrix products, arithmetic and copies ran while one was open for 0% of the time, Pallas kernels for 10%

profile of v6, /device:TPU:0, one launch (start us, length us, event | category | flops | bytes accessed | tf_op | source)
XLA Modules:
  0.0 58.1 jit_solution(16963673988411116773)
XLA Ops:
  0.0 0.0 copy-start
  0.0 1.8 %pack.1 = (bf16[8,3,40,128]{3,2,1,0:T(8,128)(2,1)S(1)}, s32[4]{0:T(128)S(1)}) custom-call(s32[1]{0:T(128)} %bitcast.refs_0_, s32[1,128]{1,0:T(1,128)} %bitcast.18, f32[128,128]{1,0:T(8,128)} %bitcast.13, f32[128,128]{1,0:T(8,128)} %bitcast.14, s32[128,128]{1,0:T(8,128)} %bitcast.15, s32[128,128]{1,0:T(8,128)} %bitcast.16, s32[128,128]{1,0:T(8,128)} %bitcast.17), custom_call_target="tpu_custom_call" | custom-call | flops 99999997952 | bytes 100000000 | tf_op jit(solution)/shard_map/pack/pallas_call | solution.py:277
  1.8 15.8 %all_to_all.10.refs_1_ = bf16[8,3,40,128]{3,2,1,0:T(8,128)(2,1)S(1)} all-to-all(bf16[8,3,40,128]{3,2,1,0:T(8,128)(2,1)S(1)} %get-tuple-element.13), channel_id=1, replica_groups=mesh['blk'=8,'beam'=4] {'blk'}, dimensions={0} | all-to-all | bytes 491520 | tf_op jit(solution)/shard_map/all_to_all | solution.py:301
  17.6 0.0 copy-done
  17.6 13.2 %bin.1 = (bf16[8,4,2,2,8,128]{5,4,3,2,1,0:T(8,128)(2,1)S(1)}, bf16[4096,1152]{1,0:T(8,128)(2,1)S(1)}, bf16[4096,1152]{1,0:T(8,128)(2,1)S(1)}, bf16[4096,1152]{1,0:T(8,128)(2,1)S(1)}, bf16[4096,1152]{1,0:T(8,128)(2,1)S(1)}) custom-call(s32[4]{0:T(128)S(1)} %get-tuple-element.12.refs_0_, bf16[8,3,40,128]{3,2,1,0:T(8,128)(2,1)S(1)} %all_to_all.10.refs_1_, ...), custom_call_target="tpu_custom_call" | custom-call | tf_op jit(solution)/shard_map/bin/pallas_call | solution.py:306
  30.8 13.9 %all_to_all.11 = bf16[32,32,128]{2,1,0:T(8,128)(2,1)S(1)} all-to-all(bf16[32,32,128]{2,1,0:T(8,128)(2,1)S(1)} %bitcast.11), channel_id=1, replica_groups=mesh['blk'=8,'beam'=4] {'blk','beam'}, dimensions={0} | all-to-all | bytes 524288 | tf_op jit(solution)/shard_map/all_to_all | solution.py:334
  44.6 0.4 coeff.1.refs_1_
  45.0 1.9 %order.7 = bf16[64,1152]{1,0:T(8,128)(2,1)S(1)} custom-call(s32[4]{0:T(128)S(1)} %get-tuple-element.12.refs_0_, bf16[256,128]{1,0:T(8,128)(2,1)S(1)} %coeff.1.refs_1_, bf16[4096,1152]{1,0:T(8,128)(2,1)S(1)} %get-tuple-element.18.refs_2_), custom_call_target="tpu_custom_call" | custom-call | tf_op jit(solution)/shard_map/order/pallas_call | solution.py:347
  46.9 0.1 collective-permute-start.1
  47.0 1.9 %order.5 = bf16[64,1152]{1,0:T(8,128)(2,1)S(1)} custom-call(s32[4]{0:T(128)S(1)} %get-tuple-element.12.refs_0_, bf16[256,128]{1,0:T(8,128)(2,1)S(1)} %coeff.1.refs_1_, bf16[4096,1152]{1,0:T(8,128)(2,1)S(1)} %get-tuple-element.16.refs_2_), custom_call_target="tpu_custom_call" | custom-call | tf_op jit(solution)/shard_map/order/pallas_call | solution.py:347
  48.8 1.9 %order.6 = f32[64,1152]{1,0:T(8,128)S(1)} custom-call(s32[4]{0:T(128)S(1)} %get-tuple-element.12.refs_0_, bf16[256,128]{1,0:T(8,128)(2,1)S(1)} %coeff.1.refs_1_, bf16[4096,1152]{1,0:T(8,128)(2,1)S(1)} %get-tuple-element.17.refs_2_), custom_call_target="tpu_custom_call" | custom-call | tf_op jit(solution)/shard_map/order/pallas_call | solution.py:347
  50.7 0.5 collective-permute-start
  51.3 0.0 collective-permute-done.1
  51.3 0.4 collective-permute-start.2
  51.7 1.9 %order.4 = f32[64,1152]{1,0:T(8,128)S(1)} custom-call(s32[4]{0:T(128)S(1)} %get-tuple-element.12.refs_0_, bf16[256,128]{1,0:T(8,128)(2,1)S(1)} %coeff.1.refs_1_, bf16[4096,1152]{1,0:T(8,128)(2,1)S(1)} %get-tuple-element.15.refs_2_), custom_call_target="tpu_custom_call" | custom-call | tf_op jit(solution)/shard_map/order/pallas_call | solution.py:347
  53.6 0.0 collective-permute-done
  53.6 3.6 %collective-permute-done.2 = bf16[64,1152]{1,0:T(8,128)(2,1)S(1)} collective-permute-done((bf16[64,1152]{1,0:T(8,128)(2,1)S(1)}, bf16[64,1152]{1,0:T(8,128)(2,1)S(1)}, u32[]{:S(2)}, u32[]{:S(2)}) %collective-permute-start.2) | collective-permute-done | bytes 147488 | tf_op jit(solution)/shard_map/ppermute | solution.py:357
  57.2 0.9 %reshape.43 = f32[32,2,1152]{2,1,0:T(2,128)} reshape(f32[64,1152]{1,0:T(8,128)S(1)} %convert_add_fusion) | data formatting | bytes 589824 | tf_op jit(solution)/shard_map/reshape | solution.py:372
  (2 shorter events, 0.1 us)
Async XLA Ops:
  0.0 17.6 %copy-start = (bf16[2,1024,1024]{2,1,0:T(8,128)(2,1)S(1)}, bf16[2,1024,1024]{2,1,0:T(8,128)(2,1)}, u32[]{:S(2)}) copy-start(bf16[2,1024,1024]{2,1,0:T(8,128)(2,1)} %constant.9.clone.refs_3_) | copy-start | bytes 12582916
  46.9 4.4 %collective-permute-start.1 = (bf16[64,1152]{1,0:T(8,128)(2,1)S(1)}, bf16[64,1152]{1,0:T(8,128)(2,1)S(1)}, u32[]{:S(2)}, u32[]{:S(2)}) collective-permute-start(bf16[64,1152]{1,0:T(8,128)(2,1)S(1)} %order.7), channel_id=1, source_target_pairs={{0,1},{1,0},{2,3},{3,2},{4,5},{5,4},{6,7},{7,6},{8,9},{9,8},{10,11... | collective-permute-start | bytes 442376 | tf_op jit(solution)/shard_map/ppermute | solution.py:357
  50.7 2.9 %collective-permute-start = (bf16[64,1152]{1,0:T(8,128)(2,1)S(1)}, bf16[64,1152]{1,0:T(8,128)(2,1)S(1)}, u32[]{:S(2)}, u32[]{:S(2)}) collective-permute-start(bf16[64,1152]{1,0:T(8,128)(2,1)S(1)} %order.5), channel_id=1, source_target_pairs={{0,1},{1,0},{2,3},{3,2},{4,5},{5,4},{6,7},{7,6},{8,9},{9,8},{10,11... | collective-permute-start | bytes 442376 | tf_op jit(solution)/shard_map/ppermute | solution.py:357
  51.3 5.8 %collective-permute-start.2 = (bf16[64,1152]{1,0:T(8,128)(2,1)S(1)}, bf16[64,1152]{1,0:T(8,128)(2,1)S(1)}, u32[]{:S(2)}, u32[]{:S(2)}) collective-permute-start(bf16[64,1152]{1,0:T(8,128)(2,1)S(1)} %add_convert_fusion), channel_id=1, source_target_pairs={{0,2},{1,3},{2,0},{3,1},{4,6},{5,7},{6,4},{7,5},{8,10},{9,11},{10,... | collective-permute-start | bytes 442376 | tf_op jit(solution)/shard_map/ppermute | solution.py:357

commit v7 on v6

--- a/solution.py
+++ b/solution.py
@@ -126,10 +126,10 @@
 def sort_tiles(tiles, first, last):
     for i, j in network(last - first):
         i, j = i + first, j + first
-        (value0, high0, low0), (value1, high1, low1) = tiles[i], tiles[j]
-        swap = low0 < low1
-        tiles[i] = (jnp.where(swap, value1, value0), jnp.where(swap, high1, high0), jnp.maximum(low0, low1))
-        tiles[j] = (jnp.where(swap, value0, value1), jnp.where(swap, high0, high1), jnp.minimum(low0, low1))
+        (value0, code0), (value1, code1) = tiles[i], tiles[j]
+        swap = code0 < code1
+        tiles[i] = (jnp.where(swap, value1, value0), jnp.maximum(code0, code1))
+        tiles[j] = (jnp.where(swap, value0, value1), jnp.minimum(code0, code1))
 
 
 def bin_kernel(share, unit, targets_ref, recv_ref, first_ref, second_ref, wigner_ref, out_ref, *rest):
@@ -141,9 +141,9 @@
     copy = pltpu.make_async_copy(second_ref, table_ref, sem)
     copy.start()
     held = []
-    size = held_refs[0].shape[0]
+    size = wigner_ref.shape[0] // len(held_refs)
     for number, held_ref in enumerate(held_refs):
-        source = wigner_ref.at[pl.ds(targets_ref[number] * size, size), :]
+        source = wigner_ref.at[pl.ds(targets_ref[number] * size, held_ref.shape[0]), :]
         held.append(pltpu.make_async_copy(source, held_ref, held_sem.at[number]))
         held[-1].start()
     acc_ref[...] = jnp.zeros_like(acc_ref)
@@ -153,11 +153,11 @@
     zero = jnp.zeros((LOW, LANES), BF16)
     one = jnp.ones((LOW, LANES), BF16)
 
-    tiles = [
-        tuple(recv_ref[source, plane, start : start + 8, :].astype(F32) for plane in range(3))
-        for source in range(groups)
-        for start in range(0, padded, 8)
-    ]
+    tiles = []
+    for source in range(groups):
+        for start in range(0, padded, 8):
+            value, high, low = (recv_ref[source, plane, start : start + 8, :].astype(F32) for plane in range(3))
+            tiles.append((value, low + jnp.where(low > 0, high, -high) * float(LOW)))
     count = len(tiles)
     sort_tiles(tiles, 0, count)
     start, stop = count // 5, count - count // 5
@@ -166,20 +166,23 @@
     sort_tiles(tiles, start, stop)
     end0 = jnp.zeros((8, LANES), F32)
     for number in range(count):
-        end0 = jnp.where(tiles[number][2] > 0, float(number + 1), end0)
+        end0 = jnp.where(tiles[number][1] > 0, float(number + 1), end0)
     begin1 = jnp.full((8, LANES), float(count), F32)
     for number in range(count - 1, -1, -1):
-        begin1 = jnp.where(tiles[number][2] < 0, float(number), begin1)
+        begin1 = jnp.where(tiles[number][1] < 0, float(number), begin1)
     for number in range(count):
-        for plane in range(3):
-            sorted_ref[plane, number] = tiles[number][plane].astype(BF16)
+        value, code = tiles[number]
+        place = jnp.abs(code)
+        high = jnp.floor((place - 1.0) * (1.0 / LOW))
+        low = place - high * float(LOW)
+        sorted_ref[0, number] = jnp.where(code > 0, value, 0.0).astype(BF16)
+        sorted_ref[1, number] = jnp.where(code > 0, 0.0, value).astype(BF16)
+        sorted_ref[2, number] = high.astype(BF16)
+        sorted_ref[3, number] = low.astype(BF16)
 
     def one_unit(t, number, carry):
         for step in range(unit):
-            value, high, low = (sorted_ref[plane, number * unit + step] for plane in range(3))
-            blank = jnp.zeros_like(value)
-            value = jnp.where(low > 0, value, blank) if t == 0 else jnp.where(low > 0, blank, value)
-            low = jnp.abs(low)
+            value, high, low = (sorted_ref[plane, number * unit + step] for plane in (t, 2, 3))
             left, right = [], []
             for row in range(8):
                 left.append(jnp.where(places_hi == high[row : row + 1, :], value[row : row + 1, :], zero))
@@ -240,19 +243,40 @@
     out_ref[...] = total.astype(BF16)
 
 
-def order_kernel(chunk, offset, where_ref, coeff_ref, wigner_ref, out_ref):
+def order_kernel(chunk, offset, late, where_ref, coeff_ref, wigner_ref, *refs):
     depth = coeff_ref.shape[1]
     size = chunk * depth
-    rows = out_ref.shape[0]
+    copy = None
+    if late:
+        source_ref, out_ref, late_ref, sem = refs
+        rows = out_ref.shape[0]
+        first = where_ref[offset] * (rows // 2 * depth) + wigner_ref.shape[0]
+        copy = pltpu.make_async_copy(source_ref.at[pl.ds(first, late * size), :], late_ref, sem)
+        copy.start()
+    else:
+        (out_ref,) = refs
+        rows = out_ref.shape[0]
     base = where_ref[offset] * rows
     shape = (2 * chunk, size)
     own = lax.broadcasted_iota(jnp.int32, shape, 0) // 2 == lax.broadcasted_iota(jnp.int32, shape, 1) // depth
-    for number in range(rows // (2 * chunk)):
+    early = wigner_ref.shape[0] // size
+    for number in range(early + late):
+        if number == early:
+            copy.wait()
+        table, at = (wigner_ref, number) if number < early else (late_ref, number - early)
         start = pl.multiple_of(base + number * 2 * chunk, 2 * chunk)
         coeff = coeff_ref[pl.ds(start, 2 * chunk), :].astype(F32)
         wide = jnp.where(own, jnp.concatenate([coeff] * chunk, axis=1), 0.0).astype(BF16)
-        part = dot(wide, wigner_ref[number * size : (number + 1) * size, :], 1, 0)
+        part = dot(wide, table[at * size : (at + 1) * size, :], 1, 0)
         out_ref[number * 2 * chunk : (number + 1) * 2 * chunk, :] = part.astype(out_ref.dtype)
+
+
+def sum_kernel(*refs):
+    *terms, out_ref = refs
+    total = terms[0][...].astype(F32)
+    for term in terms[1:]:
+        total = total + term[...].astype(F32)
+    out_ref[...] = total.reshape(out_ref.shape)
 
 
 def shards(signal, weight, cycle, phi, psi, owner, wigner):
@@ -303,16 +327,20 @@
     tiles = groups * padded // 8
     unit = next(size for size in (5, 4, 2, 1) if tiles % size == 0)
     flat = wigner.reshape(orders * depth, ells)
+    mine = orders // beams
+    chunk = 8
+    steps = mine // chunk
+    early = (steps + 1) // 2
     spectra, *held = pl.pallas_call(
         lambda *refs: bin_kernel(share, unit, *refs),
         out_shape=(
             jax.ShapeDtypeStruct((groups, beams, 2, CYCLE_DEV, share, width), BF16),
         )
-        + tuple(pltpu.VMEM((flat.shape[0] // beams, ells), BF16) for _ in range(beams)),
+        + tuple(pltpu.VMEM((count * chunk * depth, ells), BF16) for count in [early] + [steps] * (beams - 1)),
         in_specs=[scalars, whole, anywhere, anywhere, anywhere],
         out_specs=(whole,) * (1 + beams),
         scratch_shapes=[
-            pltpu.VMEM((3, tiles, 8, LANES), BF16),
+            pltpu.VMEM((4, tiles, 8, LANES), BF16),
             pltpu.VMEM((CYCLE_DEV, LOW, LOW), F32),
             pltpu.VMEM((LOW, LOW), BF16),
             pltpu.VMEM(tables.shape, BF16),
@@ -340,18 +368,20 @@
         name="coeff",
     )(parts)
 
-    mine = orders // beams
-    chunk = 8
-
     def piece(offset, kind):
+        late = 0 if offset else steps - early
+        table = pltpu.with_memory_space_constraint(held[offset], pltpu.VMEM)
+        source = [pltpu.with_memory_space_constraint(flat, pltpu.HBM)] if late else []
+        scratch = [pltpu.VMEM((late * chunk * depth, ells), BF16), pltpu.SemaphoreType.DMA] if late else []
         return pl.pallas_call(
-            lambda *refs: order_kernel(chunk, offset, *refs),
+            lambda *refs: order_kernel(chunk, offset, late, *refs),
             out_shape=jax.ShapeDtypeStruct((2 * mine, ells), kind),
-            in_specs=[scalars, whole, whole],
+            in_specs=[scalars, whole, whole] + [anywhere] * len(source),
             out_specs=whole,
+            scratch_shapes=scratch,
             compiler_params=pltpu.CompilerParams(vmem_limit_bytes=6 << 20),
             name="order",
-        )(targets, coeff, pltpu.with_memory_space_constraint(held[offset], pltpu.VMEM))
+        )(targets, coeff, table, *source)
 
     def send(part, distance):
         return lax.ppermute(part, "beam", [(i, i ^ distance) for i in range(beams)])
@@ -363,13 +393,16 @@
         part = piece(offset, BF16 if offset % 2 else F32)
         if offset % 2:
             near = send(part, 1)
+        elif offset:
+            terms.append(send((part + near.astype(F32)).astype(BF16), offset))
         else:
-            part = part + near.astype(F32)
-            terms.append(send(part.astype(BF16), offset).astype(F32) if offset else part)
-    total = terms[-1]
-    for term in terms[:-1]:
-        total = total + term
-    return total.reshape(mine, 2, ells)
+            terms = [part, near] + terms
+    return pl.pallas_call(
+        sum_kernel,
+        out_shape=jax.ShapeDtypeStruct((mine, 2, ells), F32),
+        compiler_params=pltpu.CompilerParams(vmem_limit_bytes=6 << 20),
+        name="sum",
+    )(*terms)
 
 
 def solution(mesh):

time: 58.3 us -> 56.8 us (0.974)
  waiting for transfers between devices: 3.57 us -> 1.22 us
  Pallas kernels: 22.8 us -> 24.7 us
  local copies, waits for them, and re-layouts: 0.88 us -> 0.01 us
    pallas_call x4 -> x5, Pallas kernels: 7.49 us -> 10.6 us  [the longest x4 9.83 us: piece(): pl.pallas_call(lambda *refs: order_kernel(chunk, offset, late, *refs), ou...]
    ppermute x3, waiting for transfers between devices: 3.57 us -> 1.22 us  [send(): return lax.ppermute(part, 'beam', [(i, i ^ distance) for i in range(beams)])]
    pallas_call x1, Pallas kernels: 13.2 us -> 11.9 us  [shards(): pl.pallas_call(lambda *refs: bin_kernel(share, unit, *refs), out_shape=(j...]
    reshape x1 -> x0, local copies, waits for them, and re-layouts: 0.88 us -> none  [shards(): return total.reshape(mine, 2, ells)]
  transfers between devices with their start and end apart: 3 -> 3, of which waited for: 1 -> 1; matrix products, arithmetic and copies ran while one was open for 0% -> 0% of each run, Pallas kernels for 10% -> 14%
where the time goes in v7:
time: 56.8 us; the launch traced here: 56.6 us
  blocking collectives  29.7 us (52%)
  Pallas kernels  24.7 us (43%)
  waiting for transfers between devices  1.22 us (2%)
  starting transfers between devices  1.02 us (2%)
    all_to_all x1, blocking collectives, shards(): got = lax.all_to_all(sent, 'blk', split_axis=0, concat_axis=0, tiled=True)  15.8 us
    all_to_all x1, blocking collectives, shards(): lax.all_to_all(spectra, ('blk', 'beam'), split_axis=0, concat_axis=0, til...  13.9 us
    pallas_call x1, Pallas kernels, shards(): pl.pallas_call(lambda *refs: bin_kernel(share, unit, *refs), out_shape=(j...  11.9 us
    pallas_call x4, Pallas kernels, piece(): pl.pallas_call(lambda *refs: order_kernel(chunk, offset, late, *refs), ou...  9.83 us
    pallas_call x1, Pallas kernels, shards(): pl.pallas_call(lambda *refs: pack_kernel(groups, *refs), out_shape=(jax.S...  1.77 us
    ppermute x3, waiting for transfers between devices, send(): return lax.ppermute(part, 'beam', [(i, i ^ distance) for i in range(beams)])  1.22 us
  transfers between devices with their start and end apart: 3, of which 1 were waited for; matrix products, arithmetic and copies ran while one was open for 0% of the time, Pallas kernels for 14%

profile of v7, /device:TPU:0, one launch (start us, length us, event | category | flops | bytes accessed | tf_op | source)
XLA Modules:
  0.0 56.6 jit_solution(15451491167615999150)
XLA Ops:
  0.0 0.0 copy-start
  0.0 1.8 %pack.1 = (bf16[8,3,40,128]{3,2,1,0:T(8,128)(2,1)S(1)}, s32[4]{0:T(128)S(1)}) custom-call(s32[1]{0:T(128)} %bitcast.refs_0_, s32[1,128]{1,0:T(1,128)} %bitcast.19, f32[128,128]{1,0:T(8,128)} %bitcast.14, f32[128,128]{1,0:T(8,128)} %bitcast.15, s32[128,128]{1,0:T(8,128)} %bitcast.16, s32[128,128]{1,0:T(8,128)} %bitcast.17, s32[128,128]{1,0:T(8,128)} %bitcast.18), custom_call_target="tpu_custom_call" | custom-call | flops 99999997952 | bytes 100000000 | tf_op jit(solution)/shard_map/pack/pallas_call | solution.py:301
  1.8 15.8 %all_to_all.10.refs_1_ = bf16[8,3,40,128]{3,2,1,0:T(8,128)(2,1)S(1)} all-to-all(bf16[8,3,40,128]{3,2,1,0:T(8,128)(2,1)S(1)} %get-tuple-element.13), channel_id=1, replica_groups=mesh['blk'=8,'beam'=4] {'blk'}, dimensions={0} | all-to-all | bytes 491520 | tf_op jit(solution)/shard_map/all_to_all | solution.py:325
  17.6 0.0 copy-done
  17.6 11.9 %bin.1 = (bf16[8,4,2,2,8,128]{5,4,3,2,1,0:T(8,128)(2,1)S(1)}, bf16[2048,1152]{1,0:T(8,128)(2,1)S(1)}, bf16[4096,1152]{1,0:T(8,128)(2,1)S(1)}, bf16[4096,1152]{1,0:T(8,128)(2,1)S(1)}, bf16[4096,1152]{1,0:T(8,128)(2,1)S(1)}) custom-call(s32[4]{0:T(128)S(1)} %get-tuple-element.12.refs_0_, bf16[8,3,40,128]{3,2,1,0:T(8,128)(2,1)S(1)} %all_to_all.10.refs_1_, ...), custom_call_target="tpu_custom_call" | custom-call | tf_op jit(solution)/shard_map/bin/pallas_call | solution.py:334
  29.5 13.9 %all_to_all.11 = bf16[32,32,128]{2,1,0:T(8,128)(2,1)S(1)} all-to-all(bf16[32,32,128]{2,1,0:T(8,128)(2,1)S(1)} %bitcast.11), channel_id=1, replica_groups=mesh['blk'=8,'beam'=4] {'blk','beam'}, dimensions={0} | all-to-all | bytes 524288 | tf_op jit(solution)/shard_map/all_to_all | solution.py:362
  43.3 0.4 coeff.1.refs_1_
  43.7 1.9 %order.7 = bf16[64,1152]{1,0:T(8,128)(2,1)S(1)} custom-call(s32[4]{0:T(128)S(1)} %get-tuple-element.12.refs_0_, bf16[256,128]{1,0:T(8,128)(2,1)S(1)} %coeff.1.refs_1_, bf16[4096,1152]{1,0:T(8,128)(2,1)S(1)} %get-tuple-element.18.refs_2_), custom_call_target="tpu_custom_call" | custom-call | tf_op jit(solution)/shard_map/order/pallas_call | solution.py:376
  45.6 0.1 collective-permute-start.1
  45.7 1.9 %order.5 = bf16[64,1152]{1,0:T(8,128)(2,1)S(1)} custom-call(s32[4]{0:T(128)S(1)} %get-tuple-element.12.refs_0_, bf16[256,128]{1,0:T(8,128)(2,1)S(1)} %coeff.1.refs_1_, bf16[4096,1152]{1,0:T(8,128)(2,1)S(1)} %get-tuple-element.16.refs_2_), custom_call_target="tpu_custom_call" | custom-call | tf_op jit(solution)/shard_map/order/pallas_call | solution.py:376
  47.5 1.9 %order.6 = f32[64,1152]{1,0:T(8,128)S(1)} custom-call(s32[4]{0:T(128)S(1)} %get-tuple-element.12.refs_0_, bf16[256,128]{1,0:T(8,128)(2,1)S(1)} %coeff.1.refs_1_, bf16[4096,1152]{1,0:T(8,128)(2,1)S(1)} %get-tuple-element.17.refs_2_), custom_call_target="tpu_custom_call" | custom-call | tf_op jit(solution)/shard_map/order/pallas_call | solution.py:376
  49.4 0.5 collective-permute-start
  50.0 0.0 collective-permute-done.1
  50.0 0.4 collective-permute-start.2
  50.4 4.2 %order.4.refs_0_ = f32[64,1152]{1,0:T(8,128)S(1)} custom-call(s32[4]{0:T(128)S(1)} %get-tuple-element.12.refs_0_, bf16[256,128]{1,0:T(8,128)(2,1)S(1)} %coeff.1.refs_1_, bf16[2048,1152]{1,0:T(8,128)(2,1)S(1)} %get-tuple-element.15.refs_2_, bf16[16384,1152]{1,0:T(8,128)(2,1)} %bitcast.13), custom_call_target="tpu_custom_call" | custom-call | tf_op jit(solution)/shard_map/order/pallas_call | solution.py:376
  54.6 0.0 collective-permute-done.refs_1_
  54.6 1.2 %collective-permute-done.2.refs_2_ = bf16[64,1152]{1,0:T(8,128)(2,1)S(1)} collective-permute-done((bf16[64,1152]{1,0:T(8,128)(2,1)S(1)}, bf16[64,1152]{1,0:T(8,128)(2,1)S(1)}, u32[]{:S(2)}, u32[]{:S(2)}) %collective-permute-start.2) | collective-permute-done | bytes 147488 | tf_op jit(solution)/shard_map/ppermute | solution.py:387
  55.9 0.8 %sum.1 = f32[32,2,1152]{2,1,0:T(2,128)} custom-call(f32[64,1152]{1,0:T(8,128)S(1)} %order.4.refs_0_, bf16[64,1152]{1,0:T(8,128)(2,1)S(1)} %collective-permute-done.refs_1_, bf16[64,1152]{1,0:T(8,128)(2,1)S(1)} %collective-permute-done.2.refs_2_), custom_call_target="tpu_custom_call" | custom-call | tf_op jit(solution)/shard_map/sum/pallas_call | solution.py:400
  (1 shorter events, 0.0 us)
Async XLA Ops:
  0.0 17.6 %copy-start = (bf16[2,1024,1024]{2,1,0:T(8,128)(2,1)S(1)}, bf16[2,1024,1024]{2,1,0:T(8,128)(2,1)}, u32[]{:S(2)}) copy-start(bf16[2,1024,1024]{2,1,0:T(8,128)(2,1)} %constant.9.clone.refs_3_) | copy-start | bytes 12582916
  45.6 4.4 %collective-permute-start.1 = (bf16[64,1152]{1,0:T(8,128)(2,1)S(1)}, bf16[64,1152]{1,0:T(8,128)(2,1)S(1)}, u32[]{:S(2)}, u32[]{:S(2)}) collective-permute-start(bf16[64,1152]{1,0:T(8,128)(2,1)S(1)} %order.7), channel_id=1, source_target_pairs={{0,1},{1,0},{2,3},{3,2},{4,5},{5,4},{6,7},{7,6},{8,9},{9,8},{10,11... | collective-permute-start | bytes 442376 | tf_op jit(solution)/shard_map/ppermute | solution.py:387
  49.4 5.2 %collective-permute-start = (bf16[64,1152]{1,0:T(8,128)(2,1)S(1)}, bf16[64,1152]{1,0:T(8,128)(2,1)S(1)}, u32[]{:S(2)}, u32[]{:S(2)}) collective-permute-start(bf16[64,1152]{1,0:T(8,128)(2,1)S(1)} %order.5), channel_id=1, source_target_pairs={{0,1},{1,0},{2,3},{3,2},{4,5},{5,4},{6,7},{7,6},{8,9},{9,8},{10,11... | collective-permute-start | bytes 442376 | tf_op jit(solution)/shard_map/ppermute | solution.py:387
  50.0 5.8 %collective-permute-start.2 = (bf16[64,1152]{1,0:T(8,128)(2,1)S(1)}, bf16[64,1152]{1,0:T(8,128)(2,1)S(1)}, u32[]{:S(2)}, u32[]{:S(2)}) collective-permute-start(bf16[64,1152]{1,0:T(8,128)(2,1)S(1)} %add_convert_fusion), channel_id=1, source_target_pairs={{0,2},{1,3},{2,0},{3,1},{4,6},{5,7},{6,4},{7,5},{8,10},{9,11},{10,... | collective-permute-start | bytes 442376 | tf_op jit(solution)/shard_map/ppermute | solution.py:387

commit v8 on v7

--- a/solution.py
+++ b/solution.py
@@ -246,29 +246,37 @@
 def order_kernel(chunk, offset, late, where_ref, coeff_ref, wigner_ref, *refs):
     depth = coeff_ref.shape[1]
     size = chunk * depth
-    copy = None
+    copies = []
     if late:
         source_ref, out_ref, late_ref, sem = refs
-        rows = out_ref.shape[0]
-        first = where_ref[offset] * (rows // 2 * depth) + wigner_ref.shape[0]
-        copy = pltpu.make_async_copy(source_ref.at[pl.ds(first, late * size), :], late_ref, sem)
-        copy.start()
+        first = where_ref[offset] * (out_ref.shape[0] // 2 * depth) + wigner_ref.shape[0]
+        for number in range(late):
+            source = source_ref.at[pl.ds(first + number * size, size), :]
+            copies.append(pltpu.make_async_copy(source, late_ref.at[number], sem.at[number]))
+            copies[-1].start()
     else:
         (out_ref,) = refs
-        rows = out_ref.shape[0]
+    rows = out_ref.shape[0]
     base = where_ref[offset] * rows
     shape = (2 * chunk, size)
     own = lax.broadcasted_iota(jnp.int32, shape, 0) // 2 == lax.broadcasted_iota(jnp.int32, shape, 1) // depth
     early = wigner_ref.shape[0] // size
     for number in range(early + late):
-        if number == early:
-            copy.wait()
-        table, at = (wigner_ref, number) if number < early else (late_ref, number - early)
         start = pl.multiple_of(base + number * 2 * chunk, 2 * chunk)
         coeff = coeff_ref[pl.ds(start, 2 * chunk), :].astype(F32)
         wide = jnp.where(own, jnp.concatenate([coeff] * chunk, axis=1), 0.0).astype(BF16)
-        part = dot(wide, table[at * size : (at + 1) * size, :], 1, 0)
+        if number < early:
+            table = wigner_ref[number * size : (number + 1) * size, :]
+        else:
+            copies[number - early].wait()
+            table = late_ref[number - early]
+        part = dot(wide, table, 1, 0)
         out_ref[number * 2 * chunk : (number + 1) * 2 * chunk, :] = part.astype(out_ref.dtype)
+
+
+def first_order_kernel(groups, orders, chunk, offset, where_ref, recv_ref, wigner_ref, coeff_ref, out_ref):
+    coeff_kernel(groups, orders, recv_ref, coeff_ref)
+    order_kernel(chunk, offset, 0, where_ref, coeff_ref, wigner_ref, out_ref)
 
 
 def sum_kernel(*refs):
@@ -361,18 +369,25 @@
     spectra = spectra.reshape(groups * beams, rows, width)
     parts = lax.all_to_all(spectra, ("blk", "beam"), split_axis=0, concat_axis=0, tiled=True)
     parts = parts.reshape(groups, beams, 2, CYCLE_DEV, share, width)
-    coeff = pl.pallas_call(
-        lambda *refs: coeff_kernel(groups, orders, *refs),
-        out_shape=jax.ShapeDtypeStruct((2 * orders, depth), BF16),
-        compiler_params=pltpu.CompilerParams(vmem_limit_bytes=6 << 20),
-        name="coeff",
-    )(parts)
-
-    def piece(offset, kind):
+
+    def first_piece(offset, kind):
+        return pl.pallas_call(
+            lambda *refs: first_order_kernel(groups, orders, chunk, offset, *refs),
+            out_shape=(
+                jax.ShapeDtypeStruct((2 * orders, depth), BF16),
+                jax.ShapeDtypeStruct((2 * mine, ells), kind),
+            ),
+            in_specs=[scalars, whole, whole],
+            out_specs=(whole, whole),
+            compiler_params=pltpu.CompilerParams(vmem_limit_bytes=6 << 20),
+            name="first",
+        )(targets, parts, pltpu.with_memory_space_constraint(held[offset], pltpu.VMEM))
+
+    def piece(coeff, offset, kind):
         late = 0 if offset else steps - early
         table = pltpu.with_memory_space_constraint(held[offset], pltpu.VMEM)
         source = [pltpu.with_memory_space_constraint(flat, pltpu.HBM)] if late else []
-        scratch = [pltpu.VMEM((late * chunk * depth, ells), BF16), pltpu.SemaphoreType.DMA] if late else []
+        scratch = [pltpu.VMEM((late, chunk * depth, ells), BF16), pltpu.SemaphoreType.DMA((late,))] if late else []
         return pl.pallas_call(
             lambda *refs: order_kernel(chunk, offset, late, *refs),
             out_shape=jax.ShapeDtypeStruct((2 * mine, ells), kind),
@@ -390,7 +405,10 @@
     terms = []
     near = None
     for offset in sequence:
-        part = piece(offset, BF16 if offset % 2 else F32)
+        if offset == beams - 1:
+            coeff, part = first_piece(offset, BF16)
+        else:
+            part = piece(coeff, offset, BF16 if offset % 2 else F32)
         if offset % 2:
             near = send(part, 1)
         elif offset:

time: 56.8 us -> 56.8 us (level)
  Pallas kernels: 24.7 us -> 23.8 us
  waiting for transfers between devices: 1.22 us -> 2.05 us
    pallas_call x4 -> x3, Pallas kernels: 9.83 us -> 7.13 us  [piece(): pl.pallas_call(lambda *refs: order_kernel(chunk, offset, late, *refs), ou...]
    pallas_call x1, Pallas kernels: 0.38 us -> 2.23 us  [first_piece(): pl.pallas_call(lambda *refs: first_order_kernel(groups, orders, chunk, of...]
    ppermute x3, waiting for transfers between devices: 1.22 us -> 2.05 us  [send(): return lax.ppermute(part, 'beam', [(i, i ^ distance) for i in range(beams)])]
  transfers between devices with their start and end apart: 3 -> 3, of which waited for: 1 -> 1; matrix products, arithmetic and copies ran while one was open for 0% -> 0% of each run, Pallas kernels for 14% -> 13%
where the time goes in v8:
time: 56.8 us; the launch traced here: 56.6 us
  blocking collectives  29.7 us (52%)
  Pallas kernels  23.8 us (42%)
  waiting for transfers between devices  2.05 us (4%)
  starting transfers between devices  1.02 us (2%)
    all_to_all x1, blocking collectives, shards(): got = lax.all_to_all(sent, 'blk', split_axis=0, concat_axis=0, tiled=True)  15.8 us
    all_to_all x1, blocking collectives, shards(): lax.all_to_all(spectra, ('blk', 'beam'), split_axis=0, concat_axis=0, til...  13.9 us
    pallas_call x1, Pallas kernels, shards(): pl.pallas_call(lambda *refs: bin_kernel(share, unit, *refs), out_shape=(j...  11.9 us
    pallas_call x3, Pallas kernels, piece(): pl.pallas_call(lambda *refs: order_kernel(chunk, offset, late, *refs), ou...  7.13 us
    pallas_call x1, Pallas kernels, first_piece(): pl.pallas_call(lambda *refs: first_order_kernel(groups, orders, chunk, of...  2.23 us
    ppermute x3, waiting for transfers between devices, send(): return lax.ppermute(part, 'beam', [(i, i ^ distance) for i in range(beams)])  2.05 us
    pallas_call x1, Pallas kernels, shards(): pl.pallas_call(lambda *refs: pack_kernel(groups, *refs), out_shape=(jax.S...  1.77 us
  transfers between devices with their start and end apart: 3, of which 1 were waited for; matrix products, arithmetic and copies ran while one was open for 0% of the time, Pallas kernels for 13%

profile of v8, /device:TPU:0, one launch (start us, length us, event | category | flops | bytes accessed | tf_op | source)
XLA Modules:
  0.0 56.6 jit_solution(1396582328024110147)
XLA Ops:
  0.0 0.0 copy-start
  0.0 1.8 %pack.1 = (bf16[8,3,40,128]{3,2,1,0:T(8,128)(2,1)S(1)}, s32[4]{0:T(128)S(1)}) custom-call(s32[1]{0:T(128)} %bitcast.refs_0_, s32[1,128]{1,0:T(1,128)} %bitcast.19, f32[128,128]{1,0:T(8,128)} %bitcast.14, f32[128,128]{1,0:T(8,128)} %bitcast.15, s32[128,128]{1,0:T(8,128)} %bitcast.16, s32[128,128]{1,0:T(8,128)} %bitcast.17, s32[128,128]{1,0:T(8,128)} %bitcast.18), custom_call_target="tpu_custom_call" | custom-call | flops 99999997952 | bytes 100000000 | tf_op jit(solution)/shard_map/pack/pallas_call | solution.py:309
  1.8 15.8 %all_to_all.10.refs_1_ = bf16[8,3,40,128]{3,2,1,0:T(8,128)(2,1)S(1)} all-to-all(bf16[8,3,40,128]{3,2,1,0:T(8,128)(2,1)S(1)} %get-tuple-element.15), channel_id=1, replica_groups=mesh['blk'=8,'beam'=4] {'blk'}, dimensions={0} | all-to-all | bytes 491520 | tf_op jit(solution)/shard_map/all_to_all | solution.py:333
  17.6 0.0 copy-done
  17.6 11.9 %bin.1 = (bf16[8,4,2,2,8,128]{5,4,3,2,1,0:T(8,128)(2,1)S(1)}, bf16[2048,1152]{1,0:T(8,128)(2,1)S(1)}, bf16[4096,1152]{1,0:T(8,128)(2,1)S(1)}, bf16[4096,1152]{1,0:T(8,128)(2,1)S(1)}, bf16[4096,1152]{1,0:T(8,128)(2,1)S(1)}) custom-call(s32[4]{0:T(128)S(1)} %get-tuple-element.14.refs_0_, bf16[8,3,40,128]{3,2,1,0:T(8,128)(2,1)S(1)} %all_to_all.10.refs_1_, ...), custom_call_target="tpu_custom_call" | custom-call | tf_op jit(solution)/shard_map/bin/pallas_call | solution.py:342
  29.5 13.9 %all_to_all.11 = bf16[32,32,128]{2,1,0:T(8,128)(2,1)S(1)} all-to-all(bf16[32,32,128]{2,1,0:T(8,128)(2,1)S(1)} %bitcast.11), channel_id=1, replica_groups=mesh['blk'=8,'beam'=4] {'blk','beam'}, dimensions={0} | all-to-all | bytes 524288 | tf_op jit(solution)/shard_map/all_to_all | solution.py:370
  43.3 2.2 %first.1 = (bf16[256,128]{1,0:T(8,128)(2,1)S(1)}, bf16[64,1152]{1,0:T(8,128)(2,1)S(1)}) custom-call(s32[4]{0:T(128)S(1)} %get-tuple-element.14.refs_0_, bf16[8,4,2,2,8,128]{5,4,3,2,1,0:T(8,128)(2,1)S(1)} %bitcast.10, bf16[4096,1152]{1,0:T(8,128)(2,1)S(1)} %get-tuple-element.17.refs_2_), custom_call_target="tpu_custom_call" | custom-call | tf_op jit(solution)/shard_map/first/pallas_call | solution.py:374
  45.6 0.1 collective-permute-start.1
  45.7 1.9 %order.4 = bf16[64,1152]{1,0:T(8,128)(2,1)S(1)} custom-call(s32[4]{0:T(128)S(1)} %get-tuple-element.14.refs_0_, bf16[256,128]{1,0:T(8,128)(2,1)S(1)} %get-tuple-element.18.refs_1_, bf16[4096,1152]{1,0:T(8,128)(2,1)S(1)} %get-tuple-element.20.refs_2_), custom_call_target="tpu_custom_call" | custom-call | tf_op jit(solution)/shard_map/order/pallas_call | solution.py:391
  47.5 1.9 %order.5 = f32[64,1152]{1,0:T(8,128)S(1)} custom-call(s32[4]{0:T(128)S(1)} %get-tuple-element.14.refs_0_, bf16[256,128]{1,0:T(8,128)(2,1)S(1)} %get-tuple-element.18.refs_1_, bf16[4096,1152]{1,0:T(8,128)(2,1)S(1)} %get-tuple-element.21.refs_2_), custom_call_target="tpu_custom_call" | custom-call | tf_op jit(solution)/shard_map/order/pallas_call | solution.py:391
  49.4 0.5 collective-permute-start
  50.0 0.0 collective-permute-done.1
  50.0 0.4 collective-permute-start.2
  50.4 3.4 %order.3.refs_0_ = f32[64,1152]{1,0:T(8,128)S(1)} custom-call(s32[4]{0:T(128)S(1)} %get-tuple-element.14.refs_0_, bf16[256,128]{1,0:T(8,128)(2,1)S(1)} %get-tuple-element.18.refs_1_, bf16[2048,1152]{1,0:T(8,128)(2,1)S(1)} %get-tuple-element.19.refs_2_, bf16[16384,1152]{1,0:T(8,128)(2,1)} %bitcast.13), custom_call_target="tpu_custom_call" | custom-call | tf_op jit(solution)/shard_map/order/pallas_call | solution.py:391
  53.8 0.0 collective-permute-done.refs_1_
  53.8 2.0 %collective-permute-done.2.refs_2_ = bf16[64,1152]{1,0:T(8,128)(2,1)S(1)} collective-permute-done((bf16[64,1152]{1,0:T(8,128)(2,1)S(1)}, bf16[64,1152]{1,0:T(8,128)(2,1)S(1)}, u32[]{:S(2)}, u32[]{:S(2)}) %collective-permute-start.2) | collective-permute-done | bytes 147488 | tf_op jit(solution)/shard_map/ppermute | solution.py:402
  55.8 0.8 %sum.1 = f32[32,2,1152]{2,1,0:T(2,128)} custom-call(f32[64,1152]{1,0:T(8,128)S(1)} %order.3.refs_0_, bf16[64,1152]{1,0:T(8,128)(2,1)S(1)} %collective-permute-done.refs_1_, bf16[64,1152]{1,0:T(8,128)(2,1)S(1)} %collective-permute-done.2.refs_2_), custom_call_target="tpu_custom_call" | custom-call | tf_op jit(solution)/shard_map/sum/pallas_call | solution.py:418
  (1 shorter events, 0.0 us)
Async XLA Ops:
  0.0 17.6 %copy-start = (bf16[2,1024,1024]{2,1,0:T(8,128)(2,1)S(1)}, bf16[2,1024,1024]{2,1,0:T(8,128)(2,1)}, u32[]{:S(2)}) copy-start(bf16[2,1024,1024]{2,1,0:T(8,128)(2,1)} %constant.9.clone.refs_3_) | copy-start | bytes 12582916
  45.6 4.4 %collective-permute-start.1 = (bf16[64,1152]{1,0:T(8,128)(2,1)S(1)}, bf16[64,1152]{1,0:T(8,128)(2,1)S(1)}, u32[]{:S(2)}, u32[]{:S(2)}) collective-permute-start(bf16[64,1152]{1,0:T(8,128)(2,1)S(1)} %get-tuple-element.22), channel_id=1, source_target_pairs={{0,1},{1,0},{2,3},{3,2},{4,5},{5,4},{6,7},{7,6},{8,9},{9,8},{10,11... | collective-permute-start | bytes 442376 | tf_op jit(solution)/shard_map/ppermute | solution.py:402
  49.4 4.4 %collective-permute-start = (bf16[64,1152]{1,0:T(8,128)(2,1)S(1)}, bf16[64,1152]{1,0:T(8,128)(2,1)S(1)}, u32[]{:S(2)}, u32[]{:S(2)}) collective-permute-start(bf16[64,1152]{1,0:T(8,128)(2,1)S(1)} %order.4), channel_id=1, source_target_pairs={{0,1},{1,0},{2,3},{3,2},{4,5},{5,4},{6,7},{7,6},{8,9},{9,8},{10,11... | collective-permute-start | bytes 442376 | tf_op jit(solution)/shard_map/ppermute | solution.py:402
  50.0 5.8 %collective-permute-start.2 = (bf16[64,1152]{1,0:T(8,128)(2,1)S(1)}, bf16[64,1152]{1,0:T(8,128)(2,1)S(1)}, u32[]{:S(2)}, u32[]{:S(2)}) collective-permute-start(bf16[64,1152]{1,0:T(8,128)(2,1)S(1)} %add_convert_fusion), channel_id=1, source_target_pairs={{0,2},{1,3},{2,0},{3,1},{4,6},{5,7},{6,4},{7,5},{8,10},{9,11},{10,... | collective-permute-start | bytes 442376 | tf_op jit(solution)/shard_map/ppermute | solution.py:402

commit v9 on v8

--- a/solution.py
+++ b/solution.py
@@ -192,8 +192,15 @@
 
     end0 = lax.div(jnp.max(end0).astype(jnp.int32) + (unit - 1), unit)
     begin1 = lax.div(jnp.min(begin1).astype(jnp.int32), unit)
-    lax.fori_loop(0, end0, lambda number, carry: one_unit(0, number, carry), 0)
-    lax.fori_loop(begin1, count // unit, lambda number, carry: one_unit(1, number, carry), 0)
+    both = jnp.minimum(end0, count // unit - begin1)
+
+    def two_units(number, carry):
+        one_unit(0, number, 0)
+        return one_unit(1, begin1 + number, carry)
+
+    lax.fori_loop(0, both, two_units, 0)
+    lax.fori_loop(both, end0, lambda number, carry: one_unit(0, number, carry), 0)
+    lax.fori_loop(begin1 + both, count // unit, lambda number, carry: one_unit(1, number, carry), 0)
     first_copy.wait()
     first = first_vmem[...]
     mixed = [dot(first, acc_ref[t].astype(BF16), 1, 0).astype(BF16) for t in range(CYCLE_DEV)]
@@ -243,13 +250,16 @@
     out_ref[...] = total.astype(BF16)
 
 
-def order_kernel(chunk, offset, late, where_ref, coeff_ref, wigner_ref, *refs):
+def order_kernel(chunk, offset, tables, late, where_ref, coeff_ref, *refs):
     depth = coeff_ref.shape[1]
     size = chunk * depth
+    places = [(ref, at) for ref in refs[:tables] for at in range(0, ref.shape[0], size)]
+    early = len(places)
+    refs = refs[tables:]
     copies = []
     if late:
         source_ref, out_ref, late_ref, sem = refs
-        first = where_ref[offset] * (out_ref.shape[0] // 2 * depth) + wigner_ref.shape[0]
+        first = where_ref[offset] * (out_ref.shape[0] // 2 * depth) + early * size
         for number in range(late):
             source = source_ref.at[pl.ds(first + number * size, size), :]
             copies.append(pltpu.make_async_copy(source, late_ref.at[number], sem.at[number]))
@@ -260,13 +270,13 @@
     base = where_ref[offset] * rows
     shape = (2 * chunk, size)
     own = lax.broadcasted_iota(jnp.int32, shape, 0) // 2 == lax.broadcasted_iota(jnp.int32, shape, 1) // depth
-    early = wigner_ref.shape[0] // size
     for number in range(early + late):
         start = pl.multiple_of(base + number * 2 * chunk, 2 * chunk)
         coeff = coeff_ref[pl.ds(start, 2 * chunk), :].astype(F32)
         wide = jnp.where(own, jnp.concatenate([coeff] * chunk, axis=1), 0.0).astype(BF16)
         if number < early:
-            table = wigner_ref[number * size : (number + 1) * size, :]
+            ref, at = places[number]
+            table = ref[at : at + size, :]
         else:
             copies[number - early].wait()
             table = late_ref[number - early]
@@ -274,9 +284,19 @@
         out_ref[number * 2 * chunk : (number + 1) * 2 * chunk, :] = part.astype(out_ref.dtype)
 
 
-def first_order_kernel(groups, orders, chunk, offset, where_ref, recv_ref, wigner_ref, coeff_ref, out_ref):
+def first_order_kernel(groups, orders, chunk, offset, skip, where_ref, recv_ref, wigner_ref, *refs):
+    if skip is None:
+        coeff_ref, out_ref = refs
+    else:
+        source_ref, coeff_ref, out_ref, mid_ref, sem = refs
+        size = mid_ref.shape[0]
+        first = where_ref[0] * wigner_ref.shape[0] + skip * size
+        copy = pltpu.make_async_copy(source_ref.at[pl.ds(first, size), :], mid_ref, sem)
+        copy.start()
     coeff_kernel(groups, orders, recv_ref, coeff_ref)
-    order_kernel(chunk, offset, 0, where_ref, coeff_ref, wigner_ref, out_ref)
+    order_kernel(chunk, offset, 1, 0, where_ref, coeff_ref, wigner_ref, out_ref)
+    if skip is not None:
+        copy.wait()
 
 
 def sum_kernel(*refs):
@@ -338,7 +358,9 @@
     mine = orders // beams
     chunk = 8
     steps = mine // chunk
-    early = (steps + 1) // 2
+    late = steps // 2
+    mid = 1 if steps - late > 1 else 0
+    early = steps - late - mid
     spectra, *held = pl.pallas_call(
         lambda *refs: bin_kernel(share, unit, *refs),
         out_shape=(
@@ -369,34 +391,37 @@
     spectra = spectra.reshape(groups * beams, rows, width)
     parts = lax.all_to_all(spectra, ("blk", "beam"), split_axis=0, concat_axis=0, tiled=True)
     parts = parts.reshape(groups, beams, 2, CYCLE_DEV, share, width)
+    distant = pltpu.with_memory_space_constraint(flat, pltpu.HBM)
 
     def first_piece(offset, kind):
+        table = pltpu.with_memory_space_constraint(held[offset], pltpu.VMEM)
         return pl.pallas_call(
-            lambda *refs: first_order_kernel(groups, orders, chunk, offset, *refs),
+            lambda *refs: first_order_kernel(groups, orders, chunk, offset, early if mid else None, *refs),
             out_shape=(
                 jax.ShapeDtypeStruct((2 * orders, depth), BF16),
                 jax.ShapeDtypeStruct((2 * mine, ells), kind),
-            ),
-            in_specs=[scalars, whole, whole],
-            out_specs=(whole, whole),
+            )
+            + (pltpu.VMEM((chunk * depth, ells), BF16),) * mid,
+            in_specs=[scalars, whole, whole] + [anywhere] * mid,
+            out_specs=(whole,) * (2 + mid),
+            scratch_shapes=[pltpu.SemaphoreType.DMA] * mid,
             compiler_params=pltpu.CompilerParams(vmem_limit_bytes=6 << 20),
             name="first",
-        )(targets, parts, pltpu.with_memory_space_constraint(held[offset], pltpu.VMEM))
-
-    def piece(coeff, offset, kind):
-        late = 0 if offset else steps - early
-        table = pltpu.with_memory_space_constraint(held[offset], pltpu.VMEM)
-        source = [pltpu.with_memory_space_constraint(flat, pltpu.HBM)] if late else []
-        scratch = [pltpu.VMEM((late, chunk * depth, ells), BF16), pltpu.SemaphoreType.DMA((late,))] if late else []
+        )(targets, parts, table, *[distant] * mid)
+
+    def piece(coeff, offset, tables, kind):
+        tables = [pltpu.with_memory_space_constraint(table, pltpu.VMEM) for table in tables]
+        rest = 0 if offset else late
+        scratch = [pltpu.VMEM((rest, chunk * depth, ells), BF16), pltpu.SemaphoreType.DMA((rest,))] if rest else []
         return pl.pallas_call(
-            lambda *refs: order_kernel(chunk, offset, late, *refs),
+            lambda *refs: order_kernel(chunk, offset, len(tables), rest, *refs),
             out_shape=jax.ShapeDtypeStruct((2 * mine, ells), kind),
-            in_specs=[scalars, whole, whole] + [anywhere] * len(source),
+            in_specs=[scalars, whole] + [whole] * len(tables) + [anywhere] * min(rest, 1),
             out_specs=whole,
             scratch_shapes=scratch,
             compiler_params=pltpu.CompilerParams(vmem_limit_bytes=6 << 20),
             name="order",
-        )(targets, coeff, table, *source)
+        )(targets, coeff, *tables, *[distant] * min(rest, 1))
 
     def send(part, distance):
         return lax.ppermute(part, "beam", [(i, i ^ distance) for i in range(beams)])
@@ -406,9 +431,10 @@
     near = None
     for offset in sequence:
         if offset == beams - 1:
-            coeff, part = first_piece(offset, BF16)
+            coeff, part, *fetched = first_piece(offset, BF16)
         else:
-            part = piece(coeff, offset, BF16 if offset % 2 else F32)
+            tables = [held[offset]] + ([] if offset else fetched)
+            part = piece(coeff, offset, tables, BF16 if offset % 2 else F32)
         if offset % 2:
             near = send(part, 1)
         elif offset:

time: 56.8 us -> 57.6 us (1.014)
  Pallas kernels: 23.8 us -> 24.6 us
    pallas_call x1, Pallas kernels: 2.23 us -> 3.78 us  [first_piece(): pl.pallas_call(lambda *refs: first_order_kernel(groups, orders, chunk, of...]
    pallas_call x1, Pallas kernels: 11.9 us -> 11.2 us  [shards(): pl.pallas_call(lambda *refs: bin_kernel(share, unit, *refs), out_shape=(j...]
  transfers between devices with their start and end apart: 3 -> 3, of which waited for: 1 -> 1; matrix products, arithmetic and copies ran while one was open for 0% -> 0% of each run, Pallas kernels for 13% -> 12%
where the time goes in v9:
time: 57.6 us; the launch traced here: 57.4 us
  blocking collectives  29.7 us (52%)
  Pallas kernels  24.6 us (43%)
  waiting for transfers between devices  2.05 us (4%)
  starting transfers between devices  1.02 us (2%)
    all_to_all x1, blocking collectives, shards(): got = lax.all_to_all(sent, 'blk', split_axis=0, concat_axis=0, tiled=True)  15.8 us
    all_to_all x1, blocking collectives, shards(): lax.all_to_all(spectra, ('blk', 'beam'), split_axis=0, concat_axis=0, til...  13.9 us
    pallas_call x1, Pallas kernels, shards(): pl.pallas_call(lambda *refs: bin_kernel(share, unit, *refs), out_shape=(j...  11.2 us
    pallas_call x3, Pallas kernels, piece(): pl.pallas_call(lambda *refs: order_kernel(chunk, offset, len(tables), res...  7.13 us
    pallas_call x1, Pallas kernels, first_piece(): pl.pallas_call(lambda *refs: first_order_kernel(groups, orders, chunk, of...  3.78 us
    ppermute x3, waiting for transfers between devices, send(): return lax.ppermute(part, 'beam', [(i, i ^ distance) for i in range(beams)])  2.05 us
    pallas_call x1, Pallas kernels, shards(): pl.pallas_call(lambda *refs: pack_kernel(groups, *refs), out_shape=(jax.S...  1.77 us
  transfers between devices with their start and end apart: 3, of which 1 were waited for; matrix products, arithmetic and copies ran while one was open for 0% of the time, Pallas kernels for 12%

profile of v9, /device:TPU:0, one launch (start us, length us, event | category | flops | bytes accessed | tf_op | source)
XLA Modules:
  0.0 57.4 jit_solution(17146457563629863001)
XLA Ops:
  0.0 0.0 copy-start
  0.0 1.8 %pack.1 = (bf16[8,3,40,128]{3,2,1,0:T(8,128)(2,1)S(1)}, s32[4]{0:T(128)S(1)}) custom-call(s32[1]{0:T(128)} %bitcast.refs_0_, s32[1,128]{1,0:T(1,128)} %bitcast.20, f32[128,128]{1,0:T(8,128)} %bitcast.15, f32[128,128]{1,0:T(8,128)} %bitcast.16, s32[128,128]{1,0:T(8,128)} %bitcast.17, s32[128,128]{1,0:T(8,128)} %bitcast.18, s32[128,128]{1,0:T(8,128)} %bitcast.19), custom_call_target="tpu_custom_call" | custom-call | flops 99999997952 | bytes 100000000 | tf_op jit(solution)/shard_map/pack/pallas_call | solution.py:329
  1.8 15.8 %all_to_all.10.refs_1_ = bf16[8,3,40,128]{3,2,1,0:T(8,128)(2,1)S(1)} all-to-all(bf16[8,3,40,128]{3,2,1,0:T(8,128)(2,1)S(1)} %get-tuple-element.16), channel_id=1, replica_groups=mesh['blk'=8,'beam'=4] {'blk'}, dimensions={0} | all-to-all | bytes 491520 | tf_op jit(solution)/shard_map/all_to_all | solution.py:353
  17.6 0.0 copy-done
  17.6 11.2 %bin.1 = (bf16[8,4,2,2,8,128]{5,4,3,2,1,0:T(8,128)(2,1)S(1)}, bf16[1024,1152]{1,0:T(8,128)(2,1)S(1)}, bf16[4096,1152]{1,0:T(8,128)(2,1)S(1)}, bf16[4096,1152]{1,0:T(8,128)(2,1)S(1)}, bf16[4096,1152]{1,0:T(8,128)(2,1)S(1)}) custom-call(s32[4]{0:T(128)S(1)} %get-tuple-element.15.refs_0_, bf16[8,3,40,128]{3,2,1,0:T(8,128)(2,1)S(1)} %all_to_all.10.refs_1_, ...), custom_call_target="tpu_custom_call" | custom-call | tf_op jit(solution)/shard_map/bin/pallas_call | solution.py:364
  28.7 13.9 %all_to_all.11 = bf16[32,32,128]{2,1,0:T(8,128)(2,1)S(1)} all-to-all(bf16[32,32,128]{2,1,0:T(8,128)(2,1)S(1)} %bitcast.11), channel_id=1, replica_groups=mesh['blk'=8,'beam'=4] {'blk','beam'}, dimensions={0} | all-to-all | bytes 524288 | tf_op jit(solution)/shard_map/all_to_all | solution.py:392
  42.6 3.8 %first.1 = (bf16[256,128]{1,0:T(8,128)(2,1)S(1)}, bf16[64,1152]{1,0:T(8,128)(2,1)S(1)}, bf16[1024,1152]{1,0:T(8,128)(2,1)S(1)}) custom-call(s32[4]{0:T(128)S(1)} %get-tuple-element.15.refs_0_, bf16[8,4,2,2,8,128]{5,4,3,2,1,0:T(8,128)(2,1)S(1)} %bitcast.10, bf16[4096,1152]{1,0:T(8,128)(2,1)S(1)} %get-tuple-element.18.refs_2_, bf16[16384,1152]{1,0:T(8,128)(2,1)} %bitcast.13), custom_call_target="tpu_custom_call" | custom-call | tf_op jit(solution)/shard_map/first/pallas_call | solution.py:398
  46.4 0.1 collective-permute-start.1
  46.5 1.9 %order.4 = bf16[64,1152]{1,0:T(8,128)(2,1)S(1)} custom-call(s32[4]{0:T(128)S(1)} %get-tuple-element.15.refs_0_, bf16[256,128]{1,0:T(8,128)(2,1)S(1)} %get-tuple-element.19.refs_1_, bf16[4096,1152]{1,0:T(8,128)(2,1)S(1)} %get-tuple-element.22.refs_2_), custom_call_target="tpu_custom_call" | custom-call | tf_op jit(solution)/shard_map/order/pallas_call | solution.py:416
  48.3 1.9 %order.5 = f32[64,1152]{1,0:T(8,128)S(1)} custom-call(s32[4]{0:T(128)S(1)} %get-tuple-element.15.refs_0_, bf16[256,128]{1,0:T(8,128)(2,1)S(1)} %get-tuple-element.19.refs_1_, bf16[4096,1152]{1,0:T(8,128)(2,1)S(1)} %get-tuple-element.23.refs_2_), custom_call_target="tpu_custom_call" | custom-call | tf_op jit(solution)/shard_map/order/pallas_call | solution.py:416
  50.2 0.5 collective-permute-start
  50.8 0.0 collective-permute-done.1
  50.8 0.4 collective-permute-start.2
  51.2 3.4 %order.3.refs_0_ = f32[64,1152]{1,0:T(8,128)S(1)} custom-call(s32[4]{0:T(128)S(1)} %get-tuple-element.15.refs_0_, bf16[256,128]{1,0:T(8,128)(2,1)S(1)} %get-tuple-element.19.refs_1_, bf16[1024,1152]{1,0:T(8,128)(2,1)S(1)} %get-tuple-element.20.refs_2_, bf16[1024,1152]{1,0:T(8,128)(2,1)S(1)} %get-tuple-element.21.refs_3_, bf16[16384,1152]{1,0:T(8,128)(2,1)} %bitcast.14), custom_call_target="tpu_custom_call" | custom-call | tf_op jit(solution)/shard_map/order/pallas_call | solution.py:416
  54.6 0.0 collective-permute-done.refs_1_
  54.6 2.0 %collective-permute-done.2.refs_2_ = bf16[64,1152]{1,0:T(8,128)(2,1)S(1)} collective-permute-done((bf16[64,1152]{1,0:T(8,128)(2,1)S(1)}, bf16[64,1152]{1,0:T(8,128)(2,1)S(1)}, u32[]{:S(2)}, u32[]{:S(2)}) %collective-permute-start.2) | collective-permute-done | bytes 147488 | tf_op jit(solution)/shard_map/ppermute | solution.py:427
  56.7 0.8 %sum.1 = f32[32,2,1152]{2,1,0:T(2,128)} custom-call(f32[64,1152]{1,0:T(8,128)S(1)} %order.3.refs_0_, bf16[64,1152]{1,0:T(8,128)(2,1)S(1)} %collective-permute-done.refs_1_, bf16[64,1152]{1,0:T(8,128)(2,1)S(1)} %collective-permute-done.2.refs_2_), custom_call_target="tpu_custom_call" | custom-call | tf_op jit(solution)/shard_map/sum/pallas_call | solution.py:444
  (1 shorter events, 0.0 us)
Async XLA Ops:
  0.0 17.6 %copy-start = (bf16[2,1024,1024]{2,1,0:T(8,128)(2,1)S(1)}, bf16[2,1024,1024]{2,1,0:T(8,128)(2,1)}, u32[]{:S(2)}) copy-start(bf16[2,1024,1024]{2,1,0:T(8,128)(2,1)} %constant.9.clone.refs_3_) | copy-start | bytes 12582916
  46.4 4.4 %collective-permute-start.1 = (bf16[64,1152]{1,0:T(8,128)(2,1)S(1)}, bf16[64,1152]{1,0:T(8,128)(2,1)S(1)}, u32[]{:S(2)}, u32[]{:S(2)}) collective-permute-start(bf16[64,1152]{1,0:T(8,128)(2,1)S(1)} %get-tuple-element.24), channel_id=1, source_target_pairs={{0,1},{1,0},{2,3},{3,2},{4,5},{5,4},{6,7},{7,6},{8,9},{9,8},{10,11... | collective-permute-start | bytes 442376 | tf_op jit(solution)/shard_map/ppermute | solution.py:427
  50.2 4.4 %collective-permute-start = (bf16[64,1152]{1,0:T(8,128)(2,1)S(1)}, bf16[64,1152]{1,0:T(8,128)(2,1)S(1)}, u32[]{:S(2)}, u32[]{:S(2)}) collective-permute-start(bf16[64,1152]{1,0:T(8,128)(2,1)S(1)} %order.4), channel_id=1, source_target_pairs={{0,1},{1,0},{2,3},{3,2},{4,5},{5,4},{6,7},{7,6},{8,9},{9,8},{10,11... | collective-permute-start | bytes 442376 | tf_op jit(solution)/shard_map/ppermute | solution.py:427
  50.8 5.8 %collective-permute-start.2 = (bf16[64,1152]{1,0:T(8,128)(2,1)S(1)}, bf16[64,1152]{1,0:T(8,128)(2,1)S(1)}, u32[]{:S(2)}, u32[]{:S(2)}) collective-permute-start(bf16[64,1152]{1,0:T(8,128)(2,1)S(1)} %add_convert_fusion), channel_id=1, source_target_pairs={{0,2},{1,3},{2,0},{3,1},{4,6},{5,7},{6,4},{7,5},{8,10},{9,11},{10,... | collective-permute-start | bytes 442376 | tf_op jit(solution)/shard_map/ppermute | solution.py:427

commit v10 on v8

--- a/solution.py
+++ b/solution.py
@@ -192,8 +192,15 @@
 
     end0 = lax.div(jnp.max(end0).astype(jnp.int32) + (unit - 1), unit)
     begin1 = lax.div(jnp.min(begin1).astype(jnp.int32), unit)
-    lax.fori_loop(0, end0, lambda number, carry: one_unit(0, number, carry), 0)
-    lax.fori_loop(begin1, count // unit, lambda number, carry: one_unit(1, number, carry), 0)
+    both = jnp.minimum(end0, count // unit - begin1)
+
+    def two_units(number, carry):
+        one_unit(0, number, 0)
+        return one_unit(1, begin1 + number, carry)
+
+    lax.fori_loop(0, both, two_units, 0)
+    lax.fori_loop(both, end0, lambda number, carry: one_unit(0, number, carry), 0)
+    lax.fori_loop(begin1 + both, count // unit, lambda number, carry: one_unit(1, number, carry), 0)
     first_copy.wait()
     first = first_vmem[...]
     mixed = [dot(first, acc_ref[t].astype(BF16), 1, 0).astype(BF16) for t in range(CYCLE_DEV)]

time: 56.8 us -> 56.8 us (level)
  no operation moved by 1% of the time
where the time goes in v10:
time: 56.8 us; the launch traced here: 56.6 us
  blocking collectives  29.7 us (52%)
  Pallas kernels  23.8 us (42%)
  waiting for transfers between devices  2.05 us (4%)
  starting transfers between devices  1.02 us (2%)
    all_to_all x1, blocking collectives, shards(): got = lax.all_to_all(sent, 'blk', split_axis=0, concat_axis=0, tiled=True)  15.8 us
    all_to_all x1, blocking collectives, shards(): lax.all_to_all(spectra, ('blk', 'beam'), split_axis=0, concat_axis=0, til...  13.9 us
    pallas_call x1, Pallas kernels, shards(): pl.pallas_call(lambda *refs: bin_kernel(share, unit, *refs), out_shape=(j...  11.9 us
    pallas_call x3, Pallas kernels, piece(): pl.pallas_call(lambda *refs: order_kernel(chunk, offset, late, *refs), ou...  7.13 us
    pallas_call x1, Pallas kernels, first_piece(): pl.pallas_call(lambda *refs: first_order_kernel(groups, orders, chunk, of...  2.24 us
    ppermute x3, waiting for transfers between devices, send(): return lax.ppermute(part, 'beam', [(i, i ^ distance) for i in range(beams)])  2.05 us
    pallas_call x1, Pallas kernels, shards(): pl.pallas_call(lambda *refs: pack_kernel(groups, *refs), out_shape=(jax.S...  1.77 us
  transfers between devices with their start and end apart: 3, of which 1 were waited for; matrix products, arithmetic and copies ran while one was open for 0% of the time, Pallas kernels for 13%

profile of v10, /device:TPU:0, one launch (start us, length us, event | category | flops | bytes accessed | tf_op | source)
XLA Modules:
  0.0 56.6 jit_solution(8095287730535063573)
XLA Ops:
  0.0 0.0 copy-start
  0.0 1.8 %pack.1 = (bf16[8,3,40,128]{3,2,1,0:T(8,128)(2,1)S(1)}, s32[4]{0:T(128)S(1)}) custom-call(s32[1]{0:T(128)} %bitcast.refs_0_, s32[1,128]{1,0:T(1,128)} %bitcast.19, f32[128,128]{1,0:T(8,128)} %bitcast.14, f32[128,128]{1,0:T(8,128)} %bitcast.15, s32[128,128]{1,0:T(8,128)} %bitcast.16, s32[128,128]{1,0:T(8,128)} %bitcast.17, s32[128,128]{1,0:T(8,128)} %bitcast.18), custom_call_target="tpu_custom_call" | custom-call | flops 99999997952 | bytes 100000000 | tf_op jit(solution)/shard_map/pack/pallas_call | solution.py:316
  1.8 15.8 %all_to_all.10.refs_1_ = bf16[8,3,40,128]{3,2,1,0:T(8,128)(2,1)S(1)} all-to-all(bf16[8,3,40,128]{3,2,1,0:T(8,128)(2,1)S(1)} %get-tuple-element.15), channel_id=1, replica_groups=mesh['blk'=8,'beam'=4] {'blk'}, dimensions={0} | all-to-all | bytes 491520 | tf_op jit(solution)/shard_map/all_to_all | solution.py:340
  17.6 0.0 copy-done
  17.6 11.9 %bin.1 = (bf16[8,4,2,2,8,128]{5,4,3,2,1,0:T(8,128)(2,1)S(1)}, bf16[2048,1152]{1,0:T(8,128)(2,1)S(1)}, bf16[4096,1152]{1,0:T(8,128)(2,1)S(1)}, bf16[4096,1152]{1,0:T(8,128)(2,1)S(1)}, bf16[4096,1152]{1,0:T(8,128)(2,1)S(1)}) custom-call(s32[4]{0:T(128)S(1)} %get-tuple-element.14.refs_0_, bf16[8,3,40,128]{3,2,1,0:T(8,128)(2,1)S(1)} %all_to_all.10.refs_1_, ...), custom_call_target="tpu_custom_call" | custom-call | tf_op jit(solution)/shard_map/bin/pallas_call | solution.py:349
  29.4 13.9 %all_to_all.11 = bf16[32,32,128]{2,1,0:T(8,128)(2,1)S(1)} all-to-all(bf16[32,32,128]{2,1,0:T(8,128)(2,1)S(1)} %bitcast.11), channel_id=1, replica_groups=mesh['blk'=8,'beam'=4] {'blk','beam'}, dimensions={0} | all-to-all | bytes 524288 | tf_op jit(solution)/shard_map/all_to_all | solution.py:377
  43.3 2.2 %first.1 = (bf16[256,128]{1,0:T(8,128)(2,1)S(1)}, bf16[64,1152]{1,0:T(8,128)(2,1)S(1)}) custom-call(s32[4]{0:T(128)S(1)} %get-tuple-element.14.refs_0_, bf16[8,4,2,2,8,128]{5,4,3,2,1,0:T(8,128)(2,1)S(1)} %bitcast.10, bf16[4096,1152]{1,0:T(8,128)(2,1)S(1)} %get-tuple-element.17.refs_2_), custom_call_target="tpu_custom_call" | custom-call | tf_op jit(solution)/shard_map/first/pallas_call | solution.py:381
  45.6 0.1 collective-permute-start.1
  45.6 1.9 %order.4 = bf16[64,1152]{1,0:T(8,128)(2,1)S(1)} custom-call(s32[4]{0:T(128)S(1)} %get-tuple-element.14.refs_0_, bf16[256,128]{1,0:T(8,128)(2,1)S(1)} %get-tuple-element.18.refs_1_, bf16[4096,1152]{1,0:T(8,128)(2,1)S(1)} %get-tuple-element.20.refs_2_), custom_call_target="tpu_custom_call" | custom-call | tf_op jit(solution)/shard_map/order/pallas_call | solution.py:398
  47.5 1.9 %order.5 = f32[64,1152]{1,0:T(8,128)S(1)} custom-call(s32[4]{0:T(128)S(1)} %get-tuple-element.14.refs_0_, bf16[256,128]{1,0:T(8,128)(2,1)S(1)} %get-tuple-element.18.refs_1_, bf16[4096,1152]{1,0:T(8,128)(2,1)S(1)} %get-tuple-element.21.refs_2_), custom_call_target="tpu_custom_call" | custom-call | tf_op jit(solution)/shard_map/order/pallas_call | solution.py:398
  49.4 0.5 collective-permute-start
  49.9 0.0 collective-permute-done.1
  50.0 0.4 collective-permute-start.2
  50.4 3.4 %order.3.refs_0_ = f32[64,1152]{1,0:T(8,128)S(1)} custom-call(s32[4]{0:T(128)S(1)} %get-tuple-element.14.refs_0_, bf16[256,128]{1,0:T(8,128)(2,1)S(1)} %get-tuple-element.18.refs_1_, bf16[2048,1152]{1,0:T(8,128)(2,1)S(1)} %get-tuple-element.19.refs_2_, bf16[16384,1152]{1,0:T(8,128)(2,1)} %bitcast.13), custom_call_target="tpu_custom_call" | custom-call | tf_op jit(solution)/shard_map/order/pallas_call | solution.py:398
  53.8 0.0 collective-permute-done.refs_1_
  53.8 2.0 %collective-permute-done.2.refs_2_ = bf16[64,1152]{1,0:T(8,128)(2,1)S(1)} collective-permute-done((bf16[64,1152]{1,0:T(8,128)(2,1)S(1)}, bf16[64,1152]{1,0:T(8,128)(2,1)S(1)}, u32[]{:S(2)}, u32[]{:S(2)}) %collective-permute-start.2) | collective-permute-done | bytes 147488 | tf_op jit(solution)/shard_map/ppermute | solution.py:409
  55.8 0.8 %sum.1 = f32[32,2,1152]{2,1,0:T(2,128)} custom-call(f32[64,1152]{1,0:T(8,128)S(1)} %order.3.refs_0_, bf16[64,1152]{1,0:T(8,128)(2,1)S(1)} %collective-permute-done.refs_1_, bf16[64,1152]{1,0:T(8,128)(2,1)S(1)} %collective-permute-done.2.refs_2_), custom_call_target="tpu_custom_call" | custom-call | tf_op jit(solution)/shard_map/sum/pallas_call | solution.py:425
  (1 shorter events, 0.0 us)
Async XLA Ops:
  0.0 17.6 %copy-start = (bf16[2,1024,1024]{2,1,0:T(8,128)(2,1)S(1)}, bf16[2,1024,1024]{2,1,0:T(8,128)(2,1)}, u32[]{:S(2)}) copy-start(bf16[2,1024,1024]{2,1,0:T(8,128)(2,1)} %constant.9.clone.refs_3_) | copy-start | bytes 12582916
  45.6 4.4 %collective-permute-start.1 = (bf16[64,1152]{1,0:T(8,128)(2,1)S(1)}, bf16[64,1152]{1,0:T(8,128)(2,1)S(1)}, u32[]{:S(2)}, u32[]{:S(2)}) collective-permute-start(bf16[64,1152]{1,0:T(8,128)(2,1)S(1)} %get-tuple-element.22), channel_id=1, source_target_pairs={{0,1},{1,0},{2,3},{3,2},{4,5},{5,4},{6,7},{7,6},{8,9},{9,8},{10,11... | collective-permute-start | bytes 442376 | tf_op jit(solution)/shard_map/ppermute | solution.py:409
  49.4 4.4 %collective-permute-start = (bf16[64,1152]{1,0:T(8,128)(2,1)S(1)}, bf16[64,1152]{1,0:T(8,128)(2,1)S(1)}, u32[]{:S(2)}, u32[]{:S(2)}) collective-permute-start(bf16[64,1152]{1,0:T(8,128)(2,1)S(1)} %order.4), channel_id=1, source_target_pairs={{0,1},{1,0},{2,3},{3,2},{4,5},{5,4},{6,7},{7,6},{8,9},{9,8},{10,11... | collective-permute-start | bytes 442376 | tf_op jit(solution)/shard_map/ppermute | solution.py:409
  50.0 5.8 %collective-permute-start.2 = (bf16[64,1152]{1,0:T(8,128)(2,1)S(1)}, bf16[64,1152]{1,0:T(8,128)(2,1)S(1)}, u32[]{:S(2)}, u32[]{:S(2)}) collective-permute-start(bf16[64,1152]{1,0:T(8,128)(2,1)S(1)} %add_convert_fusion), channel_id=1, source_target_pairs={{0,2},{1,3},{2,0},{3,1},{4,6},{5,7},{6,4},{7,5},{8,10},{9,11},{10,... | collective-permute-start | bytes 442376 | tf_op jit(solution)/shard_map/ppermute | solution.py:409
